TPU v7x, 32 devices: a whole 2x2x4 slice. The times are simulated.
32 devices in a mesh: pipe: 2 (over y), dp: 16 (over z, x, core).
Axes of the slice: x: 2, y: 2, z: 4, core: 2. Of those that a mesh axis runs over, the one named last changes fastest.
Arguments:
- layer_inputs: bfloat16 [2, 16, 2, 64, 2560], P('pipe', 'dp'), may hold values from -6 to 6
- top_grad: bfloat16 [16, 2, 64, 2560], P('dp'), may hold values from -6 to 6
- keys: bfloat16 [2, 16, 1024, 512], P('pipe', 'dp'), may hold values from -250 to 250
- values: bfloat16 [2, 16, 1024, 512], P('pipe', 'dp'), may hold values from -6 to 6
- query_weight: bfloat16 [2, 2560, 2560], P('pipe', 'dp'), may hold values from -0.125 to 0.125
- adapter_a: bfloat16 [2, 2560, 32], P('pipe', 'dp'), may hold values from -0.125 to 0.125
- adapter_bt: bfloat16 [2, 2560, 32], P('pipe', 'dp'), may hold values from -0.125 to 0.125
- norm_gain: bfloat16 [2, 2560], P('pipe', 'dp'), may hold values from 0.5 to 1.5
- offsets: int32 [16, 2], P('dp'), may hold values from 0 to 960, as said below
- segments: int32 [16, 1024], P('dp'), may hold values from 0 to 10, as said below
Outputs:
- section_grads: bfloat16 [2, 16, 2, 64, 2560], P('pipe', 'dp')
- grad_a: float32 [2, 2560, 32], P('pipe', 'dp')
- grad_bt: float32 [2, 2560, 32], P('pipe', 'dp')
Inputs may be any that keep to these rules, and one draw needn't show every extreme that they name: `offsets`: each offset is a multiple of 64. `segments`: segment 0 is the schema and covers positions 0 up to a length of at least 256; the numbers never fall along a sequence.
All inputs are finite; a program needn't handle non-finite values.
Results may differ from a plain program's by a relative error of at most 0.03.
The roundings to bfloat16 on the way count: a program that leaves them out, or rounds other values in their place, can miss the bound.
Values may be sent and summed in bfloat16 or wider, within the bound.
No kernel may reach another device: no remote copies, remote signals or barrier semaphores. Data moves between devices by JAX's collectives and lax.ppermute only.
A program may use at most 128 MiB of HBM per device.

v0:
```python
import jax
import jax.numpy as jnp
from jax import lax
from jax.sharding import PartitionSpec as P

HEADS = 20
KV_HEADS = 4
HEAD_DIM = 128


norm_eps = 1e-06
rope_base = 1000000.0


def passed_along(value, axis, steps):
    count = lax.axis_size(axis)
    first, last = (max(0, -steps), min(count, count - steps))
    return lax.ppermute(value, axis, [(source, source + steps) for source in range(first, last)])


def rope_tables(positions, head_dim):
    half = head_dim // 2
    expon = jnp.arange(half, dtype=jnp.float32) * (2.0 / head_dim)
    inverse = rope_base ** (-expon)
    angles = positions.astype(jnp.float32)[:, None] * inverse[None, :]
    return (jnp.cos(angles)[:, None, :], jnp.sin(angles)[:, None, :])


def rotate(query, cosine, sine):
    half = query.shape[-1] // 2
    first = query[..., :half]
    second = query[..., half:]
    return jnp.concatenate(
        [first * cosine - second * sine, second * cosine + first * sine], axis=-1
    )


def unrotate(grad, cosine, sine):
    half = grad.shape[-1] // 2
    first = grad[..., :half]
    second = grad[..., half:]
    return jnp.concatenate(
        [first * cosine + second * sine, second * cosine - first * sine], axis=-1
    )


def attend_back(rotated_rows, upstream_rows, keys_heads, values_heads, mask):
    count = rotated_rows.shape[0]
    group = HEADS // KV_HEADS
    scale = 1.0 / HEAD_DIM**0.5
    grouped = rotated_rows.reshape(count, KV_HEADS, group, HEAD_DIM).transpose(1, 0, 2, 3)
    grad_grouped = upstream_rows.reshape(count, KV_HEADS, group, HEAD_DIM).transpose(1, 0, 2, 3)

    def one_head(operands):
        query_head, grad_head, key_head, value_head = operands
        scores = (
            jnp.einsum("ngd,cd->ngc", query_head, key_head, preferred_element_type=jnp.float32)
            * scale
        )
        scores = jnp.where(mask[:, None, :], scores, -1e30)
        highest = jnp.max(scores, axis=-1, keepdims=True)
        expo = jnp.exp(scores - highest)
        probs = expo / jnp.sum(expo, axis=-1, keepdims=True)
        probs_b = probs.astype(jnp.bfloat16)
        attended = jnp.einsum(
            "ngc,cd->ngd", probs_b, value_head, preferred_element_type=jnp.float32
        )
        dprobs = jnp.einsum(
            "ngd,cd->ngc", grad_head, value_head, preferred_element_type=jnp.float32
        )
        delta = jnp.sum(grad_head.astype(jnp.float32) * attended, axis=-1, keepdims=True)
        dscores = (probs * (dprobs - delta) * scale).astype(jnp.bfloat16)
        return jnp.einsum("ngc,cd->ngd", dscores, key_head, preferred_element_type=jnp.float32)

    result = lax.map(one_head, (grouped, grad_grouped, keys_heads, values_heads))
    return result.transpose(1, 0, 2, 3).reshape(count, HEADS, HEAD_DIM)


def per_device(
    layer_inputs,
    top_grad,
    keys,
    values,
    query_weight,
    adapter_a,
    adapter_bt,
    norm_gain,
    offsets,
    segments,
):
    micro_count = layer_inputs.shape[2]
    token_total = layer_inputs.shape[3]
    width = layer_inputs.shape[4]
    row_count = micro_count * token_total
    ctx_len = keys.shape[2]
    flattened_rows = layer_inputs[0, 0].reshape(row_count, width).astype(jnp.float32)
    reciprocal_norm = lax.rsqrt(
        jnp.mean(flattened_rows * flattened_rows, axis=1, keepdims=True) + norm_eps
    )
    normalized_values = flattened_rows * reciprocal_norm
    positions = (offsets[0][:, None] + jnp.arange(token_total, dtype=jnp.int32)[None, :]).reshape(
        row_count
    )
    seg_row = segments[0]
    place = jnp.arange(ctx_len, dtype=jnp.int32)
    query_seg = jnp.take(seg_row, positions)
    visible = (place[None, :] <= positions[:, None]) & (
        (seg_row[None, :] == 0) | (seg_row[None, :] == query_seg[:, None])
    )
    keys_heads = keys[0, 0].reshape(ctx_len, KV_HEADS, HEAD_DIM).transpose(1, 0, 2)
    values_heads = values[0, 0].reshape(ctx_len, KV_HEADS, HEAD_DIM).transpose(1, 0, 2)
    cosine, sine = rope_tables(positions, HEAD_DIM)
    weight_full, factor_a, factor_bt, complete_gain = (
        lax.all_gather(query_weight, "dp", axis=1, tiled=True),
        lax.all_gather(adapter_a, "dp", axis=1, tiled=True),
        lax.all_gather(adapter_bt, "dp", axis=1, tiled=True),
        lax.all_gather(norm_gain, "dp", axis=1, tiled=True),
    )
    weight_full = weight_full[0]
    factor_a = factor_a[0]
    factor_bt = factor_bt[0]
    complete_gain = complete_gain[0]
    normalized_input = (normalized_values * complete_gain.astype(jnp.float32)[None, :]).astype(
        jnp.bfloat16
    )
    projected = jnp.dot(normalized_input, weight_full, preferred_element_type=jnp.float32)
    lowrank = jnp.dot(normalized_input, factor_a, preferred_element_type=jnp.float32).astype(
        jnp.bfloat16
    )
    query = projected + lax.dot_general(
        lowrank, factor_bt, (((1,), (1,)), ((), ())), preferred_element_type=jnp.float32
    )
    rotated = rotate(query.reshape(row_count, HEADS, HEAD_DIM), cosine, sine).astype(jnp.bfloat16)
    broadcast_gain = complete_gain.astype(jnp.float32)

    def backward(micro_index, upstream_gradient):
        start_offset = micro_index * token_total
        normalized_rows = lax.dynamic_slice_in_dim(normalized_values, start_offset, token_total, 0)
        recip_rows = lax.dynamic_slice_in_dim(reciprocal_norm, start_offset, token_total, 0)
        normed_rows = lax.dynamic_slice_in_dim(normalized_input, start_offset, token_total, 0)
        lowrank_rows = lax.dynamic_slice_in_dim(lowrank, start_offset, token_total, 0)
        rotated_rows = lax.dynamic_slice_in_dim(rotated, start_offset, token_total, 0)
        mask_rows = lax.dynamic_slice_in_dim(visible, start_offset, token_total, 0)
        cosine_rows = lax.dynamic_slice_in_dim(cosine, start_offset, token_total, 0)
        sine_rows = lax.dynamic_slice_in_dim(sine, start_offset, token_total, 0)
        drot = attend_back(
            rotated_rows,
            upstream_gradient.reshape(token_total, HEADS, HEAD_DIM),
            keys_heads,
            values_heads,
            mask_rows,
        )
        dquery = (
            unrotate(drot, cosine_rows, sine_rows)
            .reshape(token_total, HEADS * HEAD_DIM)
            .astype(jnp.bfloat16)
        )
        middle = jnp.dot(dquery, factor_bt, preferred_element_type=jnp.float32).astype(jnp.bfloat16)
        dnormed = lax.dot_general(
            dquery, weight_full, (((1,), (1,)), ((), ())), preferred_element_type=jnp.float32
        )
        dnormed = dnormed + lax.dot_general(
            middle, factor_a, (((1,), (1,)), ((), ())), preferred_element_type=jnp.float32
        )
        normalized_gradient = dnormed * broadcast_gain[None, :]
        input_gradient = upstream_gradient.astype(jnp.float32) + recip_rows * (
            normalized_gradient
            - normalized_rows
            * jnp.mean(normalized_gradient * normalized_rows, axis=1, keepdims=True)
        )
        part_a = lax.dot_general(
            normed_rows, middle, (((0,), (0,)), ((), ())), preferred_element_type=jnp.float32
        )
        part_bt = lax.dot_general(
            dquery, lowrank_rows, (((0,), (0,)), ((), ())), preferred_element_type=jnp.float32
        )
        return (input_gradient.astype(jnp.bfloat16), part_a, part_bt)

    section_count = lax.axis_size("pipe")
    section = lax.axis_index("pipe")
    last_section = section_count - 1
    top_rows = top_grad[0]

    def run_step(step_index, incoming, state):
        outgoing, grads_held, sum_a, sum_bt = state
        micro_index = step_index - (last_section - section)
        active_flag = (micro_index >= 0) & (micro_index < micro_count)
        clamped = jnp.clip(micro_index, 0, micro_count - 1)
        upstream_gradient = jnp.where(
            section == last_section,
            lax.dynamic_index_in_dim(top_rows, clamped, 0, keepdims=False),
            incoming,
        )

        def active_path(unused):
            return backward(clamped, upstream_gradient)

        def resting_path(unused):
            return (jnp.zeros_like(outgoing), jnp.zeros_like(sum_a), jnp.zeros_like(sum_bt))

        input_gradient, part_a, part_bt = lax.cond(active_flag, active_path, resting_path, 0)
        grads_held = jnp.where(
            active_flag,
            lax.dynamic_update_index_in_dim(grads_held, input_gradient, clamped, 0),
            grads_held,
        )
        return (input_gradient, grads_held, sum_a + part_a, sum_bt + part_bt)

    first_state = (
        jnp.zeros((token_total, width), jnp.bfloat16),
        jnp.zeros((micro_count, token_total, width), jnp.bfloat16),
        jnp.zeros((width, adapter_a.shape[2]), jnp.float32),
        jnp.zeros((factor_bt.shape[0], adapter_a.shape[2]), jnp.float32),
    )
    state = run_step(0, first_state[0], first_state)

    def loop_step(step_index, state):
        incoming = passed_along(state[0], "pipe", -1)
        return run_step(step_index, incoming, state)

    state = lax.fori_loop(1, section_count + micro_count - 1, loop_step, state)
    grads_held = state[1]
    share_a, share_bt = (
        lax.psum_scatter(state[2], "dp", scatter_dimension=0, tiled=True),
        lax.psum_scatter(state[3], "dp", scatter_dimension=0, tiled=True),
    )
    return (grads_held[None, None], share_a[None], share_bt[None])


def solution(mesh):
    placed = (
        P("pipe", "dp", None, None, None),
        P("dp", None, None, None),
        P("pipe", "dp", None, None),
        P("pipe", "dp", None, None),
        P("pipe", "dp", None),
        P("pipe", "dp", None),
        P("pipe", "dp", None),
        P("pipe", "dp"),
        P("dp", None),
        P("dp", None),
    )
    return jax.shard_map(
        per_device,
        mesh=mesh,
        in_specs=placed,
        out_specs=(P("pipe", "dp", None, None, None), P("pipe", "dp", None), P("pipe", "dp", None)),
        check_vma=False,
    )
```

profile of v0, /device:TPU:0, one launch (start us, length us, event | category | flops | bytes accessed | tf_op | source)
XLA Modules:
  0.0 456.2 jit_solution(5720105961619580142)
XLA Ops:
  11.9 36.8 %all-reduce = bf16[2560]{0:T(1024)(128)(2,1)S(1)} all-reduce(bf16[2560]{0:T(1024)(128)(2,1)S(1)} %dynamic-update-slice.6), channel_id=1, replica_groups=mesh['pipe'=2,'dp'=16] {'dp'}, use_global_device_ids=true, to_apply=%add | all-reduce | flops 2560 | bytes 10240
  49.6 2.7 copy.54
  52.3 22.4 %all_gather.14 = bf16[1,2560,32]{2,1,0:T(8,128)(2,1)} all-gather(bf16[1,160,32]{2,1,0:T(8,128)(2,1)S(1)} %copy.50), channel_id=1, replica_groups=mesh['pipe'=2,'dp'=16] {'dp'}, dimensions={1}, use_global_device_ids=true | all-gather | bytes 174080 | tf_op jit(solution)/shard_map/all_gather | solution.py:115
  81.1 24.8 %all_gather.15 = bf16[1,2560,32]{2,1,0:T(8,128)(2,1)S(1)} all-gather(bf16[1,160,32]{2,1,0:T(8,128)(2,1)S(1)} %copy.51), channel_id=1, replica_groups=mesh['pipe'=2,'dp'=16] {'dp'}, dimensions={1}, use_global_device_ids=true | all-gather | bytes 174080 | tf_op jit(solution)/shard_map/all_gather | solution.py:116
  107.3 18.5 %all-gather.2.cloned.1.call-done = bf16[1,2560,2560]{2,1,0:T(8,128)(2,1)} async-done(((bf16[1,160,2560]{2,1,0:T(8,128)(2,1)}), bf16[1,2560,2560]{2,1,0:T(8,128)(2,1)}) %all-gather.2.cloned.1.call-update) | async-done | bytes 13107216 | tf_op jit(solution)/shard_map/all_gather | solution.py:114
  125.8 6.7 %fusion.184 = f32[128,2560]{1,0:T(8,128)S(1)} fusion(bf16[128,2560]{1,0:T(8,128)(2,1)S(1)} %bitcast.247, bf16[1,2560,2560]{2,1,0:T(8,128)(2,1)} %all-gather.2.cloned.1.call-done), kind=kOutput, calls=%fused_computation.195 | convolution fusion | flops 1677721600 | bytes 15073280 | tf_op jit(solution)/shard_map/dot_general | solution.py:126
  137.0 3.0 conditional.2
  141.0 185.0 %while.55 = (s32[]{:T(128)}, bf16[64,2560]{1,0:T(8,128)(2,1)}, bf16[2,64,2560]{2,1,0:T(8,128)(2,1)}, f32[2560,32]{0,1:T(8,128)}, f32[2560,32]{0,1:T(8,128)}, /*i...) while((s32[]{:T(128)}, bf16[64,2560]{1,0:T(8,128)(2,1)}, ...), condition=%wide.region_18.19_spmd.clone.clone, body=%wide.region_9.0_spmd.clone.clone.sunk | while | flops 1308659712 | bytes 36471844 | solution.py:221
  142.3 67.7 %collective-permute-done = bf16[64,2560]{1,0:T(8,128)(2,1)S(1)} collective-permute-done((bf16[64,2560]{1,0:T(8,128)(2,1)}, bf16[64,2560]{1,0:T(8,128)(2,1)S(1)}, u32[]{:S(2)}, u32[]{:S(2)}) %collective-permute-start) | collective-permute-done | bytes 327712 | tf_op jit(solution)/shard_map/while/body/eval_jaxpr/ppermute | solution.py:18
  210.1 46.9 %conditional.6 = (bf16[64,2560]{1,0:T(8,128)(2,1)}, f32[2560,32]{0,1:T(8,128)S(1)}, f32[2560,32]{0,1:T(8,128)S(1)}, bf16[1,64,2560]{2,1,0:T(8,128)(2,1)S(1)}) conditional(s32[]{:T(128)} %convert_element_type.164, () %tuple.130, (pred[]{:T(512)}, bf16[2,64,2560]{2,1,0:T(8,128)(2,1)}, s32[]{:T(128)}, bf16[64,2560]{1,0:T(8,128)(2,1)S(1)}, ...), branch_computations={%region_10.10_spmd, %region_11.17_spmd} | conditional | flops 1308323840 | bytes 31653144 | solution.py:201
  213.8 27.5 %while.54 = (s32[]{:T(128)}, f32[4,64,5,128]{3,1,2,0:T(8,128)S(1)}, pred[64,1024]{1,0:T(8,128)(4,1)S(1)}, bf16[4,64,5,128]{3,1,2,0:T(8,128)(2,1)}, bf16[4,1024,1...) while((s32[]{:T(128)}, f32[4,64,5,128]{3,1,2,0:T(8,128)S(1)}, ...), condition=%wide.region_16.15_spmd, body=%wide.region_12.14_spmd.sunk | while | flops 424142848 | bytes 4571989 | solution.py:75
  213.8 2.6 fusion.244
  220.7 2.6 fusion.244
  227.6 2.6 fusion.244
  234.4 2.6 fusion.244
  242.9 8.7 %fusion.167 = f32[64,2560]{1,0:T(8,128)S(1)} fusion(bf16[2560,2560]{1,0:T(8,128)(2,1)} %get-tuple-element.788, bf16[8,8,20,128]{3,2,1,0:T(8,128)(2,1)S(1)} %bitcast.234), kind=kOutput, calls=%fused_computation.147 | convolution fusion | flops 838860800 | bytes 14090240 | tf_op jit(solution)/shard_map/while/body/eval_jaxpr/cond/branch_1_fun/dot_general | solution.py:159
  263.7 10.1 %collective-permute-done = bf16[64,2560]{1,0:T(8,128)(2,1)S(1)} collective-permute-done((bf16[64,2560]{1,0:T(8,128)(2,1)}, bf16[64,2560]{1,0:T(8,128)(2,1)S(1)}, u32[]{:S(2)}, u32[]{:S(2)}) %collective-permute-start) | collective-permute-done | bytes 327712 | tf_op jit(solution)/shard_map/while/body/eval_jaxpr/ppermute | solution.py:18
  273.8 46.9 %conditional.6 = (bf16[64,2560]{1,0:T(8,128)(2,1)}, f32[2560,32]{0,1:T(8,128)S(1)}, f32[2560,32]{0,1:T(8,128)S(1)}, bf16[1,64,2560]{2,1,0:T(8,128)(2,1)S(1)}) conditional(s32[]{:T(128)} %convert_element_type.164, () %tuple.130, (pred[]{:T(512)}, bf16[2,64,2560]{2,1,0:T(8,128)(2,1)}, s32[]{:T(128)}, bf16[64,2560]{1,0:T(8,128)(2,1)S(1)}, ...), branch_computations={%region_10.10_spmd, %region_11.17_spmd} | conditional | flops 1308323840 | bytes 31653144 | solution.py:201
  277.5 27.5 %while.54 = (s32[]{:T(128)}, f32[4,64,5,128]{3,1,2,0:T(8,128)S(1)}, pred[64,1024]{1,0:T(8,128)(4,1)S(1)}, bf16[4,64,5,128]{3,1,2,0:T(8,128)(2,1)}, bf16[4,1024,1...) while((s32[]{:T(128)}, f32[4,64,5,128]{3,1,2,0:T(8,128)S(1)}, ...), condition=%wide.region_16.15_spmd, body=%wide.region_12.14_spmd.sunk | while | flops 424142848 | bytes 4571989 | solution.py:75
  277.5 2.6 fusion.244
  291.3 2.6 fusion.244
  306.6 8.7 %fusion.167 = f32[64,2560]{1,0:T(8,128)S(1)} fusion(bf16[2560,2560]{1,0:T(8,128)(2,1)} %get-tuple-element.788, bf16[8,8,20,128]{3,2,1,0:T(8,128)(2,1)S(1)} %bitcast.234), kind=kOutput, calls=%fused_computation.147 | convolution fusion | flops 838860800 | bytes 14090240 | tf_op jit(solution)/shard_map/while/body/eval_jaxpr/cond/branch_1_fun/dot_general | solution.py:159
  331.0 55.7 %reduce-scatter.7.cloned.1.call-done = f32[160,32]{1,0:T(8,128)} async-done(((f32[2560,32]{1,0:T(8,128)}), f32[160,32]{1,0:T(8,128)}) %reduce-scatter.7.cloned.1.call-update) | async-done | bytes 20496
  388.2 59.9 %reduce-scatter.9.cloned.1.call-done = f32[160,32]{1,0:T(8,128)} async-done(((f32[2560,32]{1,0:T(8,128)}), f32[160,32]{1,0:T(8,128)}) %reduce-scatter.9.cloned.1.call-update) | async-done | bytes 20496
  (139 shorter events, 102.7 us)
Async XLA Ops:
  7.2 3.2 copy-start.10
  7.2 4.4 copy-start.9
  7.2 41.6 %copy-start.7 = (bf16[1,160,32]{1,2,0:T(8,128)(2,1)S(1)}, bf16[1,160,32]{1,2,0:T(8,128)(2,1)}, u32[]{:S(2)}) copy-start(bf16[1,160,32]{1,2,0:T(8,128)(2,1)} %param.25) | copy-start | bytes 30724
  7.2 41.7 %copy-start.8 = (bf16[1,160,32]{1,2,0:T(8,128)(2,1)S(1)}, bf16[1,160,32]{1,2,0:T(8,128)(2,1)}, u32[]{:S(2)}) copy-start(bf16[1,160,32]{1,2,0:T(8,128)(2,1)} %param.26) | copy-start | bytes 30724
  7.2 41.8 %copy-start.5 = (bf16[1,1,1024,512]{3,2,1,0:T(8,128)(2,1)S(1)}, bf16[1,1,1024,512]{3,2,1,0:T(8,128)(2,1)}, u32[]{:S(2)}) copy-start(bf16[1,1,1024,512]{3,2,1,0:T(8,128)(2,1)} %param.22) | copy-start | bytes 3145732
  7.2 118.5 %all-gather.2.cloned.1.call-start = ((), (), s32[]{:S(2)}) async-start(), calls=%async_computation.2 | async-start | bytes 13926400 | tf_op jit(solution)/shard_map/all_gather | solution.py:114
  8.0 378.7 %reduce-scatter.7.cloned.1.call-start = ((), (), s32[]{:S(2)}) async-start(), calls=%async_computation.3 | async-start | bytes 1392640
  49.6 27.0 %copy-start.3 = (bf16[1,1,1024,512]{2,3,1,0:T(8,128)(2,1)}, bf16[1,1,1024,512]{2,3,1,0:T(8,128)(2,1)S(1)}, u32[]{:S(2)}) copy-start(bf16[1,1,1024,512]{2,3,1,0:T(8,128)(2,1)S(1)} %copy.53) | copy-start | bytes 3145732
  49.6 25.1 %copy-start.2 = (bf16[1,1,2,64,2560]{4,3,2,1,0:T(8,128)(2,1)S(1)}, bf16[1,1,2,64,2560]{4,3,2,1,0:T(8,128)(2,1)}, u32[]{:S(2)}) copy-start(bf16[1,1,2,64,2560]{4,3,2,1,0:T(8,128)(2,1)} %param.20) | copy-start | bytes 1966084
  77.8 2.3 copy-start
  140.1 0.8 copy-start.1
  141.0 69.1 %collective-permute-start = (bf16[64,2560]{1,0:T(8,128)(2,1)}, bf16[64,2560]{1,0:T(8,128)(2,1)S(1)}, u32[]{:S(2)}, u32[]{:S(2)}) collective-permute-start(bf16[64,2560]{1,0:T(8,128)(2,1)} %get-tuple-element.1605), channel_id=1, source_target_pairs={{16,0},{17,1},{18,2},{19,3},{20,4},{21,5},{22,6},{23,7},{24,8},{25... | collective-permute-start | bytes 983048 | tf_op jit(solution)/shard_map/while/body/eval_jaxpr/ppermute | solution.py:18
  262.3 11.5 %collective-permute-start = (bf16[64,2560]{1,0:T(8,128)(2,1)}, bf16[64,2560]{1,0:T(8,128)(2,1)S(1)}, u32[]{:S(2)}, u32[]{:S(2)}) collective-permute-start(bf16[64,2560]{1,0:T(8,128)(2,1)} %get-tuple-element.1605), channel_id=1, source_target_pairs={{16,0},{17,1},{18,2},{19,3},{20,4},{21,5},{22,6},{23,7},{24,8},{25... | collective-permute-start | bytes 983048 | tf_op jit(solution)/shard_map/while/body/eval_jaxpr/ppermute | solution.py:18
  328.5 119.7 %reduce-scatter.9.cloned.1.call-start = ((), (), s32[]{:S(2)}) async-start(), calls=%async_computation.4 | async-start | bytes 1392640
Sparse Core Ops, SparseCore 0:
  10.3 115.3 all-gather.1
  328.6 58.0 reduce-scatter.6
  390.7 57.3 reduce-scatter.8
where the time goes:
time: 458 us; the launch traced here: 456 us
  waiting for transfers between devices  213 us (47%)
  matrix products  87.3 us (19%)
  blocking collectives  84 us (18%)
  local copies, waits for them, and re-layouts  32 us (7%)
  other arithmetic  22.6 us (5%)
  between operations  14.7 us (3%)
    unnamed x5, waiting for transfers between devices  116 us
    ppermute x2, waiting for transfers between devices, passed_along(): lax.ppermute(value, axis, [(source, source + steps) for source in range(f...  77.8 us
    unnamed x1, blocking collectives  36.8 us
    all_gather x1, blocking collectives, per_device(): lax.all_gather(adapter_bt, 'dp', axis=1, tiled=True)  24.8 us
    all_gather x1, blocking collectives, per_device(): lax.all_gather(adapter_a, 'dp', axis=1, tiled=True)  22.4 us
    sub x8, matrix products, one_head(): expo = jnp.exp(scores - highest)  20.9 us
    all_gather x1, waiting for transfers between devices, per_device(): lax.all_gather(query_weight, 'dp', axis=1, tiled=True)  18.5 us
    unnamed x33, local copies, waits for them, and re-layouts  18.1 us
  transfers between devices with their start and end apart: 5, of which 5 were waited for; matrix products, arithmetic and copies ran while one was open for 4% of the time, Pallas kernels for 0%

commit v1 on v0

v1 whole, which is shorter than its diff:
```python
import jax
import jax.numpy as jnp
from jax import lax
from jax.experimental import pallas as pl
from jax.experimental.pallas import tpu as pltpu
from jax.sharding import PartitionSpec as P

HEADS = 20
KV_HEADS = 4
HEAD_DIM = 128
GROUP = HEADS // KV_HEADS

norm_eps = 1e-06
rope_base = 1000000.0
SCALE = 1.0 / HEAD_DIM**0.5

NT = (((1,), (1,)), ((), ()))
TN = (((0,), (0,)), ((), ()))


def dot(a, b, dims=(((1,), (0,)), ((), ()))):
    return lax.dot_general(a, b, dims, preferred_element_type=jnp.float32)


def rope_tables(positions):
    half = HEAD_DIM // 2
    expon = jnp.arange(half, dtype=jnp.float32) * (2.0 / HEAD_DIM)
    inverse = rope_base ** (-expon)
    angles = positions.astype(jnp.float32)[:, None] * inverse[None, :]
    cosine, sine = jnp.cos(angles), jnp.sin(angles)
    return (
        jnp.concatenate([cosine, cosine], axis=1),
        jnp.concatenate([-sine, sine], axis=1),
    )


def query_kernel(normed, lowrank, weight, factor_bt, cosine, sine, rotated):
    query = dot(normed[...], weight[...]) + dot(lowrank[...], factor_bt[...], NT)
    for j in range(GROUP):
        part = query[:, j * HEAD_DIM : (j + 1) * HEAD_DIM]
        turned = part * cosine[...] + pltpu.roll(part, HEAD_DIM // 2, 1) * sine[...]
        rotated[:, j * HEAD_DIM : (j + 1) * HEAD_DIM] = turned.astype(jnp.bfloat16)


def project(normed, lowrank, weight, factor_bt, cosine, sine):
    rows, width = normed.shape
    features = weight.shape[1]
    rank = lowrank.shape[1]
    block = features // KV_HEADS
    return pl.pallas_call(
        query_kernel,
        grid=(KV_HEADS,),
        in_specs=[
            pl.BlockSpec((rows, width), lambda h: (0, 0)),
            pl.BlockSpec((rows, rank), lambda h: (0, 0)),
            pl.BlockSpec((width, block), lambda h: (0, h)),
            pl.BlockSpec((block, rank), lambda h: (h, 0)),
            pl.BlockSpec((rows, HEAD_DIM), lambda h: (0, 0)),
            pl.BlockSpec((rows, HEAD_DIM), lambda h: (0, 0)),
        ],
        out_specs=pl.BlockSpec((rows, block), lambda h: (0, h)),
        out_shape=jax.ShapeDtypeStruct((rows, features), jnp.bfloat16),
        name="project",
    )(normed, lowrank, weight, factor_bt, cosine, sine)


def backward_kernel(
    micro,
    rotated,
    upstream,
    keys,
    values,
    bias,
    cosine,
    sine,
    weight,
    factor_bt,
    factor_a,
    rows_in,
    reciprocal,
    gain,
    kept_dquery,
    kept_middle,
    input_gradient,
    dquery,
    middle,
    total,
    middle_sum,
):
    h = pl.program_id(0)
    block = GROUP * HEAD_DIM
    for j in range(GROUP):
        at = slice(j * HEAD_DIM, (j + 1) * HEAD_DIM)
        where = pl.ds(pl.multiple_of(h * block + j * HEAD_DIM, HEAD_DIM), HEAD_DIM)
        scores = dot(rotated[0, :, at], keys[...], NT) * SCALE + bias[0]
        highest = jnp.max(scores, axis=-1, keepdims=True)
        expo = jnp.exp(scores - highest)
        probs = expo * (1.0 / jnp.sum(expo, axis=-1, keepdims=True))
        rounded = probs.astype(jnp.bfloat16).astype(jnp.float32)
        dprobs = dot(upstream[:, where], values[...], NT)
        delta = jnp.sum(rounded * dprobs, axis=-1, keepdims=True)
        dscores = (probs * (dprobs - delta) * SCALE).astype(jnp.bfloat16)
        drot = dot(dscores, keys[...])
        turned = drot * cosine[0] - pltpu.roll(drot, HEAD_DIM // 2, 1) * sine[0]
        dquery[0, :, at] = turned.astype(jnp.bfloat16)
    mine = dquery[0]
    part = dot(mine, weight[...], NT)
    low = dot(mine, factor_bt[...])

    @pl.when(h == 0)
    def _():
        total[...] = part
        middle_sum[...] = low

    @pl.when(h > 0)
    def _():
        total[...] += part
        middle_sum[...] += low

    @pl.when(h == pl.num_programs(0) - 1)
    def _():
        mid = middle_sum[...].astype(jnp.bfloat16)
        middle[0] = mid
        dh = (total[...] + dot(mid, factor_a[...], NT)) * gain[...]
        scaled = rows_in[0].astype(jnp.float32) * reciprocal[0]
        mean = jnp.mean(dh * scaled, axis=1, keepdims=True)
        result = upstream[...].astype(jnp.float32) + reciprocal[0] * (dh - scaled * mean)
        input_gradient[...] = result.astype(jnp.bfloat16)


def backward(
    micro,
    rotated,
    upstream,
    keys,
    values,
    bias,
    cosine,
    sine,
    weight,
    factor_bt,
    factor_a,
    rows_in,
    reciprocal,
    gain,
    kept,
):
    micros, tokens, features = rotated.shape
    width = weight.shape[0]
    rank = factor_a.shape[1]
    ctx = keys.shape[0]
    block = features // KV_HEADS
    whole = lambda *dims: pl.BlockSpec(dims, lambda h, m: (0,) * len(dims))
    of_micro = lambda *dims: pl.BlockSpec(
        (1, *dims), lambda h, m: (m[0],) + (0,) * len(dims)
    )
    untouched = pl.BlockSpec(memory_space=pl.ANY)
    return pl.pallas_call(
        backward_kernel,
        grid_spec=pltpu.PrefetchScalarGridSpec(
            num_scalar_prefetch=1,
            grid=(KV_HEADS,),
            in_specs=[
                pl.BlockSpec((1, tokens, block), lambda h, m: (m[0], 0, h)),
                whole(tokens, features),
                pl.BlockSpec((ctx, HEAD_DIM), lambda h, m: (0, h)),
                pl.BlockSpec((ctx, HEAD_DIM), lambda h, m: (0, h)),
                of_micro(tokens, ctx),
                of_micro(tokens, HEAD_DIM),
                of_micro(tokens, HEAD_DIM),
                pl.BlockSpec((width, block), lambda h, m: (0, h)),
                pl.BlockSpec((block, rank), lambda h, m: (h, 0)),
                whole(width, rank),
                of_micro(tokens, width),
                of_micro(tokens, 1),
                whole(1, width),
                untouched,
                untouched,
            ],
            out_specs=[
                whole(tokens, width),
                pl.BlockSpec((1, tokens, block), lambda h, m: (m[0], 0, h)),
                of_micro(tokens, rank),
            ],
            scratch_shapes=[
                pltpu.VMEM((tokens, width), jnp.float32),
                pltpu.VMEM((tokens, rank), jnp.float32),
            ],
        ),
        out_shape=[
            jax.ShapeDtypeStruct((tokens, width), jnp.bfloat16),
            jax.ShapeDtypeStruct((micros, tokens, features), jnp.bfloat16),
            jax.ShapeDtypeStruct((micros, tokens, rank), jnp.bfloat16),
        ],
        input_output_aliases={14: 1, 15: 2},
        name="backward",
    )(
        micro,
        rotated,
        upstream,
        keys,
        values,
        bias,
        cosine,
        sine,
        weight,
        factor_bt,
        factor_a,
        rows_in,
        reciprocal,
        gain,
        *kept,
    )


def gather_small(adapter_a, adapter_bt, norm_gain):
    count = lax.axis_size("dp")
    share, rank = adapter_a.shape
    packed = jnp.concatenate([adapter_a, adapter_bt, norm_gain[:, None]], axis=1)
    sent = jnp.broadcast_to(packed[None], (count, *packed.shape))
    got = lax.all_to_all(sent, "dp", split_axis=0, concat_axis=0, tiled=True)
    got = got.reshape(count * share, 2 * rank + 1)
    return got[:, :rank], got[:, rank : 2 * rank], got[:, 2 * rank]


def summed_shares(grad_a, grad_bt):
    count = lax.axis_size("dp")
    width, rank = grad_a.shape
    share = width // count
    both = jnp.concatenate([grad_a, grad_bt], axis=1).reshape(count, share, 2 * rank)
    packed = jnp.concatenate([both[:, : share // 2], both[:, share // 2 :]], axis=2)
    got = lax.all_to_all(packed, "dp", split_axis=0, concat_axis=0, tiled=True)
    total = jnp.sum(got, axis=0)
    total = jnp.concatenate([total[:, : 2 * rank], total[:, 2 * rank :]], axis=0)
    return total[:, :rank], total[:, rank:]


def per_device(
    layer_inputs,
    top_grad,
    keys,
    values,
    query_weight,
    adapter_a,
    adapter_bt,
    norm_gain,
    offsets,
    segments,
):
    rows_in = layer_inputs[0, 0]
    micros, tokens, width = rows_in.shape
    rows = micros * tokens
    ctx = keys.shape[2]
    keys, values = keys[0, 0], values[0, 0]
    features = query_weight.shape[2]

    weight = lax.all_gather(query_weight[0], "dp", axis=0, tiled=True)
    factor_a, factor_bt, gain = gather_small(adapter_a[0], adapter_bt[0], norm_gain[0])

    flat = rows_in.reshape(rows, width).astype(jnp.float32)
    reciprocal = lax.rsqrt(jnp.mean(flat * flat, axis=1, keepdims=True) + norm_eps)
    gain = gain.astype(jnp.float32)[None, :]
    normed = (flat * reciprocal * gain).astype(jnp.bfloat16)
    lowrank = dot(normed, factor_a).astype(jnp.bfloat16)

    positions = (
        offsets[0][:, None] + jnp.arange(tokens, dtype=jnp.int32)[None, :]
    ).reshape(rows)
    seg_row = segments[0]
    place = jnp.arange(ctx, dtype=jnp.int32)
    query_seg = jnp.take(seg_row, positions)
    visible = (place[None, :] <= positions[:, None]) & (
        (seg_row[None, :] == 0) | (seg_row[None, :] == query_seg[:, None])
    )
    bias = jnp.where(visible, 0.0, -1e30).astype(jnp.float32)
    cosine, sine = rope_tables(positions)

    rotated = project(normed, lowrank, weight, factor_bt, cosine, sine)

    by_micro = lambda a: a.reshape(micros, tokens, a.shape[-1])
    section_count = lax.axis_size("pipe")
    section = lax.axis_index("pipe")
    last = section_count - 1
    kept = (
        jnp.zeros((micros, tokens, features), jnp.bfloat16),
        jnp.zeros((micros, tokens, adapter_a.shape[2]), jnp.bfloat16),
    )
    results = []
    incoming = None
    for step in range(section_count + micros - 1):
        micro = jnp.clip(step - (last - section), 0, micros - 1)
        own = top_grad[0, min(step, micros - 1)]
        upstream = own if step == 0 else jnp.where(section == last, own, incoming)
        result, *kept = backward(
            micro.reshape(1).astype(jnp.int32),
            by_micro(rotated),
            upstream,
            keys,
            values,
            by_micro(bias),
            by_micro(cosine),
            by_micro(sine),
            weight,
            factor_bt,
            factor_a,
            rows_in,
            by_micro(reciprocal),
            gain,
            kept,
        )
        results.append(result)
        if step < section_count + micros - 2:
            incoming = lax.ppermute(
                result, "pipe", [(s, s - 1) for s in range(1, section_count)]
            )

    def of_micro(m):
        chosen = results[m]
        for back in range(1, section_count):
            chosen = jnp.where(last - section == back, results[m + back], chosen)
        return chosen

    grads = jnp.stack([of_micro(m) for m in range(micros)])
    dquery = kept[0].reshape(rows, features)
    middle = kept[1].reshape(rows, -1)
    share_a, share_bt = summed_shares(dot(normed, middle, TN), dot(dquery, lowrank, TN))
    return (grads[None, None], share_a[None], share_bt[None])


def solution(mesh):
    placed = (
        P("pipe", "dp", None, None, None),
        P("dp", None, None, None),
        P("pipe", "dp", None, None),
        P("pipe", "dp", None, None),
        P("pipe", "dp", None),
        P("pipe", "dp", None),
        P("pipe", "dp", None),
        P("pipe", "dp"),
        P("dp", None),
        P("dp", None),
    )
    return jax.shard_map(
        per_device,
        mesh=mesh,
        in_specs=placed,
        out_specs=(
            P("pipe", "dp", None, None, None),
            P("pipe", "dp", None),
            P("pipe", "dp", None),
        ),
        check_vma=False,
    )
```

time: 458 us -> 256 us (0.56)
  matrix products: 87.3 us -> 3.3 us
  blocking collectives: 84 us -> 0 us
  waiting for transfers between devices: 213 us -> 134 us
  Pallas kernels: 0 us -> 71 us
  local copies, waits for them, and re-layouts: 32 us -> 9.41 us
  other arithmetic: 22.6 us -> 9.11 us
  starting transfers between devices: 2.68 us -> 13.8 us
    unnamed x5 -> x1, waiting for transfers between devices: 116 us -> 0.68 us
    pallas_call x0 -> x4, Pallas kernels: none -> 71 us  [the longest x3 63.3 us: backward(): pl.pallas_call(backward_kernel, grid_spec=pltpu.PrefetchScalarGridSpec(nu...]
    all_gather x1, waiting for transfers between devices: 18.5 us -> 83.5 us  [per_device(): weight = lax.all_gather(query_weight[0], 'dp', axis=0, tiled=True)]
    dot_general x29 -> x3, matrix products: 66.4 us -> 3.3 us  [dot(): return lax.dot_general(a, b, dims, preferred_element_type=jnp.float32)]
    ppermute x2, waiting for transfers between devices: 77.8 us -> 20.1 us  [per_device(): lax.ppermute(result, 'pipe', [(s, s - 1) for s in range(1, section_count)])]
    all_gather x2 -> x0, blocking collectives: 47.2 us -> none  [the longest x1 24.8 us: per_device(): lax.all_gather(adapter_bt, 'dp', axis=1, tiled=True)]
    unnamed x1 -> x0, blocking collectives: 36.8 us -> none
    all_to_all x0 -> x2, waiting for transfers between devices: none -> 30.1 us  [the longest x1 15.6 us: summed_shares(): got = lax.all_to_all(packed, 'dp', split_axis=0, concat_axis=0, tiled=True)]
  transfers between devices with their start and end apart: 5 -> 5, of which waited for: 5 -> 5; matrix products, arithmetic and copies ran while one was open for 4% -> 5% of each run, Pallas kernels for 0% -> 0%
where the time goes in v1:
time: 256 us; the launch traced here: 255 us
  waiting for transfers between devices  134 us (52%)
  Pallas kernels  71 us (28%)
  between operations  14.3 us (6%)
  starting transfers between devices  13.8 us (5%)
  local copies, waits for them, and re-layouts  9.41 us (4%)
  other arithmetic  9.11 us (4%)
  matrix products  3.3 us (1%)
    all_gather x1, waiting for transfers between devices, per_device(): weight = lax.all_gather(query_weight[0], 'dp', axis=0, tiled=True)  83.5 us
    pallas_call x3, Pallas kernels, backward(): pl.pallas_call(backward_kernel, grid_spec=pltpu.PrefetchScalarGridSpec(nu...  63.3 us
    ppermute x2, waiting for transfers between devices, per_device(): lax.ppermute(result, 'pipe', [(s, s - 1) for s in range(1, section_count)])  20.1 us
    all_to_all x1, waiting for transfers between devices, summed_shares(): got = lax.all_to_all(packed, 'dp', split_axis=0, concat_axis=0, tiled=True)  15.6 us
    all_to_all x1, waiting for transfers between devices, gather_small(): got = lax.all_to_all(sent, 'dp', split_axis=0, concat_axis=0, tiled=True)  14.6 us
    pallas_call x1, Pallas kernels, project(): pl.pallas_call(query_kernel, grid=(KV_HEADS,), in_specs=[pl.BlockSpec((ro...  7.78 us
    all_to_all x1, starting transfers between devices, gather_small(): got = lax.all_to_all(sent, 'dp', split_axis=0, concat_axis=0, tiled=True)  7.36 us
  transfers between devices with their start and end apart: 5, of which 5 were waited for; matrix products, arithmetic and copies ran while one was open for 5% of the time, Pallas kernels for 0%

profile of v1, /device:TPU:0, one launch (start us, length us, event | category | flops | bytes accessed | tf_op | source)
XLA Modules:
  0.0 255.4 jit_solution(12212443935831009658)
XLA Ops:
  7.9 0.8 pad_maximum_fusion.7
  8.8 0.9 broadcast_in_dim.42
  9.6 7.4 %all-to-all-start = ((bf16[16,160,65]{1,2,0:T(8,128)(2,1)}), bf16[16,160,65]{1,2,0:T(8,128)(2,1)S(1)}, u32[]{:S(2)}, u32[]{:S(2)}) async-start(bf16[16,160,65]{1,2,0:T(8,128)(2,1)} %broadcast_in_dim.42), calls=%async_computation | async-start | bytes 1179648 | tf_op jit(solution)/shard_map/all_to_all | solution.py:221
  17.2 1.0 gather_fusion
  21.6 1.0 fusion.3.bias
  23.4 14.6 %all-to-all-done = bf16[16,160,65]{1,2,0:T(8,128)(2,1)S(1)} async-done(((bf16[16,160,65]{1,2,0:T(8,128)(2,1)}), bf16[16,160,65]{1,2,0:T(8,128)(2,1)S(1)}, u32[]{:S(2)}, u32[]{:S(2)}) %all-to-all-start) | async-done | bytes 332832 | tf_op jit(solution)/shard_map/all_to_all | solution.py:221
  39.7 0.9 convolution_convert_fusion.lowrank
  40.7 1.3 fusion.12
  42.0 83.5 %all-gather.3.cloned.1.call-done = bf16[1,2560,2560]{2,1,0:T(8,128)(2,1)} async-done(((bf16[1,160,2560]{2,1,0:T(8,128)(2,1)}), bf16[1,2560,2560]{2,1,0:T(8,128)(2,1)}) %all-gather.3.cloned.1.call-update) | async-done | bytes 13107216 | tf_op jit(solution)/shard_map/all_gather | solution.py:257
  125.4 7.8 %project.1 = bf16[128,2560]{1,0:T(8,128)(2,1)} custom-call(bf16[128,2560]{1,0:T(8,128)(2,1)} %copy-done.3, bf16[128,32]{1,0:T(8,128)(2,1)} %convolution_convert_fusion.lowrank, bf16[2560,2560]{1,0:T(8,128)(2,1)} %bitcast.48, bf16[2560,32]{1,0:T(8,128)(2,1)} %get-tuple-element.30.factor_bt, f32[128,128]{1,0:T(8,128)} %get-tuple-element.47.cosine, ...), custom_call_target="tpu_custom_call" | custom-call | tf_op jit(solution)/shard_map/project/pallas_call | solution.py:50
  133.2 0.9 broadcast_in_dim.46.kept_dquery
  134.7 21.1 %backward.3 = (bf16[64,2560]{1,0:T(8,128)(2,1)}, bf16[2,64,2560]{2,1,0:T(8,128)(2,1)}, bf16[2,64,32]{2,1,0:T(8,128)(2,1)}) custom-call(s32[1]{0:T(128)} %bitcast.10.micro, bf16[2,64,2560]{2,1,0:T(8,128)(2,1)} %bitcast.58, bf16[64,2560]{1,0:T(8,128)(2,1)} %slice_bitcast_fusion.upstream, ...), custom_call_target="tpu_custom_call", output_to_operand_aliasing={{1}: (14, {}), {2}: (15, {})} | custom-call | tf_op jit(solution)/shard_map/backward/pallas_call | solution.py:158
  155.8 1.3 collective-permute-start
  157.1 10.7 %collective-permute-done = bf16[64,2560]{1,0:T(8,128)(2,1)S(1)} collective-permute-done((bf16[64,2560]{1,0:T(8,128)(2,1)}, bf16[64,2560]{1,0:T(8,128)(2,1)S(1)}, u32[]{:S(2)}, u32[]{:S(2)}) %collective-permute-start) | collective-permute-done | bytes 327712 | tf_op jit(solution)/shard_map/ppermute | solution.py:313
  168.6 21.1 %backward.4 = (bf16[64,2560]{1,0:T(8,128)(2,1)}, bf16[2,64,2560]{2,1,0:T(8,128)(2,1)}, bf16[2,64,32]{2,1,0:T(8,128)(2,1)}) custom-call(s32[1]{0:T(128)} %bitcast.micro, bf16[2,64,2560]{2,1,0:T(8,128)(2,1)} %bitcast.59, bf16[64,2560]{1,0:T(8,128)(2,1)} %bitcast_select_fusion.1.upstream, ...), custom_call_target="tpu_custom_call", output_to_operand_aliasing={{1}: (14, {}), {2}: (15, {})} | custom-call | tf_op jit(solution)/shard_map/backward/pallas_call | solution.py:158
  189.7 1.5 collective-permute-start.1
  191.4 9.5 %collective-permute-done.1 = bf16[64,2560]{1,0:T(8,128)(2,1)S(1)} collective-permute-done((bf16[64,2560]{1,0:T(8,128)(2,1)}, bf16[64,2560]{1,0:T(8,128)(2,1)S(1)}, u32[]{:S(2)}, u32[]{:S(2)}) %collective-permute-start.1) | collective-permute-done | bytes 327712 | tf_op jit(solution)/shard_map/ppermute | solution.py:313
  201.6 21.1 %backward.5 = (bf16[64,2560]{1,0:T(8,128)(2,1)}, bf16[2,64,2560]{2,1,0:T(8,128)(2,1)}, bf16[2,64,32]{2,1,0:T(8,128)(2,1)}) custom-call(s32[1]{0:T(128)} %bitcast.19.micro, bf16[2,64,2560]{2,1,0:T(8,128)(2,1)} %bitcast.60, bf16[64,2560]{1,0:T(8,128)(2,1)} %bitcast_select_fusion.upstream, ...), custom_call_target="tpu_custom_call", output_to_operand_aliasing={{1}: (14, {}), {2}: (15, {})} | custom-call | tf_op jit(solution)/shard_map/backward/pallas_call | solution.py:158
  222.7 1.3 fusion.15
  224.0 1.0 fusion.14
  225.7 1.1 pad_maximum_fusion.1
  226.8 3.6 %all-to-all-start.1 = ((f32[16,80,128]{2,1,0:T(8,128)}), f32[16,80,128]{2,1,0:T(8,128)S(1)}, u32[]{:S(2)}, u32[]{:S(2)}) async-start(f32[16,80,128]{2,1,0:T(8,128)} %pad_maximum_fusion.1), calls=%async_computation.1 | async-start | bytes 1310720 | tf_op jit(solution)/shard_map/all_to_all | solution.py:232
  230.5 0.9 maximum_bitcast_fusion
  231.3 15.6 %all-to-all-done.1 = f32[16,80,128]{2,1,0:T(8,128)S(1)} async-done(((f32[16,80,128]{2,1,0:T(8,128)}), f32[16,80,128]{2,1,0:T(8,128)S(1)}, u32[]{:S(2)}, u32[]{:S(2)}) %all-to-all-start.1) | async-done | bytes 655392 | tf_op jit(solution)/shard_map/all_to_all | solution.py:232
  (57 shorter events, 11.4 us)
Async XLA Ops:
  7.2 9.8 %copy-start.9 = (s32[1,2]{1,0:T(1,128)S(1)}, s32[1,2]{1,0:T(1,128)}, u32[]{:S(2)}) copy-start(s32[1,2]{1,0:T(1,128)} %param.18) | copy-start | bytes 28
  7.2 10.0 %copy-start = (s32[1,1024]{1,0:T(1,128)S(1)}, s32[1,1024]{1,0:T(1,128)}, u32[]{:S(2)}) copy-start(s32[1,1024]{1,0:T(1,128)} %param.19) | copy-start | bytes 12292
  7.2 118.3 %all-gather.3.cloned.1.call-start = ((), (), s32[]{:S(2)}) async-start(), calls=%async_computation.2 | async-start | bytes 13926400 | tf_op jit(solution)/shard_map/all_gather | solution.py:257
  7.9 10.5 %copy-start.1 = (bf16[1,1,2,64,2560]{4,3,2,1,0:T(8,128)(2,1)S(1)}, bf16[1,1,2,64,2560]{4,3,2,1,0:T(8,128)(2,1)}, u32[]{:S(2)}) copy-start(bf16[1,1,2,64,2560]{4,3,2,1,0:T(8,128)(2,1)} %param.10) | copy-start | bytes 1966084
  9.6 28.4 %all-to-all-start = ((bf16[16,160,65]{1,2,0:T(8,128)(2,1)}), bf16[16,160,65]{1,2,0:T(8,128)(2,1)S(1)}, u32[]{:S(2)}, u32[]{:S(2)}) async-start(bf16[16,160,65]{1,2,0:T(8,128)(2,1)} %broadcast_in_dim.42), calls=%async_computation | async-start | bytes 1179648 | tf_op jit(solution)/shard_map/all_to_all | solution.py:221
  17.2 5.5 %copy-start.4 = (bf16[1,2,64,2560]{3,2,1,0:T(8,128)(2,1)S(1)}, bf16[1,2,64,2560]{3,2,1,0:T(8,128)(2,1)}, u32[]{:S(2)}) copy-start(bf16[1,2,64,2560]{3,2,1,0:T(8,128)(2,1)} %param.11) | copy-start | bytes 1966084
  39.7 2.2 copy-start.3
  155.8 12.0 %collective-permute-start = (bf16[64,2560]{1,0:T(8,128)(2,1)}, bf16[64,2560]{1,0:T(8,128)(2,1)S(1)}, u32[]{:S(2)}, u32[]{:S(2)}) collective-permute-start(bf16[64,2560]{1,0:T(8,128)(2,1)} %get-tuple-element.12), channel_id=1, source_target_pairs={{16,0},{17,1},{18,2},{19,3},{20,4},{21,5},{22,6},{23,7},{24,8},{25... | collective-permute-start | bytes 983048 | tf_op jit(solution)/shard_map/ppermute | solution.py:313
  168.6 22.6 %copy-start.2 = (bf16[1,1,2,64,2560]{4,3,2,1,0:T(8,128)(2,1)S(1)}, bf16[1,1,2,64,2560]{4,3,2,1,0:T(8,128)(2,1)}, u32[]{:S(2)}) copy-start(bf16[1,1,2,64,2560]{4,3,2,1,0:T(8,128)(2,1)} %param.10) | copy-start | bytes 1966084
  189.7 11.2 %collective-permute-start.1 = (bf16[64,2560]{1,0:T(8,128)(2,1)}, bf16[64,2560]{1,0:T(8,128)(2,1)S(1)}, u32[]{:S(2)}, u32[]{:S(2)}) collective-permute-start(bf16[64,2560]{1,0:T(8,128)(2,1)} %get-tuple-element.15), channel_id=1, source_target_pairs={{16,0},{17,1},{18,2},{19,3},{20,4},{21,5},{22,6},{23,7},{24,8},{25... | collective-permute-start | bytes 983048 | tf_op jit(solution)/shard_map/ppermute | solution.py:313
  201.6 21.1 %copy-start.8 = (bf16[128,32]{1,0:T(8,128)(2,1)S(1)}, bf16[128,32]{1,0:T(8,128)(2,1)}, u32[]{:S(2)}) copy-start(bf16[128,32]{1,0:T(8,128)(2,1)} %convolution_convert_fusion.lowrank) | copy-start | bytes 24580
  225.6 4.7 %copy-start.5 = (bf16[64,2560]{1,0:T(8,128)(2,1)S(1)}, bf16[64,2560]{1,0:T(8,128)(2,1)}, u32[]{:S(2)}) copy-start(bf16[64,2560]{1,0:T(8,128)(2,1)} %get-tuple-element.12) | copy-start | bytes 983044
  225.6 4.7 %copy-start.6 = (bf16[64,2560]{1,0:T(8,128)(2,1)S(1)}, bf16[64,2560]{1,0:T(8,128)(2,1)}, u32[]{:S(2)}) copy-start(bf16[64,2560]{1,0:T(8,128)(2,1)} %get-tuple-element.15) | copy-start | bytes 983044
  225.6 4.7 %copy-start.7 = (bf16[64,2560]{1,0:T(8,128)(2,1)S(1)}, bf16[64,2560]{1,0:T(8,128)(2,1)}, u32[]{:S(2)}) copy-start(bf16[64,2560]{1,0:T(8,128)(2,1)} %get-tuple-element.18) | copy-start | bytes 983044
  226.8 20.2 %all-to-all-start.1 = ((f32[16,80,128]{2,1,0:T(8,128)}), f32[16,80,128]{2,1,0:T(8,128)S(1)}, u32[]{:S(2)}, u32[]{:S(2)}) async-start(f32[16,80,128]{2,1,0:T(8,128)} %pad_maximum_fusion.1), calls=%async_computation.1 | async-start | bytes 1310720 | tf_op jit(solution)/shard_map/all_to_all | solution.py:232
Sparse Core Ops, SparseCore 0:
  10.3 115.0 all-gather.2

commit v2 on v1

--- a/solution.py
+++ b/solution.py
@@ -1,3 +1,5 @@
+import functools
+
 import jax
 import jax.numpy as jnp
 from jax import lax
@@ -64,7 +66,34 @@
     )(normed, lowrank, weight, factor_bt, cosine, sine)
 
 
+def ring_order(count):
+    if count % 4:
+        return list(range(count))
+    chips = count // 2
+    columns = 2 ** ((chips.bit_length() - 1) // 2)
+    lines = chips // columns
+    walk = [(z, 0) for z in range(lines)]
+    for step, z in enumerate(range(lines - 1, -1, -1)):
+        side = range(1, columns) if step % 2 == 0 else range(columns - 1, 0, -1)
+        walk += [(z, x) for x in side]
+    return [(z * columns + x) * 2 + core for z, x in walk for core in range(2)]
+
+
+def reordered(value, order):
+    share = value.shape[-1] // len(order)
+    return jnp.concatenate(
+        [value[..., i * share : (i + 1) * share] for i in order], axis=-1
+    )
+
+
+def stacked(value):
+    return jnp.concatenate(
+        [value[:, j * HEAD_DIM : (j + 1) * HEAD_DIM] for j in range(GROUP)], axis=0
+    )
+
+
 def backward_kernel(
+    order,
     micro,
     rotated,
     upstream,
@@ -79,33 +108,32 @@
     rows_in,
     reciprocal,
     gain,
-    kept_dquery,
-    kept_middle,
-    input_gradient,
-    dquery,
-    middle,
-    total,
-    middle_sum,
+    *rest,
 ):
+    input_gradient, dquery, middle, total, middle_sum = rest[-5:]
     h = pl.program_id(0)
+    tokens = bias.shape[1]
     block = GROUP * HEAD_DIM
+    mine = pl.ds(pl.multiple_of(h * block, HEAD_DIM), block)
+    scores = dot(stacked(rotated[0]), keys[...], NT)
+    dprobs = dot(stacked(upstream[:, mine]), values[...], NT)
+    dscores = []
     for j in range(GROUP):
-        at = slice(j * HEAD_DIM, (j + 1) * HEAD_DIM)
-        where = pl.ds(pl.multiple_of(h * block + j * HEAD_DIM, HEAD_DIM), HEAD_DIM)
-        scores = dot(rotated[0, :, at], keys[...], NT) * SCALE + bias[0]
-        highest = jnp.max(scores, axis=-1, keepdims=True)
-        expo = jnp.exp(scores - highest)
+        at = slice(j * tokens, (j + 1) * tokens)
+        masked = scores[at] * SCALE + bias[0]
+        expo = jnp.exp(masked - jnp.max(masked, axis=-1, keepdims=True))
         probs = expo * (1.0 / jnp.sum(expo, axis=-1, keepdims=True))
         rounded = probs.astype(jnp.bfloat16).astype(jnp.float32)
-        dprobs = dot(upstream[:, where], values[...], NT)
-        delta = jnp.sum(rounded * dprobs, axis=-1, keepdims=True)
-        dscores = (probs * (dprobs - delta) * SCALE).astype(jnp.bfloat16)
-        drot = dot(dscores, keys[...])
-        turned = drot * cosine[0] - pltpu.roll(drot, HEAD_DIM // 2, 1) * sine[0]
-        dquery[0, :, at] = turned.astype(jnp.bfloat16)
-    mine = dquery[0]
-    part = dot(mine, weight[...], NT)
-    low = dot(mine, factor_bt[...])
+        delta = jnp.sum(rounded * dprobs[at], axis=-1, keepdims=True)
+        dscores.append((probs * (dprobs[at] - delta) * SCALE).astype(jnp.bfloat16))
+    drot = dot(jnp.concatenate(dscores, axis=0), keys[...])
+    for j in range(GROUP):
+        part = drot[j * tokens : (j + 1) * tokens]
+        turned = part * cosine[0] - pltpu.roll(part, HEAD_DIM // 2, 1) * sine[0]
+        dquery[0, :, j * HEAD_DIM : (j + 1) * HEAD_DIM] = turned.astype(jnp.bfloat16)
+    dq = dquery[0]
+    part = dot(dq, weight[...], NT)
+    low = dot(dq, factor_bt[...])
 
     @pl.when(h == 0)
     def _():
@@ -124,11 +152,16 @@
         dh = (total[...] + dot(mid, factor_a[...], NT)) * gain[...]
         scaled = rows_in[0].astype(jnp.float32) * reciprocal[0]
         mean = jnp.mean(dh * scaled, axis=1, keepdims=True)
-        result = upstream[...].astype(jnp.float32) + reciprocal[0] * (dh - scaled * mean)
-        input_gradient[...] = result.astype(jnp.bfloat16)
+        change = reciprocal[0] * (dh - scaled * mean)
+        share = change.shape[1] // len(order)
+        for k, i in enumerate(order):
+            here = slice(i * share, (i + 1) * share)
+            result = upstream[:, here].astype(jnp.float32) + change[:, k * share : (k + 1) * share]
+            input_gradient[:, here] = result.astype(jnp.bfloat16)
 
 
 def backward(
+    order,
     micro,
     rotated,
     upstream,
@@ -154,9 +187,8 @@
     of_micro = lambda *dims: pl.BlockSpec(
         (1, *dims), lambda h, m: (m[0],) + (0,) * len(dims)
     )
-    untouched = pl.BlockSpec(memory_space=pl.ANY)
     return pl.pallas_call(
-        backward_kernel,
+        functools.partial(backward_kernel, order),
         grid_spec=pltpu.PrefetchScalarGridSpec(
             num_scalar_prefetch=1,
             grid=(KV_HEADS,),
@@ -174,9 +206,8 @@
                 of_micro(tokens, width),
                 of_micro(tokens, 1),
                 whole(1, width),
-                untouched,
-                untouched,
-            ],
+            ]
+            + [pl.BlockSpec(memory_space=pl.ANY)] * len(kept),
             out_specs=[
                 whole(tokens, width),
                 pl.BlockSpec((1, tokens, block), lambda h, m: (m[0], 0, h)),
@@ -192,7 +223,12 @@
             jax.ShapeDtypeStruct((micros, tokens, features), jnp.bfloat16),
             jax.ShapeDtypeStruct((micros, tokens, rank), jnp.bfloat16),
         ],
-        input_output_aliases={14: 1, 15: 2},
+        input_output_aliases={14: 1, 15: 2} if kept else {},
+        cost_estimate=pl.CostEstimate(
+            flops=2 * tokens * features * (width + 3 * ctx),
+            bytes_accessed=2 * width * features,
+            transcendentals=tokens * HEADS * ctx,
+        ),
         name="backward",
     )(
         micro,
@@ -215,19 +251,18 @@
 
 def gather_small(adapter_a, adapter_bt, norm_gain):
     count = lax.axis_size("dp")
-    share, rank = adapter_a.shape
     packed = jnp.concatenate([adapter_a, adapter_bt, norm_gain[:, None]], axis=1)
     sent = jnp.broadcast_to(packed[None], (count, *packed.shape))
-    got = lax.all_to_all(sent, "dp", split_axis=0, concat_axis=0, tiled=True)
-    got = got.reshape(count * share, 2 * rank + 1)
-    return got[:, :rank], got[:, rank : 2 * rank], got[:, 2 * rank]
-
-
-def summed_shares(grad_a, grad_bt):
+    return lax.all_to_all(sent, "dp", split_axis=0, concat_axis=0, tiled=True)
+
+
+def summed_shares(grad_a, grad_bt, order):
     count = lax.axis_size("dp")
     width, rank = grad_a.shape
     share = width // count
-    both = jnp.concatenate([grad_a, grad_bt], axis=1).reshape(count, share, 2 * rank)
+    walked = grad_a.reshape(count, share, rank)
+    grad_a = jnp.concatenate([walked[order.index(i)][None] for i in range(count)], axis=0)
+    both = jnp.concatenate([grad_a, grad_bt.reshape(count, share, rank)], axis=2)
     packed = jnp.concatenate([both[:, : share // 2], both[:, share // 2 :]], axis=2)
     got = lax.all_to_all(packed, "dp", split_axis=0, concat_axis=0, tiled=True)
     total = jnp.sum(got, axis=0)
@@ -247,19 +282,26 @@
     offsets,
     segments,
 ):
-    rows_in = layer_inputs[0, 0]
-    micros, tokens, width = rows_in.shape
+    order = ring_order(lax.axis_size("dp"))
+    _, _, micros, tokens, width = layer_inputs.shape
     rows = micros * tokens
     ctx = keys.shape[2]
     keys, values = keys[0, 0], values[0, 0]
     features = query_weight.shape[2]
-
-    weight = lax.all_gather(query_weight[0], "dp", axis=0, tiled=True)
-    factor_a, factor_bt, gain = gather_small(adapter_a[0], adapter_bt[0], norm_gain[0])
-
+    rank = adapter_a.shape[2]
+
+    weight = lax.all_gather(
+        query_weight[0], "dp", axis=0, tiled=True, axis_index_groups=[order]
+    )
+    small = gather_small(adapter_a[0], adapter_bt[0], norm_gain[0])
+    factor_bt = small[:, :, rank : 2 * rank].reshape(features, rank)
+    walked = jnp.concatenate([small[i : i + 1] for i in order], axis=0)
+    factor_a = walked[:, :, :rank].reshape(width, rank)
+    gain = walked[:, :, 2 * rank].reshape(1, width).astype(jnp.float32)
+
+    rows_in = reordered(layer_inputs[0, 0], order)
     flat = rows_in.reshape(rows, width).astype(jnp.float32)
     reciprocal = lax.rsqrt(jnp.mean(flat * flat, axis=1, keepdims=True) + norm_eps)
-    gain = gain.astype(jnp.float32)[None, :]
     normed = (flat * reciprocal * gain).astype(jnp.bfloat16)
     lowrank = dot(normed, factor_a).astype(jnp.bfloat16)
 
@@ -281,17 +323,15 @@
     section_count = lax.axis_size("pipe")
     section = lax.axis_index("pipe")
     last = section_count - 1
-    kept = (
-        jnp.zeros((micros, tokens, features), jnp.bfloat16),
-        jnp.zeros((micros, tokens, adapter_a.shape[2]), jnp.bfloat16),
-    )
-    results = []
-    incoming = None
-    for step in range(section_count + micros - 1):
-        micro = jnp.clip(step - (last - section), 0, micros - 1)
-        own = top_grad[0, min(step, micros - 1)]
-        upstream = own if step == 0 else jnp.where(section == last, own, incoming)
+    steps = 2 * last + micros
+    kept, results, arrived = (), [], []
+    for step in range(steps):
+        micro = jnp.clip(step - 2 * (last - section), 0, micros - 1)
+        upstream = top_grad[0, min(step, micros - 1)]
+        if step >= 2:
+            upstream = jnp.where(section == last, upstream, arrived[step - 2])
         result, *kept = backward(
+            order,
             micro.reshape(1).astype(jnp.int32),
             by_micro(rotated),
             upstream,
@@ -309,21 +349,23 @@
             kept,
         )
         results.append(result)
-        if step < section_count + micros - 2:
-            incoming = lax.ppermute(
-                result, "pipe", [(s, s - 1) for s in range(1, section_count)]
+        if step < steps - 2:
+            arrived.append(
+                lax.ppermute(result, "pipe", [(s, s - 1) for s in range(1, section_count)])
             )
 
     def of_micro(m):
         chosen = results[m]
         for back in range(1, section_count):
-            chosen = jnp.where(last - section == back, results[m + back], chosen)
+            chosen = jnp.where(last - section == back, results[m + 2 * back], chosen)
         return chosen
 
     grads = jnp.stack([of_micro(m) for m in range(micros)])
     dquery = kept[0].reshape(rows, features)
     middle = kept[1].reshape(rows, -1)
-    share_a, share_bt = summed_shares(dot(normed, middle, TN), dot(dquery, lowrank, TN))
+    share_a, share_bt = summed_shares(
+        dot(normed, middle, TN), dot(dquery, lowrank, TN), order
+    )
     return (grads[None, None], share_a[None], share_bt[None])
 
 

time: 256 us -> 221 us (0.86)
  waiting for transfers between devices: 134 us -> 96.1 us
  starting transfers between devices: 13.8 us -> 17.2 us
    all_gather x1, waiting for transfers between devices: 83.5 us -> 47 us  [per_device(): lax.all_gather(query_weight[0], 'dp', axis=0, tiled=True, axis_index_grou...]
    ppermute x2, waiting for transfers between devices: 20.1 us -> 16.2 us  [per_device(): lax.ppermute(result, 'pipe', [(s, s - 1) for s in range(1, section_count)])]
    all_to_all x1, starting transfers between devices: 3.59 us -> 7.03 us  [summed_shares(): got = lax.all_to_all(packed, 'dp', split_axis=0, concat_axis=0, tiled=True)]
    pallas_call x3 -> x4, Pallas kernels: 63.3 us -> 63.6 us  [backward(): pl.pallas_call(functools.partial(backward_kernel, order), grid_spec=pltpu...]
  transfers between devices with their start and end apart: 5 -> 5, of which waited for: 5 -> 5; matrix products, arithmetic and copies ran while one was open for 5% -> 7% of each run, Pallas kernels for 0% -> 0%
where the time goes in v2:
time: 221 us
  waiting for transfers between devices  96.1 us (43%)
  Pallas kernels  71.4 us (32%)
  starting transfers between devices  17.2 us (8%)
  between operations  14.4 us (7%)
  local copies, waits for them, and re-layouts  11.1 us (5%)
  other arithmetic  7.79 us (4%)
  matrix products  2.7 us (1%)
    pallas_call x4, Pallas kernels, backward(): pl.pallas_call(functools.partial(backward_kernel, order), grid_spec=pltpu...  63.6 us
    all_gather x1, waiting for transfers between devices, per_device(): lax.all_gather(query_weight[0], 'dp', axis=0, tiled=True, axis_index_grou...  47 us
    all_to_all x1, waiting for transfers between devices, gather_small(): return lax.all_to_all(sent, 'dp', split_axis=0, concat_axis=0, tiled=True)  16.7 us
    ppermute x2, waiting for transfers between devices, per_device(): lax.ppermute(result, 'pipe', [(s, s - 1) for s in range(1, section_count)])  16.2 us
    all_to_all x1, waiting for transfers between devices, summed_shares(): got = lax.all_to_all(packed, 'dp', split_axis=0, concat_axis=0, tiled=True)  15.6 us
    pallas_call x1, Pallas kernels, project(): pl.pallas_call(query_kernel, grid=(KV_HEADS,), in_specs=[pl.BlockSpec((ro...  7.78 us
    all_to_all x1, starting transfers between devices, gather_small(): return lax.all_to_all(sent, 'dp', split_axis=0, concat_axis=0, tiled=True)  7.36 us
    all_to_all x1, starting transfers between devices, summed_shares(): got = lax.all_to_all(packed, 'dp', split_axis=0, concat_axis=0, tiled=True)  7.03 us
  transfers between devices with their start and end apart: 5, of which 5 were waited for; matrix products, arithmetic and copies ran while one was open for 7% of the time, Pallas kernels for 0%

profile of v2, /device:TPU:0, one launch (start us, length us, event | category | flops | bytes accessed | tf_op | source)
XLA Modules:
  0.0 220.8 jit_solution(1611807280220659663)
XLA Ops:
  9.6 7.4 %all-to-all-start = ((bf16[16,160,65]{1,2,0:T(8,128)(2,1)}), bf16[16,160,65]{1,2,0:T(8,128)(2,1)S(1)}, u32[]{:S(2)}, u32[]{:S(2)}) async-start(bf16[16,160,65]{1,2,0:T(8,128)(2,1)} %broadcast_in_dim.35), calls=%async_computation | async-start | bytes 1179648 | tf_op jit(solution)/shard_map/all_to_all | solution.py:256
  17.2 1.0 gather_fusion
  22.8 1.0 fusion.10.bias
  23.8 0.9 slice_bitcast_fusion
  24.7 16.7 %all-to-all-done = bf16[16,160,65]{1,2,0:T(8,128)(2,1)S(1)} async-done(((bf16[16,160,65]{1,2,0:T(8,128)(2,1)}), bf16[16,160,65]{1,2,0:T(8,128)(2,1)S(1)}, u32[]{:S(2)}, u32[]{:S(2)}) %all-to-all-start) | async-done | bytes 332832 | tf_op jit(solution)/shard_map/all_to_all | solution.py:256
  42.4 1.1 copy.49
  43.8 1.0 convolution_convert_fusion.lowrank
  44.8 1.1 fusion.1.normed
  45.9 47.0 %all-gather.3.cloned.1.call-done = bf16[1,2560,2560]{2,1,0:T(8,128)(2,1)} async-done(((bf16[1,160,2560]{2,1,0:T(8,128)(2,1)}), bf16[1,2560,2560]{2,1,0:T(8,128)(2,1)}) %all-gather.3.cloned.1.call-update) | async-done | bytes 13107216 | tf_op jit(solution)/shard_map/all_gather | solution.py:293
  92.8 7.8 %project.1 = bf16[128,2560]{1,0:T(8,128)(2,1)} custom-call(bf16[128,2560]{1,0:T(8,128)(2,1)} %fusion.1.normed, bf16[128,32]{1,0:T(8,128)(2,1)} %convolution_convert_fusion.lowrank, bf16[2560,2560]{1,0:T(8,128)(2,1)} %bitcast.127, bf16[2560,32]{1,0:T(8,128)(2,1)} %bitcast.134, f32[128,128]{1,0:T(8,128)} %get-tuple-element.54.cosine, ...), custom_call_target="tpu_custom_call" | custom-call | tf_op jit(solution)/shard_map/project/pallas_call | solution.py:52
  100.6 15.9 %backward.4 = (bf16[64,2560]{1,0:T(8,128)(2,1)}, bf16[2,64,2560]{2,1,0:T(8,128)(2,1)}, bf16[2,64,32]{2,1,0:T(8,128)(2,1)}) custom-call(s32[1]{0:T(128)} %bitcast.19.micro, bf16[2,64,2560]{2,1,0:T(8,128)(2,1)} %bitcast.152, bf16[64,2560]{1,0:T(8,128)(2,1)} %get-tuple-element.32.upstream, bf16[1024,512]{1,0:T(8,128)(2,1)} %bitcast.139, ...), custom_call_target="tpu_custom_call" | custom-call | flops 1845493760 | bytes 13107200 | tf_op jit(solution)/shard_map/backward/pallas_call | solution.py:190
  116.5 15.9 %backward.5 = (bf16[64,2560]{1,0:T(8,128)(2,1)}, bf16[2,64,2560]{2,1,0:T(8,128)(2,1)}, bf16[2,64,32]{2,1,0:T(8,128)(2,1)}) custom-call(s32[1]{0:T(128)} %bitcast.26.micro, bf16[2,64,2560]{2,1,0:T(8,128)(2,1)} %bitcast.153, bf16[64,2560]{1,0:T(8,128)(2,1)} %get-tuple-element.33.upstream, ...), custom_call_target="tpu_custom_call", output_to_operand_aliasing={{1}: (14, {}), {2}: (15, {})} | custom-call | flops 1845493760 | bytes 13107200 | tf_op jit(solution)/shard_map/backward/pallas_call | solution.py:190
  132.4 1.3 collective-permute-start.1
  133.8 1.5 collective-permute-start
  135.2 9.8 %collective-permute-done.1 = bf16[64,2560]{1,0:T(8,128)(2,1)S(1)} collective-permute-done((bf16[64,2560]{1,0:T(8,128)(2,1)}, bf16[64,2560]{1,0:T(8,128)(2,1)S(1)}, u32[]{:S(2)}, u32[]{:S(2)}) %collective-permute-start.1) | collective-permute-done | bytes 327712 | tf_op jit(solution)/shard_map/ppermute | solution.py:354
  145.1 6.4 %collective-permute-done = bf16[64,2560]{1,0:T(8,128)(2,1)S(1)} collective-permute-done((bf16[64,2560]{1,0:T(8,128)(2,1)S(1)}, bf16[64,2560]{1,0:T(8,128)(2,1)S(1)}, u32[]{:S(2)}, u32[]{:S(2)}) %collective-permute-start) | collective-permute-done | bytes 327712 | tf_op jit(solution)/shard_map/ppermute | solution.py:354
  151.4 0.9 broadcast_select_fusion.1
  152.3 15.9 %backward.6 = (bf16[64,2560]{1,0:T(8,128)(2,1)}, bf16[2,64,2560]{2,1,0:T(8,128)(2,1)}, bf16[2,64,32]{2,1,0:T(8,128)(2,1)}) custom-call(s32[1]{0:T(128)} %bitcast.micro, bf16[2,64,2560]{2,1,0:T(8,128)(2,1)} %bitcast.154, bf16[64,2560]{1,0:T(8,128)(2,1)} %get-tuple-element.30.upstream, ...), custom_call_target="tpu_custom_call", output_to_operand_aliasing={{1}: (14, {}), {2}: (15, {})} | custom-call | flops 1845493760 | bytes 13107200 | tf_op jit(solution)/shard_map/backward/pallas_call | solution.py:190
  168.2 15.9 %backward.7 = (bf16[64,2560]{1,0:T(8,128)(2,1)}, bf16[2,64,2560]{2,1,0:T(8,128)(2,1)}, bf16[2,64,32]{2,1,0:T(8,128)(2,1)}) custom-call(s32[1]{0:T(128)} %bitcast.28.micro, bf16[2,64,2560]{2,1,0:T(8,128)(2,1)} %bitcast.155, bf16[64,2560]{1,0:T(8,128)(2,1)} %get-tuple-element.31.upstream, ...), custom_call_target="tpu_custom_call", output_to_operand_aliasing={{1}: (14, {}), {2}: (15, {})} | custom-call | flops 1845493760 | bytes 13107200 | tf_op jit(solution)/shard_map/backward/pallas_call | solution.py:190
  184.2 1.2 convolution_bitcast_fusion
  187.5 1.2 copy.56
  188.7 7.0 %all-to-all-start.1 = ((f32[16,80,128]{2,1,0:T(8,128)}), f32[16,80,128]{2,1,0:T(8,128)S(1)}, u32[]{:S(2)}, u32[]{:S(2)}) async-start(f32[16,80,128]{2,1,0:T(8,128)} %copy.56), calls=%async_computation.1 | async-start | bytes 1310720 | tf_op jit(solution)/shard_map/all_to_all | solution.py:267
  195.8 0.9 maximum_bitcast_fusion
  196.7 15.6 %all-to-all-done.1 = f32[16,80,128]{2,1,0:T(8,128)S(1)} async-done(((f32[16,80,128]{2,1,0:T(8,128)}), f32[16,80,128]{2,1,0:T(8,128)S(1)}, u32[]{:S(2)}, u32[]{:S(2)}) %all-to-all-start.1) | async-done | bytes 655392 | tf_op jit(solution)/shard_map/all_to_all | solution.py:267
  (91 shorter events, 12.1 us)
Async XLA Ops:
  7.2 9.8 %copy-start.12 = (s32[1,2]{1,0:T(1,128)S(1)}, s32[1,2]{1,0:T(1,128)}, u32[]{:S(2)}) copy-start(s32[1,2]{1,0:T(1,128)} %param.18) | copy-start | bytes 28
  7.2 10.0 %copy-start = (s32[1,1024]{1,0:T(1,128)S(1)}, s32[1,1024]{1,0:T(1,128)}, u32[]{:S(2)}) copy-start(s32[1,1024]{1,0:T(1,128)} %param.19) | copy-start | bytes 12292
  7.2 85.7 %all-gather.3.cloned.1.call-start = ((), (), s32[]{:S(2)}) async-start(), calls=%async_computation.2 | async-start | bytes 13926400 | tf_op jit(solution)/shard_map/all_gather | solution.py:293
  7.9 10.5 %copy-start.6 = (bf16[1,1,2,64,2560]{4,3,2,1,0:T(8,128)(2,1)S(1)}, bf16[1,1,2,64,2560]{4,3,2,1,0:T(8,128)(2,1)}, u32[]{:S(2)}) copy-start(bf16[1,1,2,64,2560]{4,3,2,1,0:T(8,128)(2,1)} %param.10) | copy-start | bytes 1966084
  9.6 31.8 %all-to-all-start = ((bf16[16,160,65]{1,2,0:T(8,128)(2,1)}), bf16[16,160,65]{1,2,0:T(8,128)(2,1)S(1)}, u32[]{:S(2)}, u32[]{:S(2)}) async-start(bf16[16,160,65]{1,2,0:T(8,128)(2,1)} %broadcast_in_dim.35), calls=%async_computation | async-start | bytes 1179648 | tf_op jit(solution)/shard_map/all_to_all | solution.py:256
  19.1 25.7 %copy-start.1 = (bf16[2,64,2560]{2,1,0:T(8,128)(2,1)}, bf16[2,64,2560]{2,1,0:T(8,128)(2,1)S(1)}, u32[]{:S(2)}) copy-start(bf16[2,64,2560]{2,1,0:T(8,128)(2,1)S(1)} %concatenate.51.rows_in) | copy-start | bytes 1966084
  20.1 3.7 %copy-start.5 = (bf16[1,2,64,2560]{3,2,1,0:T(8,128)(2,1)S(1)}, bf16[1,2,64,2560]{3,2,1,0:T(8,128)(2,1)}, u32[]{:S(2)}) copy-start(bf16[1,2,64,2560]{3,2,1,0:T(8,128)(2,1)} %param.11) | copy-start | bytes 1966084
  43.8 2.1 copy-start.3
  116.5 17.2 %copy-start.7 = (bf16[64,2560]{1,0:T(8,128)(2,1)S(1)}, bf16[64,2560]{1,0:T(8,128)(2,1)}, u32[]{:S(2)}) copy-start(bf16[64,2560]{1,0:T(8,128)(2,1)} %get-tuple-element.15) | copy-start | bytes 983044
  132.4 12.6 %collective-permute-start.1 = (bf16[64,2560]{1,0:T(8,128)(2,1)}, bf16[64,2560]{1,0:T(8,128)(2,1)S(1)}, u32[]{:S(2)}, u32[]{:S(2)}) collective-permute-start(bf16[64,2560]{1,0:T(8,128)(2,1)} %get-tuple-element.21), channel_id=1, source_target_pairs={{16,0},{17,1},{18,2},{19,3},{20,4},{21,5},{22,6},{23,7},{24,8},{25... | collective-permute-start | bytes 983048 | tf_op jit(solution)/shard_map/ppermute | solution.py:354
  133.8 17.7 %collective-permute-start = (bf16[64,2560]{1,0:T(8,128)(2,1)S(1)}, bf16[64,2560]{1,0:T(8,128)(2,1)S(1)}, u32[]{:S(2)}, u32[]{:S(2)}) collective-permute-start(bf16[64,2560]{1,0:T(8,128)(2,1)S(1)} %copy-done.7), channel_id=1, source_target_pairs={{16,0},{17,1},{18,2},{19,3},{20,4},{21,5},{22,6},{23,7},{24,8},{25... | collective-permute-start | bytes 983048 | tf_op jit(solution)/shard_map/ppermute | solution.py:354
  168.2 16.0 %copy-start.2 = (bf16[2,64,2560]{2,1,0:T(8,128)(2,1)S(1)}, bf16[2,64,2560]{2,1,0:T(8,128)(2,1)}, u32[]{:S(2)}) copy-start(bf16[2,64,2560]{2,1,0:T(8,128)(2,1)} %copy-done.1) | copy-start | bytes 1966084
  184.2 2.2 copy-start.4
  185.4 1.3 copy-start.11
  187.5 8.2 %copy-start.9 = (bf16[64,2560]{1,0:T(8,128)(2,1)S(1)}, bf16[64,2560]{1,0:T(8,128)(2,1)}, u32[]{:S(2)}) copy-start(bf16[64,2560]{1,0:T(8,128)(2,1)} %get-tuple-element.20) | copy-start | bytes 983044
  188.7 7.1 %copy-start.8 = (bf16[64,2560]{1,0:T(8,128)(2,1)S(1)}, bf16[64,2560]{1,0:T(8,128)(2,1)}, u32[]{:S(2)}) copy-start(bf16[64,2560]{1,0:T(8,128)(2,1)} %get-tuple-element.21) | copy-start | bytes 983044
  188.7 7.1 %copy-start.10 = (bf16[64,2560]{1,0:T(8,128)(2,1)S(1)}, bf16[64,2560]{1,0:T(8,128)(2,1)}, u32[]{:S(2)}) copy-start(bf16[64,2560]{1,0:T(8,128)(2,1)} %get-tuple-element.24) | copy-start | bytes 983044
  188.7 23.6 %all-to-all-start.1 = ((f32[16,80,128]{2,1,0:T(8,128)}), f32[16,80,128]{2,1,0:T(8,128)S(1)}, u32[]{:S(2)}, u32[]{:S(2)}) async-start(f32[16,80,128]{2,1,0:T(8,128)} %copy.56), calls=%async_computation.1 | async-start | bytes 1310720 | tf_op jit(solution)/shard_map/all_to_all | solution.py:267
Sparse Core Ops, SparseCore 0:
  9.6 83.1 all-gather.2

commit v3 on v2

v3 whole, which is shorter than its diff:
```python
import functools

import jax
import jax.numpy as jnp
from jax import lax
from jax.experimental import pallas as pl
from jax.experimental.pallas import tpu as pltpu
from jax.sharding import PartitionSpec as P

HEADS = 20
KV_HEADS = 4
HEAD_DIM = 128
GROUP = HEADS // KV_HEADS
CHUNK = 16

norm_eps = 1e-06
rope_base = 1000000.0
SCALE = 1.0 / HEAD_DIM**0.5

NT = (((1,), (1,)), ((), ()))
TN = (((0,), (0,)), ((), ()))


def dot(a, b, dims=(((1,), (0,)), ((), ()))):
    return lax.dot_general(a, b, dims, preferred_element_type=jnp.float32)


def rope_tables(positions):
    half = HEAD_DIM // 2
    expon = jnp.arange(half, dtype=jnp.float32) * (2.0 / HEAD_DIM)
    inverse = rope_base ** (-expon)
    angles = positions.astype(jnp.float32)[:, None] * inverse[None, :]
    cosine, sine = jnp.cos(angles), jnp.sin(angles)
    return (
        jnp.concatenate([cosine, cosine], axis=1),
        jnp.concatenate([-sine, sine], axis=1),
    )


def ring_order(count):
    if count % 4:
        return list(range(count))
    chips = count // 2
    columns = 2 ** ((chips.bit_length() - 1) // 2)
    lines = chips // columns
    walk = [(z, 0) for z in range(lines)]
    for step, z in enumerate(range(lines - 1, -1, -1)):
        side = range(1, columns) if step % 2 == 0 else range(columns - 1, 0, -1)
        walk += [(z, x) for x in side]
    return [(z * columns + x) * 2 + core for z, x in walk for core in range(2)]


def reordered(value, order):
    share = value.shape[-1] // len(order)
    return jnp.concatenate(
        [value[..., i * share : (i + 1) * share] for i in order], axis=-1
    )


def in_hbm(value):
    return pltpu.with_memory_space_constraint(value, pltpu.HBM)


def stacked(value):
    return jnp.concatenate(
        [value[:, j * HEAD_DIM : (j + 1) * HEAD_DIM] for j in range(GROUP)], axis=0
    )


def step_kernel(order, step, chosen, *refs):
    refs = list(refs)
    first = step == 0
    own = refs.pop(0)
    incoming = refs.pop(0) if step >= 2 else None
    normed, lowrank = (refs.pop(0), refs.pop(0)) if first else (None, None)
    rotated = None if first else refs.pop(0)
    keys, values, bias, cosine, sine, weight, factor_bt, factor_a = refs[:8]
    rows_in, reciprocal, gain = refs[8:11]
    if first:
        held, rotated, input_gradient, dquery, middle, grads = refs[11:17]
        sems = refs[-1]
        upstream, dq, total, middle_sum = refs[-5:-1]
    else:
        held = weight
        input_gradient, dquery, middle, grads = refs[-9:-5]
        upstream, dq, total, middle_sum = refs[-4:]
    h = pl.program_id(0)
    groups = pl.num_programs(0) - 1
    micro = chosen[step]
    tokens = bias.shape[1]
    width = gain.shape[1]
    block = GROUP * HEAD_DIM
    columns = lambda g: pl.ds(pl.multiple_of(g * block, HEAD_DIM), block)
    fetch = lambda g: pltpu.make_async_copy(
        weight.at[:, columns(g)], held.at[g], sems.at[g]
    )

    @pl.when(h == 0)
    def _():
        if first:
            fetch(0).start()
            fetch(1).start()
        total[...] = jnp.zeros_like(total)
        middle_sum[...] = jnp.zeros_like(middle_sum)
        if incoming is None:
            upstream[...] = own[0]
        else:
            is_last = chosen[chosen.shape[0] - 1] == 1
            upstream[...] = jnp.where(is_last, own[0], incoming[...])

    def project():
        query = dot(normed[...], held[h]) + dot(lowrank[...], factor_bt[columns(h), :], NT)
        for m in range(rotated.shape[0] // tokens):
            rows = slice(m * tokens, (m + 1) * tokens)
            for j in range(GROUP):
                part = query[rows, j * HEAD_DIM : (j + 1) * HEAD_DIM]
                turned = part * cosine[m] + pltpu.roll(part, HEAD_DIM // 2, 1) * sine[m]
                rotated[rows, j * HEAD_DIM : (j + 1) * HEAD_DIM] = turned.astype(jnp.bfloat16)

    def pull_back(piece, before):
        at = slice(piece * (width // GROUP), (piece + 1) * (width // GROUP))
        total[:, at] += dot(before, held[h - 1, at, :], NT)

    def attend(before=None):
        if first:
            mine = rotated[pl.ds(pl.multiple_of(micro * tokens, tokens), tokens), :]
        else:
            mine = rotated[...]
        scores = dot(stacked(mine), keys[...], NT)
        dprobs = dot(stacked(upstream[:, columns(h)]), values[...], NT)
        dscores = []
        for j in range(GROUP):
            for row in range(0, tokens, CHUNK):
                at = slice(j * tokens + row, j * tokens + row + CHUNK)
                masked = scores[at] * SCALE + bias[0, row : row + CHUNK]
                expo = jnp.exp(masked - jnp.max(masked, axis=-1, keepdims=True))
                probs = expo * (1.0 / jnp.sum(expo, axis=-1, keepdims=True))
                rounded = probs.astype(jnp.bfloat16).astype(jnp.float32)
                delta = jnp.sum(rounded * dprobs[at], axis=-1, keepdims=True)
                dscores.append((probs * (dprobs[at] - delta) * SCALE).astype(jnp.bfloat16))
            if before is not None:
                pull_back(j, before)
        drot = dot(jnp.concatenate(dscores, axis=0), keys[...])
        for j in range(GROUP):
            part = drot[j * tokens : (j + 1) * tokens]
            turned = part * cosine[micro] - pltpu.roll(part, HEAD_DIM // 2, 1) * sine[micro]
            at = slice(j * HEAD_DIM, (j + 1) * HEAD_DIM)
            dq[:, at] = turned.astype(jnp.bfloat16)
            dquery[0, :, at] = turned.astype(jnp.bfloat16)
        middle_sum[...] += dot(dq[...], factor_bt[columns(h), :])

    @pl.when(h == 0)
    def _():
        if first:
            fetch(h).wait()
            project()
        attend()

    if first:

        @pl.when((h > 0) & (h + 1 < groups))
        def _():
            fetch(h + 1).start()

    @pl.when((h > 0) & (h < groups))
    def _():
        if first:
            fetch(h).wait()
            project()
        attend(dq[...])

    @pl.when(h == groups)
    def _():
        for piece in range(GROUP):
            pull_back(piece, dq[...])
        mid = middle_sum[...].astype(jnp.bfloat16)
        middle[0] = mid
        dh = (total[...] + dot(mid, factor_a[...], NT)) * gain[...]
        scaled = rows_in[0].astype(jnp.float32) * reciprocal[0]
        mean = jnp.mean(dh * scaled, axis=1, keepdims=True)
        change = reciprocal[0] * (dh - scaled * mean)
        share = change.shape[1] // len(order)
        for k, i in enumerate(order):
            here = slice(i * share, (i + 1) * share)
            result = upstream[:, here].astype(jnp.float32) + change[:, k * share : (k + 1) * share]
            input_gradient[:, here] = result.astype(jnp.bfloat16)
        grads[0] = input_gradient[...]


def backward(
    order,
    step,
    chosen,
    own,
    incoming,
    normed,
    lowrank,
    rotated,
    keys,
    values,
    bias,
    cosine,
    sine,
    weight,
    factor_bt,
    factor_a,
    rows_in,
    reciprocal,
    gain,
    kept,
):
    first = step == 0
    micros, tokens, features = own.shape
    width, rank = factor_a.shape
    ctx = keys.shape[0]
    rows = micros * tokens
    block = features // KV_HEADS
    group = lambda h: jnp.minimum(h, KV_HEADS - 1)
    whole = lambda *dims: pl.BlockSpec(dims, lambda h, m: (0,) * len(dims))
    of_micro = lambda *dims: pl.BlockSpec(
        (1, *dims), lambda h, m: (m[step],) + (0,) * len(dims)
    )
    untouched = pl.BlockSpec(memory_space=pl.ANY)
    of_group = lambda dim: pl.BlockSpec((dim, HEAD_DIM), lambda h, m: (0, group(h)))
    ins = [(own, of_micro(tokens, features))]
    if first:
        ins += [(normed, whole(rows, width)), (lowrank, whole(rows, rank))]
    else:
        if incoming is not None:
            ins.append((incoming, whole(tokens, features)))
        ins += [
            (rotated, pl.BlockSpec((tokens, block), lambda h, m: (m[step], group(h)))),
        ]
    ins += [
        (keys, of_group(ctx)),
        (values, of_group(ctx)),
        (bias, of_micro(tokens, ctx)),
        (cosine, whole(micros, tokens, HEAD_DIM)),
        (sine, whole(micros, tokens, HEAD_DIM)),
        (weight, untouched if first else pl.BlockSpec(memory_space=pltpu.VMEM)),
        (factor_bt, whole(features, rank)),
        (factor_a, whole(width, rank)),
        (rows_in, of_micro(tokens, width)),
        (reciprocal, of_micro(tokens, 1)),
        (gain, whole(1, width)),
    ]
    ins += [(a, untouched) for a in kept]
    outs = [
        (pltpu.HBM((tokens, width), jnp.bfloat16), whole(tokens, width)),
        (
            pltpu.HBM((micros, tokens, features), jnp.bfloat16),
            pl.BlockSpec((1, tokens, block), lambda h, m: (m[step], 0, group(h))),
        ),
        (pltpu.HBM((micros, tokens, rank), jnp.bfloat16), of_micro(tokens, rank)),
        (pltpu.HBM((micros, tokens, width), jnp.bfloat16), of_micro(tokens, width)),
    ]
    scratch = [
        pltpu.VMEM((tokens, features), jnp.bfloat16),
        pltpu.VMEM((tokens, block), jnp.bfloat16),
        pltpu.VMEM((tokens, width), jnp.float32),
        pltpu.VMEM((tokens, rank), jnp.float32),
    ]
    if first:
        outs[:0] = [
            (
                pltpu.VMEM((KV_HEADS, width, block), jnp.bfloat16),
                pl.BlockSpec(memory_space=pltpu.VMEM),
            ),
            (
                pltpu.HBM((rows, features), jnp.bfloat16),
                pl.BlockSpec((rows, block), lambda h, m: (0, group(h))),
            ),
        ]
        scratch.append(pltpu.SemaphoreType.DMA((KV_HEADS,)))
        aliases = {}
    else:
        outs.append(
            (
                pltpu.VMEM((KV_HEADS, width, block), jnp.bfloat16),
                pl.BlockSpec(memory_space=pltpu.VMEM),
            )
        )
        at = [a is weight for a, _ in ins].index(True)
        aliases = {1 + at: 4, len(ins) - 2: 1, len(ins) - 1: 2, len(ins): 3}
    return pl.pallas_call(
        functools.partial(step_kernel, order, step),
        grid_spec=pltpu.PrefetchScalarGridSpec(
            num_scalar_prefetch=1,
            grid=(KV_HEADS + 1,),
            in_specs=[spec for _, spec in ins],
            out_specs=[spec for _, spec in outs],
            scratch_shapes=scratch,
        ),
        out_shape=[shape for shape, _ in outs],
        input_output_aliases=aliases,
        compiler_params=pltpu.CompilerParams(vmem_limit_bytes=24 * 2**20),
        cost_estimate=pl.CostEstimate(
            flops=2 * tokens * features * (width + 3 * ctx),
            bytes_accessed=2 * width * features,
            transcendentals=tokens * HEADS * ctx,
        ),
        name="first_step" if first else "step",
    )(chosen, *(a if a is incoming or (a is weight and not first) else in_hbm(a) for a, _ in ins))


def gradients_kernel(order, normed, middle, dquery, lowrank, out):
    of_a = dot(middle[...], normed[...], TN)
    of_bt = dot(lowrank[...], dquery[...], TN)
    rank = of_a.shape[0]
    share = out.shape[2]
    for k, i in enumerate(order):
        out[i, :rank] = of_a[:, k * share : (k + 1) * share].astype(out.dtype)
        out[k, rank:] = of_bt[:, k * share : (k + 1) * share].astype(out.dtype)


def gradients(order, normed, middle, dquery, lowrank):
    rows, width = normed.shape
    rank = middle.shape[1]
    count = len(order)
    return pl.pallas_call(
        functools.partial(gradients_kernel, order),
        out_shape=jax.ShapeDtypeStruct((count, 2 * rank, width // count), jnp.float32),
        name="gradients",
    )(normed, middle, dquery, lowrank)


def gather_small(adapter_a, adapter_bt, norm_gain):
    count = lax.axis_size("dp")
    packed = jnp.concatenate([adapter_a, adapter_bt, norm_gain[:, None]], axis=1)
    sent = jnp.broadcast_to(packed[None], (count, *packed.shape))
    return lax.all_to_all(sent, "dp", split_axis=0, concat_axis=0, tiled=True)


def per_device(
    layer_inputs,
    top_grad,
    keys,
    values,
    query_weight,
    adapter_a,
    adapter_bt,
    norm_gain,
    offsets,
    segments,
):
    order = ring_order(lax.axis_size("dp"))
    _, _, micros, tokens, width = layer_inputs.shape
    rows = micros * tokens
    ctx = keys.shape[2]
    keys, values = keys[0, 0], values[0, 0]
    features = query_weight.shape[2]
    rank = adapter_a.shape[2]

    weight = lax.all_gather(
        query_weight[0], "dp", axis=0, tiled=True, axis_index_groups=[order]
    )
    small = gather_small(adapter_a[0], adapter_bt[0], norm_gain[0])
    factor_bt = small[:, :, rank : 2 * rank].reshape(features, rank)
    walked = jnp.concatenate([small[i : i + 1] for i in order], axis=0)
    factor_a = walked[:, :, :rank].reshape(width, rank)
    gain = walked[:, :, 2 * rank].reshape(1, width).astype(jnp.float32)

    rows_in = reordered(layer_inputs[0, 0], order)
    flat = rows_in.reshape(rows, width).astype(jnp.float32)
    reciprocal = lax.rsqrt(jnp.mean(flat * flat, axis=1, keepdims=True) + norm_eps)
    normed = (flat * reciprocal * gain).astype(jnp.bfloat16)
    lowrank = dot(normed, factor_a).astype(jnp.bfloat16)

    positions = (
        offsets[0][:, None] + jnp.arange(tokens, dtype=jnp.int32)[None, :]
    ).reshape(rows)
    seg_row = segments[0]
    place = jnp.arange(ctx, dtype=jnp.int32)
    query_seg = jnp.take(seg_row, positions)
    visible = (place[None, :] <= positions[:, None]) & (
        (seg_row[None, :] == 0) | (seg_row[None, :] == query_seg[:, None])
    )
    bias = jnp.where(visible, 0.0, -1e30).astype(jnp.float32)
    cosine, sine = rope_tables(positions)

    by_micro = lambda a: a.reshape(micros, tokens, a.shape[-1])
    section_count = lax.axis_size("pipe")
    section = lax.axis_index("pipe")
    last = section_count - 1
    steps = 2 * last + micros
    kept, arrived, rotated = (), [], None
    micro = jnp.clip(jnp.arange(steps) - 2 * (last - section), 0, micros - 1)
    chosen = jnp.append(micro, section == last).astype(jnp.int32)
    bias, cosine, sine, reciprocal = map(by_micro, (bias, cosine, sine, reciprocal))
    for step in range(steps):
        made = list(
            backward(
                order,
                step,
                chosen,
                top_grad[0],
                arrived[step - 2] if step >= 2 else None,
                normed,
                lowrank,
                rotated,
                keys,
                values,
                bias,
                cosine,
                sine,
                weight,
                factor_bt,
                factor_a,
                rows_in,
                reciprocal,
                gain,
                kept,
            )
        )
        if rotated is None:
            weight, rotated = made.pop(0), made.pop(0)
        else:
            weight = made.pop()
        result, *kept = made
        if step < steps - 2:
            arrived.append(
                lax.ppermute(result, "pipe", [(s, s - 1) for s in range(1, section_count)])
            )

    grads = kept[2]
    dquery = kept[0].reshape(rows, features)
    middle = kept[1].reshape(rows, -1)
    partial = gradients(order, normed, middle, dquery, lowrank)
    got = lax.all_to_all(partial, "dp", split_axis=0, concat_axis=0, tiled=True)
    total = jnp.sum(got.astype(jnp.float32), axis=0)
    return (grads[None, None], total[:rank].T[None], total[rank:].T[None])


def solution(mesh):
    placed = (
        P("pipe", "dp", None, None, None),
        P("dp", None, None, None),
        P("pipe", "dp", None, None),
        P("pipe", "dp", None, None),
        P("pipe", "dp", None),
        P("pipe", "dp", None),
        P("pipe", "dp", None),
        P("pipe", "dp"),
        P("dp", None),
        P("dp", None),
    )
    return jax.shard_map(
        per_device,
        mesh=mesh,
        in_specs=placed,
        out_specs=(
            P("pipe", "dp", None, None, None),
            P("pipe", "dp", None),
            P("pipe", "dp", None),
        ),
        check_vma=False,
    )
```

time: 221 us -> 198 us (0.90)
  blocking collectives: 0 us -> 31.7 us
  waiting for transfers between devices: 96.1 us -> 66.3 us
  Pallas kernels: 71.4 us -> 61.4 us
  starting transfers between devices: 17.2 us -> 10.1 us
  local copies, waits for them, and re-layouts: 11.1 us -> 6.84 us
  other arithmetic: 7.79 us -> 4.6 us
    all_to_all x0 -> x1, blocking collectives: none -> 31.7 us  [per_device(): got = lax.all_to_all(partial, 'dp', split_axis=0, concat_axis=0, tiled=True)]
    ppermute x2, waiting for transfers between devices: 16.2 us -> 0.01 us  [per_device(): lax.ppermute(result, 'pipe', [(s, s - 1) for s in range(1, section_count)])]
    all_to_all x1 -> x0, waiting for transfers between devices: 15.6 us -> none  [summed_shares(): got = lax.all_to_all(packed, 'dp', split_axis=0, concat_axis=0, tiled=True)]
    pallas_call x5, Pallas kernels: 71.4 us -> 61.4 us  [the longest x4 58.6 us: backward(): pl.pallas_call(functools.partial(step_kernel, order, step), grid_spec=plt...]
    all_to_all x1 -> x0, starting transfers between devices: 7.03 us -> none  [summed_shares(): got = lax.all_to_all(packed, 'dp', split_axis=0, concat_axis=0, tiled=True)]
    unnamed x49 -> x16, local copies, waits for them, and re-layouts: 2.35 us -> 0.07 us
  transfers between devices with their start and end apart: 5 -> 4, of which waited for: 5 -> 2; matrix products, arithmetic and copies ran while one was open for 7% -> 6% of each run, Pallas kernels for 0% -> 14%
where the time goes in v3:
time: 198 us; the launch traced here: 196 us
  waiting for transfers between devices  66.3 us (33%)
  Pallas kernels  61.4 us (31%)
  blocking collectives  31.7 us (16%)
  between operations  14.3 us (7%)
  starting transfers between devices  10.1 us (5%)
  local copies, waits for them, and re-layouts  6.84 us (3%)
  other arithmetic  4.6 us (2%)
    pallas_call x4, Pallas kernels, backward(): pl.pallas_call(functools.partial(step_kernel, order, step), grid_spec=plt...  58.6 us
    all_gather x1, waiting for transfers between devices, per_device(): lax.all_gather(query_weight[0], 'dp', axis=0, tiled=True, axis_index_grou...  46.9 us
    all_to_all x1, blocking collectives, per_device(): got = lax.all_to_all(partial, 'dp', split_axis=0, concat_axis=0, tiled=True)  31.7 us
    all_to_all x1, waiting for transfers between devices, gather_small(): return lax.all_to_all(sent, 'dp', split_axis=0, concat_axis=0, tiled=True)  18.7 us
    all_to_all x1, starting transfers between devices, gather_small(): return lax.all_to_all(sent, 'dp', split_axis=0, concat_axis=0, tiled=True)  7.36 us
  transfers between devices with their start and end apart: 4, of which 2 were waited for; matrix products, arithmetic and copies ran while one was open for 6% of the time, Pallas kernels for 14%

profile of v3, /device:TPU:0, one launch (start us, length us, event | category | flops | bytes accessed | tf_op | source)
XLA Modules:
  0.0 196.3 jit_solution(2750294446196548167)
XLA Ops:
  7.2 0.7 all-gather.3.cloned.1.call-update
  7.9 0.8 pad_maximum_fusion.2
  8.8 0.9 broadcast_in_dim.35
  9.6 7.4 %all-to-all-start = ((bf16[16,160,65]{1,2,0:T(8,128)(2,1)}), bf16[16,160,65]{1,2,0:T(8,128)(2,1)S(1)}, u32[]{:S(2)}, u32[]{:S(2)}) async-start(bf16[16,160,65]{1,2,0:T(8,128)(2,1)} %broadcast_in_dim.35), calls=%async_computation | async-start | bytes 1179648 | tf_op jit(solution)/shard_map/all_to_all | solution.py:331
  17.2 1.0 gather_fusion
  18.4 0.5 concatenate.40.refs_11_.refs_10_
  19.4 0.7 copy.42.refs_12_.refs_11_
  21.0 0.8 pad_maximum_fusion
  21.7 1.0 fusion.5.refs_5_.refs_4_
  22.7 18.7 %all-to-all-done = bf16[16,160,65]{1,2,0:T(8,128)(2,1)S(1)} async-done(((bf16[16,160,65]{1,2,0:T(8,128)(2,1)}), bf16[16,160,65]{1,2,0:T(8,128)(2,1)S(1)}, u32[]{:S(2)}, u32[]{:S(2)}) %all-to-all-start) | async-done | bytes 332832 | tf_op jit(solution)/shard_map/all_to_all | solution.py:331
  41.6 0.7 reshape.246.refs_13_.refs_12_
  42.4 1.1 copy.41
  43.8 1.0 convolution_convert_fusion.refs_2_.lowrank
  44.8 1.1 fusion.1.refs_1_.normed
  45.9 46.9 %all-gather.3.cloned.1.call-done = bf16[1,2560,2560]{2,1,0:T(8,128)(2,1)} async-done(((bf16[1,160,2560]{2,1,0:T(8,128)(2,1)}), bf16[1,2560,2560]{2,1,0:T(8,128)(2,1)}) %all-gather.3.cloned.1.call-update) | async-done | bytes 13107216 | tf_op jit(solution)/shard_map/all_gather | solution.py:354
  92.8 18.6 %first_step.1 = (bf16[4,2560,640]{2,1,0:T(8,128)(2,1)S(1)}, bf16[128,2560]{1,0:T(8,128)(2,1)}, bf16[64,2560]{1,0:T(8,128)(2,1)}, bf16[2,64,2560]{2,1,0:T(8,128)(...) custom-call(s32[5]{0:T(128)S(1)} %pad_add_fusion.chosen, bf16[2,64,2560]{2,1,0:T(8,128)(2,1)} %bitcast.62, ...), custom_call_target="tpu_custom_call" | custom-call | flops 1845493760 | bytes 13107200 | tf_op jit(solution)/shard_map/first_step/pallas_call | solution.py:285
  111.5 1.5 collective-permute-start.1
  113.0 13.3 %step.3 = (bf16[64,2560]{1,0:T(8,128)(2,1)}, bf16[2,64,2560]{2,1,0:T(8,128)(2,1)}, bf16[2,64,32]{2,1,0:T(8,128)(2,1)}, bf16[2,64,2560]{2,1,0:T(8,128)(2,1)}, bf16[4,2560,640]{2,1,0:T(8,128)(2,1)S(1)}) custom-call(s32[5]{0:T(128)S(1)} %pad_add_fusion.chosen, ...), custom_call_target="tpu_custom_call", output_to_operand_aliasing={{4}: (8, {}), {1}: (14, {}), {2}: (15, {}), {3}: (16, {})} | custom-call | flops 1845493760 | bytes 13107200 | tf_op jit(solution)/shard_map/step/pallas_call | solution.py:285
  126.3 1.3 collective-permute-start
  127.6 13.3 %step.4 = (bf16[64,2560]{1,0:T(8,128)(2,1)}, bf16[2,64,2560]{2,1,0:T(8,128)(2,1)}, bf16[2,64,32]{2,1,0:T(8,128)(2,1)}, bf16[2,64,2560]{2,1,0:T(8,128)(2,1)}, bf16[4,2560,640]{2,1,0:T(8,128)(2,1)S(1)}) custom-call(s32[5]{0:T(128)S(1)} %pad_add_fusion.chosen, ...), custom_call_target="tpu_custom_call", output_to_operand_aliasing={{4}: (9, {}), {1}: (15, {}), {2}: (16, {}), {3}: (17, {})} | custom-call | flops 1845493760 | bytes 13107200 | tf_op jit(solution)/shard_map/step/pallas_call | solution.py:285
  140.9 13.3 %step.5 = (bf16[64,2560]{1,0:T(8,128)(2,1)}, bf16[2,64,2560]{2,1,0:T(8,128)(2,1)}, bf16[2,64,32]{2,1,0:T(8,128)(2,1)}, bf16[2,64,2560]{2,1,0:T(8,128)(2,1)}, bf16[4,2560,640]{2,1,0:T(8,128)(2,1)S(1)}) custom-call(s32[5]{0:T(128)S(1)} %pad_add_fusion.chosen, ...), custom_call_target="tpu_custom_call", output_to_operand_aliasing={{4}: (9, {}), {1}: (15, {}), {2}: (16, {}), {3}: (17, {})} | custom-call | flops 1845493760 | bytes 13107200 | tf_op jit(solution)/shard_map/step/pallas_call | solution.py:285
  154.3 2.7 %gradients.1 = f32[16,64,160]{2,1,0:T(8,128)} custom-call(bf16[128,2560]{1,0:T(8,128)(2,1)} %fusion.1.refs_1_.normed, bf16[128,32]{1,0:T(8,128)(2,1)} %bitcast.77, bf16[128,2560]{1,0:T(8,128)(2,1)} %bitcast.66, bf16[128,32]{1,0:T(8,128)(2,1)} %convolution_convert_fusion.refs_2_.lowrank), custom_call_target="tpu_custom_call" | custom-call | tf_op jit(solution)/shard_map/gradients/pallas_call | solution.py:320
  157.0 31.7 %all_to_all.10 = f32[16,64,160]{2,1,0:T(8,128)S(1)} all-to-all(f32[16,64,160]{2,1,0:T(8,128)} %gradients.1), channel_id=1, replica_groups=mesh['pipe'=2,'dp'=16] {'dp'}, dimensions={0} | all-to-all | bytes 1310720 | tf_op jit(solution)/shard_map/all_to_all | solution.py:429
  188.8 0.6 slice_bitcast_fusion
  (43 shorter events, 2.4 us)
Async XLA Ops:
  7.2 9.8 %copy-start.4 = (s32[1,2]{1,0:T(1,128)S(1)}, s32[1,2]{1,0:T(1,128)}, u32[]{:S(2)}) copy-start(s32[1,2]{1,0:T(1,128)} %param.18) | copy-start | bytes 28
  7.2 10.0 %copy-start = (s32[1,1024]{1,0:T(1,128)S(1)}, s32[1,1024]{1,0:T(1,128)}, u32[]{:S(2)}) copy-start(s32[1,1024]{1,0:T(1,128)} %param.19) | copy-start | bytes 12292
  7.2 85.7 %all-gather.3.cloned.1.call-start = ((), (), s32[]{:S(2)}) async-start(), calls=%async_computation.2 | async-start | bytes 13926400 | tf_op jit(solution)/shard_map/all_gather | solution.py:354
  7.9 10.3 %copy-start.3 = (bf16[1,1,2,64,2560]{4,3,2,1,0:T(8,128)(2,1)S(1)}, bf16[1,1,2,64,2560]{4,3,2,1,0:T(8,128)(2,1)}, u32[]{:S(2)}) copy-start(bf16[1,1,2,64,2560]{4,3,2,1,0:T(8,128)(2,1)} %param.10) | copy-start | bytes 1966084
  9.6 31.8 %all-to-all-start = ((bf16[16,160,65]{1,2,0:T(8,128)(2,1)}), bf16[16,160,65]{1,2,0:T(8,128)(2,1)S(1)}, u32[]{:S(2)}, u32[]{:S(2)}) async-start(bf16[16,160,65]{1,2,0:T(8,128)(2,1)} %broadcast_in_dim.35), calls=%async_computation | async-start | bytes 1179648 | tf_op jit(solution)/shard_map/all_to_all | solution.py:331
  18.9 25.9 %copy-start.1 = (bf16[2,64,2560]{2,1,0:T(8,128)(2,1)}, bf16[2,64,2560]{2,1,0:T(8,128)(2,1)S(1)}, u32[]{:S(2)}) copy-start(bf16[2,64,2560]{2,1,0:T(8,128)(2,1)S(1)} %concatenate.40.refs_11_.refs_10_) | copy-start | bytes 1966084
  43.8 2.1 %copy-start.2 = (bf16[16,160,32]{2,1,0:T(8,128)(2,1)}, bf16[16,160,32]{2,1,0:T(8,128)(2,1)S(1)}, u32[]{:S(2)}) copy-start(bf16[16,160,32]{2,1,0:T(8,128)(2,1)S(1)} %copy.39) | copy-start | bytes 491524
  111.5 16.1 %collective-permute-start.1 = (bf16[64,2560]{1,0:T(8,128)(2,1)}, bf16[64,2560]{1,0:T(8,128)(2,1)S(1)}, u32[]{:S(2)}, u32[]{:S(2)}) collective-permute-start(bf16[64,2560]{1,0:T(8,128)(2,1)} %get-tuple-element.27), channel_id=1, source_target_pairs={{16,0},{17,1},{18,2},{19,3},{20,4},{21,5},{22,6},{23,7},{24,8},{25... | collective-permute-start | bytes 983048 | tf_op jit(solution)/shard_map/ppermute | solution.py:422
  126.3 14.6 %collective-permute-start = (bf16[64,2560]{1,0:T(8,128)(2,1)}, bf16[64,2560]{1,0:T(8,128)(2,1)S(1)}, u32[]{:S(2)}, u32[]{:S(2)}) collective-permute-start(bf16[64,2560]{1,0:T(8,128)(2,1)} %get-tuple-element.26), channel_id=1, source_target_pairs={{16,0},{17,1},{18,2},{19,3},{20,4},{21,5},{22,6},{23,7},{24,8},{25... | collective-permute-start | bytes 983048 | tf_op jit(solution)/shard_map/ppermute | solution.py:422
Sparse Core Ops, SparseCore 0:
  9.6 83.1 all-gather.2

commit v4 on v3

--- a/solution.py
+++ b/solution.py
@@ -307,21 +307,52 @@
     of_a = dot(middle[...], normed[...], TN)
     of_bt = dot(lowrank[...], dquery[...], TN)
     rank = of_a.shape[0]
-    share = out.shape[2]
+    share = of_a.shape[1] // len(order)
+    lanes = out.shape[2]
     for k, i in enumerate(order):
-        out[i, :rank] = of_a[:, k * share : (k + 1) * share].astype(out.dtype)
-        out[k, rank:] = of_bt[:, k * share : (k + 1) * share].astype(out.dtype)
+        for to, top, value in ((i, 0, of_a), (k, rank, of_bt)):
+            mine = value[:, k * share : (k + 1) * share].astype(out.dtype)
+            if share <= lanes:
+                out[to, top : top + rank, :] = mine
+                continue
+            out[to, top : top + rank, :] = mine[:, :lanes]
+            over = share - lanes
+            side = lanes // over
+            deep = rank // side
+            folded = [mine[n * deep : (n + 1) * deep, lanes:] for n in range(side)]
+            low = 2 * rank + top // side
+            out[to, low : low + deep, :] = jnp.concatenate(folded, axis=1)
 
 
 def gradients(order, normed, middle, dquery, lowrank):
     rows, width = normed.shape
     rank = middle.shape[1]
     count = len(order)
+    share = width // count
+    lanes = min(share, HEAD_DIM)
+    deep = 2 * rank * share // lanes
     return pl.pallas_call(
         functools.partial(gradients_kernel, order),
-        out_shape=jax.ShapeDtypeStruct((count, 2 * rank, width // count), jnp.float32),
+        out_shape=jax.ShapeDtypeStruct((count, deep, lanes), jnp.bfloat16),
         name="gradients",
     )(normed, middle, dquery, lowrank)
+
+
+def unfolded(total, rank, share):
+    lanes = total.shape[1]
+    if share == lanes:
+        return total
+    over = share - lanes
+    side = lanes // over
+    deep = rank // side
+    parts = []
+    for top in (0, rank):
+        low = 2 * rank + top // side
+        folded = total[low : low + deep]
+        parts.append(
+            jnp.concatenate([folded[:, n * over : (n + 1) * over] for n in range(side)], axis=0)
+        )
+    return jnp.concatenate([total[: 2 * rank], jnp.concatenate(parts, axis=0)], axis=1)
 
 
 def gather_small(adapter_a, adapter_bt, norm_gain):
@@ -427,7 +458,7 @@
     middle = kept[1].reshape(rows, -1)
     partial = gradients(order, normed, middle, dquery, lowrank)
     got = lax.all_to_all(partial, "dp", split_axis=0, concat_axis=0, tiled=True)
-    total = jnp.sum(got.astype(jnp.float32), axis=0)
+    total = unfolded(jnp.sum(got.astype(jnp.float32), axis=0), rank, width // len(order))
     return (grads[None, None], total[:rank].T[None], total[rank:].T[None])
 
 

time: 198 us -> 183 us (0.924)
  blocking collectives: 31.7 us -> 18 us
    all_to_all x1, blocking collectives: 31.7 us -> 18 us  [per_device(): got = lax.all_to_all(partial, 'dp', split_axis=0, concat_axis=0, tiled=True)]
  transfers between devices with their start and end apart: 4 -> 4, of which waited for: 2 -> 2; matrix products, arithmetic and copies ran while one was open for 6% -> 6% of each run, Pallas kernels for 14% -> 15%
where the time goes in v4:
time: 183 us
  waiting for transfers between devices  66.3 us (36%)
  Pallas kernels  61.1 us (33%)
  blocking collectives  18 us (10%)
  between operations  14.3 us (8%)
  starting transfers between devices  10.1 us (6%)
  local copies, waits for them, and re-layouts  6.64 us (4%)
  other arithmetic  5.21 us (3%)
    pallas_call x4, Pallas kernels, backward(): pl.pallas_call(functools.partial(step_kernel, order, step), grid_spec=plt...  58.6 us
    all_gather x1, waiting for transfers between devices, per_device(): lax.all_gather(query_weight[0], 'dp', axis=0, tiled=True, axis_index_grou...  47 us
    all_to_all x1, waiting for transfers between devices, gather_small(): return lax.all_to_all(sent, 'dp', split_axis=0, concat_axis=0, tiled=True)  18.7 us
    all_to_all x1, blocking collectives, per_device(): got = lax.all_to_all(partial, 'dp', split_axis=0, concat_axis=0, tiled=True)  18 us
    all_to_all x1, starting transfers between devices, gather_small(): return lax.all_to_all(sent, 'dp', split_axis=0, concat_axis=0, tiled=True)  7.36 us
  transfers between devices with their start and end apart: 4, of which 2 were waited for; matrix products, arithmetic and copies ran while one was open for 6% of the time, Pallas kernels for 15%

profile of v4, /device:TPU:0, one launch (start us, length us, event | category | flops | bytes accessed | tf_op | source)
XLA Modules:
  0.0 182.8 jit_solution(18095285007618663746)
XLA Ops:
  7.2 0.7 all-gather.3.cloned.1.call-update
  7.9 0.8 pad_maximum_fusion.2
  8.8 0.9 broadcast_in_dim.35
  9.6 7.4 %all-to-all-start = ((bf16[16,160,65]{1,2,0:T(8,128)(2,1)}), bf16[16,160,65]{1,2,0:T(8,128)(2,1)S(1)}, u32[]{:S(2)}, u32[]{:S(2)}) async-start(bf16[16,160,65]{1,2,0:T(8,128)(2,1)} %broadcast_in_dim.35), calls=%async_computation | async-start | bytes 1179648 | tf_op jit(solution)/shard_map/all_to_all | solution.py:362
  17.2 1.0 gather_fusion
  18.4 0.5 concatenate.46.refs_11_.refs_10_
  19.4 0.7 copy.42.refs_12_.refs_11_
  21.0 0.8 pad_maximum_fusion
  21.7 1.0 fusion.5.refs_5_.refs_4_
  22.7 18.7 %all-to-all-done = bf16[16,160,65]{1,2,0:T(8,128)(2,1)S(1)} async-done(((bf16[16,160,65]{1,2,0:T(8,128)(2,1)}), bf16[16,160,65]{1,2,0:T(8,128)(2,1)S(1)}, u32[]{:S(2)}, u32[]{:S(2)}) %all-to-all-start) | async-done | bytes 332832 | tf_op jit(solution)/shard_map/all_to_all | solution.py:362
  41.6 0.7 reshape.246.refs_13_.refs_12_
  42.4 1.1 copy.41
  43.8 1.0 convolution_convert_fusion.refs_2_.lowrank
  44.8 1.1 fusion.1.refs_1_.normed
  45.9 47.0 %all-gather.3.cloned.1.call-done = bf16[1,2560,2560]{2,1,0:T(8,128)(2,1)} async-done(((bf16[1,160,2560]{2,1,0:T(8,128)(2,1)}), bf16[1,2560,2560]{2,1,0:T(8,128)(2,1)}) %all-gather.3.cloned.1.call-update) | async-done | bytes 13107216 | tf_op jit(solution)/shard_map/all_gather | solution.py:385
  92.8 18.6 %first_step.1 = (bf16[4,2560,640]{2,1,0:T(8,128)(2,1)S(1)}, bf16[128,2560]{1,0:T(8,128)(2,1)}, bf16[64,2560]{1,0:T(8,128)(2,1)}, bf16[2,64,2560]{2,1,0:T(8,128)(...) custom-call(s32[5]{0:T(128)S(1)} %pad_add_fusion.chosen, bf16[2,64,2560]{2,1,0:T(8,128)(2,1)} %bitcast.62, ...), custom_call_target="tpu_custom_call" | custom-call | flops 1845493760 | bytes 13107200 | tf_op jit(solution)/shard_map/first_step/pallas_call | solution.py:285
  111.5 1.5 collective-permute-start.1
  113.0 13.3 %step.3 = (bf16[64,2560]{1,0:T(8,128)(2,1)}, bf16[2,64,2560]{2,1,0:T(8,128)(2,1)}, bf16[2,64,32]{2,1,0:T(8,128)(2,1)}, bf16[2,64,2560]{2,1,0:T(8,128)(2,1)}, bf16[4,2560,640]{2,1,0:T(8,128)(2,1)S(1)}) custom-call(s32[5]{0:T(128)S(1)} %pad_add_fusion.chosen, ...), custom_call_target="tpu_custom_call", output_to_operand_aliasing={{4}: (8, {}), {1}: (14, {}), {2}: (15, {}), {3}: (16, {})} | custom-call | flops 1845493760 | bytes 13107200 | tf_op jit(solution)/shard_map/step/pallas_call | solution.py:285
  126.3 1.3 collective-permute-start
  127.6 13.3 %step.4 = (bf16[64,2560]{1,0:T(8,128)(2,1)}, bf16[2,64,2560]{2,1,0:T(8,128)(2,1)}, bf16[2,64,32]{2,1,0:T(8,128)(2,1)}, bf16[2,64,2560]{2,1,0:T(8,128)(2,1)}, bf16[4,2560,640]{2,1,0:T(8,128)(2,1)S(1)}) custom-call(s32[5]{0:T(128)S(1)} %pad_add_fusion.chosen, ...), custom_call_target="tpu_custom_call", output_to_operand_aliasing={{4}: (9, {}), {1}: (15, {}), {2}: (16, {}), {3}: (17, {})} | custom-call | flops 1845493760 | bytes 13107200 | tf_op jit(solution)/shard_map/step/pallas_call | solution.py:285
  140.9 13.3 %step.5 = (bf16[64,2560]{1,0:T(8,128)(2,1)}, bf16[2,64,2560]{2,1,0:T(8,128)(2,1)}, bf16[2,64,32]{2,1,0:T(8,128)(2,1)}, bf16[2,64,2560]{2,1,0:T(8,128)(2,1)}, bf16[4,2560,640]{2,1,0:T(8,128)(2,1)S(1)}) custom-call(s32[5]{0:T(128)S(1)} %pad_add_fusion.chosen, ...), custom_call_target="tpu_custom_call", output_to_operand_aliasing={{4}: (9, {}), {1}: (15, {}), {2}: (16, {}), {3}: (17, {})} | custom-call | flops 1845493760 | bytes 13107200 | tf_op jit(solution)/shard_map/step/pallas_call | solution.py:285
  154.3 2.5 %gradients.1 = bf16[16,80,128]{2,1,0:T(8,128)(2,1)} custom-call(bf16[128,2560]{1,0:T(8,128)(2,1)} %fusion.1.refs_1_.normed, bf16[128,32]{1,0:T(8,128)(2,1)} %bitcast.77, bf16[128,2560]{1,0:T(8,128)(2,1)} %bitcast.66, bf16[128,32]{1,0:T(8,128)(2,1)} %convolution_convert_fusion.refs_2_.lowrank), custom_call_target="tpu_custom_call" | custom-call | tf_op jit(solution)/shard_map/gradients/pallas_call | solution.py:334
  156.8 18.0 %all_to_all.10 = bf16[16,80,128]{2,1,0:T(8,128)(2,1)S(1)} all-to-all(bf16[16,80,128]{2,1,0:T(8,128)(2,1)} %gradients.1), channel_id=1, replica_groups=mesh['pipe'=2,'dp'=16] {'dp'}, dimensions={0} | all-to-all | bytes 655360 | tf_op jit(solution)/shard_map/all_to_all | solution.py:460
  175.3 0.6 fusion.8
  (52 shorter events, 2.8 us)
Async XLA Ops:
  7.2 9.8 %copy-start.4 = (s32[1,2]{1,0:T(1,128)S(1)}, s32[1,2]{1,0:T(1,128)}, u32[]{:S(2)}) copy-start(s32[1,2]{1,0:T(1,128)} %param.18) | copy-start | bytes 28
  7.2 10.0 %copy-start = (s32[1,1024]{1,0:T(1,128)S(1)}, s32[1,1024]{1,0:T(1,128)}, u32[]{:S(2)}) copy-start(s32[1,1024]{1,0:T(1,128)} %param.19) | copy-start | bytes 12292
  7.2 85.7 %all-gather.3.cloned.1.call-start = ((), (), s32[]{:S(2)}) async-start(), calls=%async_computation.2 | async-start | bytes 13926400 | tf_op jit(solution)/shard_map/all_gather | solution.py:385
  7.9 10.3 %copy-start.3 = (bf16[1,1,2,64,2560]{4,3,2,1,0:T(8,128)(2,1)S(1)}, bf16[1,1,2,64,2560]{4,3,2,1,0:T(8,128)(2,1)}, u32[]{:S(2)}) copy-start(bf16[1,1,2,64,2560]{4,3,2,1,0:T(8,128)(2,1)} %param.10) | copy-start | bytes 1966084
  9.6 31.8 %all-to-all-start = ((bf16[16,160,65]{1,2,0:T(8,128)(2,1)}), bf16[16,160,65]{1,2,0:T(8,128)(2,1)S(1)}, u32[]{:S(2)}, u32[]{:S(2)}) async-start(bf16[16,160,65]{1,2,0:T(8,128)(2,1)} %broadcast_in_dim.35), calls=%async_computation | async-start | bytes 1179648 | tf_op jit(solution)/shard_map/all_to_all | solution.py:362
  18.9 25.9 %copy-start.1 = (bf16[2,64,2560]{2,1,0:T(8,128)(2,1)}, bf16[2,64,2560]{2,1,0:T(8,128)(2,1)S(1)}, u32[]{:S(2)}) copy-start(bf16[2,64,2560]{2,1,0:T(8,128)(2,1)S(1)} %concatenate.46.refs_11_.refs_10_) | copy-start | bytes 1966084
  43.8 2.1 %copy-start.2 = (bf16[16,160,32]{2,1,0:T(8,128)(2,1)}, bf16[16,160,32]{2,1,0:T(8,128)(2,1)S(1)}, u32[]{:S(2)}) copy-start(bf16[16,160,32]{2,1,0:T(8,128)(2,1)S(1)} %copy.39) | copy-start | bytes 491524
  111.5 16.1 %collective-permute-start.1 = (bf16[64,2560]{1,0:T(8,128)(2,1)}, bf16[64,2560]{1,0:T(8,128)(2,1)S(1)}, u32[]{:S(2)}, u32[]{:S(2)}) collective-permute-start(bf16[64,2560]{1,0:T(8,128)(2,1)} %get-tuple-element.27), channel_id=1, source_target_pairs={{16,0},{17,1},{18,2},{19,3},{20,4},{21,5},{22,6},{23,7},{24,8},{25... | collective-permute-start | bytes 983048 | tf_op jit(solution)/shard_map/ppermute | solution.py:453
  126.3 14.6 %collective-permute-start = (bf16[64,2560]{1,0:T(8,128)(2,1)}, bf16[64,2560]{1,0:T(8,128)(2,1)S(1)}, u32[]{:S(2)}, u32[]{:S(2)}) collective-permute-start(bf16[64,2560]{1,0:T(8,128)(2,1)} %get-tuple-element.26), channel_id=1, source_target_pairs={{16,0},{17,1},{18,2},{19,3},{20,4},{21,5},{22,6},{23,7},{24,8},{25... | collective-permute-start | bytes 983048 | tf_op jit(solution)/shard_map/ppermute | solution.py:453
Sparse Core Ops, SparseCore 0:
  9.6 83.1 all-gather.2

commit v5 on v4

--- a/solution.py
+++ b/solution.py
@@ -57,33 +57,41 @@
     )
 
 
-def in_hbm(value):
-    return pltpu.with_memory_space_constraint(value, pltpu.HBM)
-
-
 def stacked(value):
     return jnp.concatenate(
         [value[:, j * HEAD_DIM : (j + 1) * HEAD_DIM] for j in range(GROUP)], axis=0
     )
 
 
+NEEDED_FIRST = (1, 2, 8, 6, 7)
+NEEDED_NEXT = (0, 3, 4, 5)
+NEEDED_LAST = (9, 10, 11, 12)
+
+
+def in_hbm(value):
+    return pltpu.with_memory_space_constraint(value, pltpu.HBM)
+
+
 def step_kernel(order, step, chosen, *refs):
+    first = step == 0
     refs = list(refs)
-    first = step == 0
-    own = refs.pop(0)
-    incoming = refs.pop(0) if step >= 2 else None
-    normed, lowrank = (refs.pop(0), refs.pop(0)) if first else (None, None)
-    rotated = None if first else refs.pop(0)
-    keys, values, bias, cosine, sine, weight, factor_bt, factor_a = refs[:8]
-    rows_in, reciprocal, gain = refs[8:11]
+    given, weight = refs[:13], refs[13]
+    arrays = given
+    incoming = refs[14] if step >= 2 else None
     if first:
-        held, rotated, input_gradient, dquery, middle, grads = refs[11:17]
-        sems = refs[-1]
-        upstream, dq, total, middle_sum = refs[-5:-1]
+        held, rotated, input_gradient, dquery, middle, grads = refs[14:20]
+        staged = refs[20:33]
+        sems, stage_sems = refs[-2:]
+        upstream, dq, total, middle_sum = refs[-6:-2]
+        stage = lambda i: pltpu.make_async_copy(given[i], staged[i], stage_sems.at[i])
+        arrays = staged
     else:
         held = weight
+        rotated = refs[14 + (step >= 2)]
         input_gradient, dquery, middle, grads = refs[-9:-5]
         upstream, dq, total, middle_sum = refs[-4:]
+    own, normed, lowrank, keys, values, bias, cosine, sine = arrays[:8]
+    factor_bt, factor_a, rows_in, reciprocal, gain = arrays[8:]
     h = pl.program_id(0)
     groups = pl.num_programs(0) - 1
     micro = chosen[step]
@@ -98,15 +106,25 @@
     @pl.when(h == 0)
     def _():
         if first:
+            for i in NEEDED_FIRST:
+                stage(i).start()
             fetch(0).start()
+            for i in NEEDED_NEXT:
+                stage(i).start()
             fetch(1).start()
+            for i in NEEDED_LAST:
+                stage(i).start()
+            for i in NEEDED_FIRST:
+                stage(i).wait()
         total[...] = jnp.zeros_like(total)
         middle_sum[...] = jnp.zeros_like(middle_sum)
-        if incoming is None:
-            upstream[...] = own[0]
+        if first:
+            pass
+        elif incoming is None:
+            upstream[...] = own[micro]
         else:
             is_last = chosen[chosen.shape[0] - 1] == 1
-            upstream[...] = jnp.where(is_last, own[0], incoming[...])
+            upstream[...] = jnp.where(is_last, own[micro], incoming[...])
 
     def project():
         query = dot(normed[...], held[h]) + dot(lowrank[...], factor_bt[columns(h), :], NT)
@@ -115,24 +133,23 @@
             for j in range(GROUP):
                 part = query[rows, j * HEAD_DIM : (j + 1) * HEAD_DIM]
                 turned = part * cosine[m] + pltpu.roll(part, HEAD_DIM // 2, 1) * sine[m]
-                rotated[rows, j * HEAD_DIM : (j + 1) * HEAD_DIM] = turned.astype(jnp.bfloat16)
+                at = pl.ds(pl.multiple_of(h * block + j * HEAD_DIM, HEAD_DIM), HEAD_DIM)
+                rotated[rows, at] = turned.astype(jnp.bfloat16)
 
     def pull_back(piece, before):
         at = slice(piece * (width // GROUP), (piece + 1) * (width // GROUP))
         total[:, at] += dot(before, held[h - 1, at, :], NT)
 
     def attend(before=None):
-        if first:
-            mine = rotated[pl.ds(pl.multiple_of(micro * tokens, tokens), tokens), :]
-        else:
-            mine = rotated[...]
-        scores = dot(stacked(mine), keys[...], NT)
-        dprobs = dot(stacked(upstream[:, columns(h)]), values[...], NT)
+        mine = rotated[pl.ds(pl.multiple_of(micro * tokens, tokens), tokens), columns(h)]
+        head = pl.ds(pl.multiple_of(h * HEAD_DIM, HEAD_DIM), HEAD_DIM)
+        scores = dot(stacked(mine), keys[:, head], NT)
+        dprobs = dot(stacked(upstream[:, columns(h)]), values[:, head], NT)
         dscores = []
         for j in range(GROUP):
             for row in range(0, tokens, CHUNK):
                 at = slice(j * tokens + row, j * tokens + row + CHUNK)
-                masked = scores[at] * SCALE + bias[0, row : row + CHUNK]
+                masked = scores[at] * SCALE + bias[micro, row : row + CHUNK]
                 expo = jnp.exp(masked - jnp.max(masked, axis=-1, keepdims=True))
                 probs = expo * (1.0 / jnp.sum(expo, axis=-1, keepdims=True))
                 rounded = probs.astype(jnp.bfloat16).astype(jnp.float32)
@@ -140,13 +157,13 @@
                 dscores.append((probs * (dprobs[at] - delta) * SCALE).astype(jnp.bfloat16))
             if before is not None:
                 pull_back(j, before)
-        drot = dot(jnp.concatenate(dscores, axis=0), keys[...])
+        drot = dot(jnp.concatenate(dscores, axis=0), keys[:, head])
         for j in range(GROUP):
             part = drot[j * tokens : (j + 1) * tokens]
             turned = part * cosine[micro] - pltpu.roll(part, HEAD_DIM // 2, 1) * sine[micro]
             at = slice(j * HEAD_DIM, (j + 1) * HEAD_DIM)
             dq[:, at] = turned.astype(jnp.bfloat16)
-            dquery[0, :, at] = turned.astype(jnp.bfloat16)
+        dquery[micro, :, columns(h)] = dq[...]
         middle_sum[...] += dot(dq[...], factor_bt[columns(h), :])
 
     @pl.when(h == 0)
@@ -154,6 +171,9 @@
         if first:
             fetch(h).wait()
             project()
+            for i in NEEDED_NEXT:
+                stage(i).wait()
+            upstream[...] = own[micro]
         attend()
 
     if first:
@@ -171,14 +191,17 @@
 
     @pl.when(h == groups)
     def _():
+        if first:
+            for i in NEEDED_LAST:
+                stage(i).wait()
         for piece in range(GROUP):
             pull_back(piece, dq[...])
         mid = middle_sum[...].astype(jnp.bfloat16)
-        middle[0] = mid
+        middle[micro] = mid
         dh = (total[...] + dot(mid, factor_a[...], NT)) * gain[...]
-        scaled = rows_in[0].astype(jnp.float32) * reciprocal[0]
+        scaled = rows_in[micro].astype(jnp.float32) * reciprocal[micro]
         mean = jnp.mean(dh * scaled, axis=1, keepdims=True)
-        change = reciprocal[0] * (dh - scaled * mean)
+        change = reciprocal[micro] * (dh - scaled * mean)
         share = change.shape[1] // len(order)
         for k, i in enumerate(order):
             here = slice(i * share, (i + 1) * share)
@@ -187,72 +210,34 @@
         grads[0] = input_gradient[...]
 
 
-def backward(
-    order,
-    step,
-    chosen,
-    own,
-    incoming,
-    normed,
-    lowrank,
-    rotated,
-    keys,
-    values,
-    bias,
-    cosine,
-    sine,
-    weight,
-    factor_bt,
-    factor_a,
-    rows_in,
-    reciprocal,
-    gain,
-    kept,
-):
+def backward(order, step, chosen, staged, weight, incoming, rotated, kept):
     first = step == 0
+    own, keys, factor_a = staged[0], staged[3], staged[9]
     micros, tokens, features = own.shape
     width, rank = factor_a.shape
     ctx = keys.shape[0]
     rows = micros * tokens
     block = features // KV_HEADS
-    group = lambda h: jnp.minimum(h, KV_HEADS - 1)
-    whole = lambda *dims: pl.BlockSpec(dims, lambda h, m: (0,) * len(dims))
-    of_micro = lambda *dims: pl.BlockSpec(
-        (1, *dims), lambda h, m: (m[step],) + (0,) * len(dims)
-    )
     untouched = pl.BlockSpec(memory_space=pl.ANY)
-    of_group = lambda dim: pl.BlockSpec((dim, HEAD_DIM), lambda h, m: (0, group(h)))
-    ins = [(own, of_micro(tokens, features))]
-    if first:
-        ins += [(normed, whole(rows, width)), (lowrank, whole(rows, rank))]
-    else:
-        if incoming is not None:
-            ins.append((incoming, whole(tokens, features)))
-        ins += [
-            (rotated, pl.BlockSpec((tokens, block), lambda h, m: (m[step], group(h)))),
-        ]
-    ins += [
-        (keys, of_group(ctx)),
-        (values, of_group(ctx)),
-        (bias, of_micro(tokens, ctx)),
-        (cosine, whole(micros, tokens, HEAD_DIM)),
-        (sine, whole(micros, tokens, HEAD_DIM)),
-        (weight, untouched if first else pl.BlockSpec(memory_space=pltpu.VMEM)),
-        (factor_bt, whole(features, rank)),
-        (factor_a, whole(width, rank)),
-        (rows_in, of_micro(tokens, width)),
-        (reciprocal, of_micro(tokens, 1)),
-        (gain, whole(1, width)),
-    ]
-    ins += [(a, untouched) for a in kept]
+    in_vmem = pl.BlockSpec(memory_space=pltpu.VMEM)
+    ins = [(in_hbm(a), untouched) if first else (a, in_vmem) for a in staged]
+    ins.append((in_hbm(weight), untouched) if first else (weight, in_vmem))
+    if incoming is not None:
+        ins.append((incoming, in_vmem))
+    if not first:
+        ins.append((rotated, in_vmem))
+    ins += [(a, in_vmem) for a in kept[:2]] + [(a, untouched) for a in kept[2:]]
     outs = [
-        (pltpu.HBM((tokens, width), jnp.bfloat16), whole(tokens, width)),
         (
-            pltpu.HBM((micros, tokens, features), jnp.bfloat16),
-            pl.BlockSpec((1, tokens, block), lambda h, m: (m[step], 0, group(h))),
+            pltpu.HBM((tokens, width), jnp.bfloat16),
+            pl.BlockSpec((tokens, width), lambda h, m: (0, 0)),
         ),
-        (pltpu.HBM((micros, tokens, rank), jnp.bfloat16), of_micro(tokens, rank)),
-        (pltpu.HBM((micros, tokens, width), jnp.bfloat16), of_micro(tokens, width)),
+        (pltpu.VMEM((micros, tokens, features), jnp.bfloat16), in_vmem),
+        (pltpu.VMEM((micros, tokens, rank), jnp.bfloat16), in_vmem),
+        (
+            pltpu.HBM((micros, tokens, width), jnp.bfloat16),
+            pl.BlockSpec((1, tokens, width), lambda h, m: (m[step], 0, 0)),
+        ),
     ]
     scratch = [
         pltpu.VMEM((tokens, features), jnp.bfloat16),
@@ -262,25 +247,16 @@
     ]
     if first:
         outs[:0] = [
-            (
-                pltpu.VMEM((KV_HEADS, width, block), jnp.bfloat16),
-                pl.BlockSpec(memory_space=pltpu.VMEM),
-            ),
-            (
-                pltpu.HBM((rows, features), jnp.bfloat16),
-                pl.BlockSpec((rows, block), lambda h, m: (0, group(h))),
-            ),
+            (pltpu.VMEM((KV_HEADS, width, block), jnp.bfloat16), in_vmem),
+            (pltpu.VMEM((rows, features), jnp.bfloat16), in_vmem),
         ]
+        outs += [(pltpu.VMEM(a.shape, a.dtype), in_vmem) for a in staged]
         scratch.append(pltpu.SemaphoreType.DMA((KV_HEADS,)))
+        scratch.append(pltpu.SemaphoreType.DMA((len(staged),)))
         aliases = {}
     else:
-        outs.append(
-            (
-                pltpu.VMEM((KV_HEADS, width, block), jnp.bfloat16),
-                pl.BlockSpec(memory_space=pltpu.VMEM),
-            )
-        )
-        at = [a is weight for a, _ in ins].index(True)
+        outs.append((pltpu.VMEM((KV_HEADS, width, block), jnp.bfloat16), in_vmem))
+        at = len(staged)
         aliases = {1 + at: 4, len(ins) - 2: 1, len(ins) - 1: 2, len(ins): 3}
     return pl.pallas_call(
         functools.partial(step_kernel, order, step),
@@ -293,19 +269,20 @@
         ),
         out_shape=[shape for shape, _ in outs],
         input_output_aliases=aliases,
-        compiler_params=pltpu.CompilerParams(vmem_limit_bytes=24 * 2**20),
+        compiler_params=pltpu.CompilerParams(vmem_limit_bytes=12 * 2**20),
         cost_estimate=pl.CostEstimate(
             flops=2 * tokens * features * (width + 3 * ctx),
             bytes_accessed=2 * width * features,
             transcendentals=tokens * HEADS * ctx,
         ),
         name="first_step" if first else "step",
-    )(chosen, *(a if a is incoming or (a is weight and not first) else in_hbm(a) for a, _ in ins))
+    )(chosen, *(a for a, _ in ins))
 
 
 def gradients_kernel(order, normed, middle, dquery, lowrank, out):
-    of_a = dot(middle[...], normed[...], TN)
-    of_bt = dot(lowrank[...], dquery[...], TN)
+    flat = lambda ref: ref[...].reshape(normed.shape[0], ref.shape[-1])
+    of_a = dot(flat(middle), normed[...], TN)
+    of_bt = dot(lowrank[...], flat(dquery), TN)
     rank = of_a.shape[0]
     share = of_a.shape[1] // len(order)
     lanes = out.shape[2]
@@ -326,14 +303,16 @@
 
 def gradients(order, normed, middle, dquery, lowrank):
     rows, width = normed.shape
-    rank = middle.shape[1]
+    rank = middle.shape[-1]
     count = len(order)
     share = width // count
     lanes = min(share, HEAD_DIM)
     deep = 2 * rank * share // lanes
     return pl.pallas_call(
         functools.partial(gradients_kernel, order),
+        in_specs=[pl.BlockSpec(memory_space=pltpu.VMEM)] * 4,
         out_shape=jax.ShapeDtypeStruct((count, deep, lanes), jnp.bfloat16),
+        compiler_params=pltpu.CompilerParams(vmem_limit_bytes=12 * 2**20),
         name="gradients",
     )(normed, middle, dquery, lowrank)
 
@@ -418,33 +397,27 @@
     micro = jnp.clip(jnp.arange(steps) - 2 * (last - section), 0, micros - 1)
     chosen = jnp.append(micro, section == last).astype(jnp.int32)
     bias, cosine, sine, reciprocal = map(by_micro, (bias, cosine, sine, reciprocal))
+    staged = [
+        top_grad[0],
+        normed,
+        lowrank,
+        keys,
+        values,
+        bias,
+        cosine,
+        sine,
+        factor_bt,
+        factor_a,
+        rows_in,
+        reciprocal,
+        gain,
+    ]
     for step in range(steps):
-        made = list(
-            backward(
-                order,
-                step,
-                chosen,
-                top_grad[0],
-                arrived[step - 2] if step >= 2 else None,
-                normed,
-                lowrank,
-                rotated,
-                keys,
-                values,
-                bias,
-                cosine,
-                sine,
-                weight,
-                factor_bt,
-                factor_a,
-                rows_in,
-                reciprocal,
-                gain,
-                kept,
-            )
-        )
+        incoming = arrived[step - 2] if step >= 2 else None
+        made = list(backward(order, step, chosen, staged, weight, incoming, rotated, kept))
         if rotated is None:
             weight, rotated = made.pop(0), made.pop(0)
+            made, staged = made[:4], made[4:]
         else:
             weight = made.pop()
         result, *kept = made
@@ -454,9 +427,7 @@
             )
 
     grads = kept[2]
-    dquery = kept[0].reshape(rows, features)
-    middle = kept[1].reshape(rows, -1)
-    partial = gradients(order, normed, middle, dquery, lowrank)
+    partial = gradients(order, staged[1], kept[1], kept[0], staged[2])
     got = lax.all_to_all(partial, "dp", split_axis=0, concat_axis=0, tiled=True)
     total = unfolded(jnp.sum(got.astype(jnp.float32), axis=0), rank, width // len(order))
     return (grads[None, None], total[:rank].T[None], total[rank:].T[None])

time: 183 us -> 174 us (0.951)
  Pallas kernels: 61.1 us -> 52.2 us
    pallas_call x4, Pallas kernels: 58.6 us -> 51.7 us  [backward(): pl.pallas_call(functools.partial(step_kernel, order, step), grid_spec=plt...]
    pallas_call x1, Pallas kernels: 2.5 us -> 0.47 us  [gradients(): pl.pallas_call(functools.partial(gradients_kernel, order), in_specs=[pl.B...]
  transfers between devices with their start and end apart: 4 -> 4, of which waited for: 2 -> 2; matrix products, arithmetic and copies ran while one was open for 6% -> 7% of each run, Pallas kernels for 15% -> 13%
where the time goes in v5:
time: 174 us
  waiting for transfers between devices  66.2 us (38%)
  Pallas kernels  52.2 us (30%)
  blocking collectives  17.8 us (10%)
  between operations  14.3 us (8%)
  starting transfers between devices  10.1 us (6%)
  local copies, waits for them, and re-layouts  7.39 us (4%)
  other arithmetic  5.23 us (3%)
    pallas_call x4, Pallas kernels, backward(): pl.pallas_call(functools.partial(step_kernel, order, step), grid_spec=plt...  51.7 us
    all_gather x1, waiting for transfers between devices, per_device(): lax.all_gather(query_weight[0], 'dp', axis=0, tiled=True, axis_index_grou...  46.8 us
    all_to_all x1, waiting for transfers between devices, gather_small(): return lax.all_to_all(sent, 'dp', split_axis=0, concat_axis=0, tiled=True)  18.7 us
    all_to_all x1, blocking collectives, per_device(): got = lax.all_to_all(partial, 'dp', split_axis=0, concat_axis=0, tiled=True)  17.8 us
    all_to_all x1, starting transfers between devices, gather_small(): return lax.all_to_all(sent, 'dp', split_axis=0, concat_axis=0, tiled=True)  7.36 us
  transfers between devices with their start and end apart: 4, of which 2 were waited for; matrix products, arithmetic and copies ran while one was open for 7% of the time, Pallas kernels for 13%

profile of v5, /device:TPU:0, one launch (start us, length us, event | category | flops | bytes accessed | tf_op | source)
XLA Modules:
  0.0 173.6 jit_solution(3392174792992497710)
XLA Ops:
  7.2 0.7 all-gather.3.cloned.1.call-update
  7.9 0.8 pad_maximum_fusion.2
  8.8 0.9 broadcast_in_dim.35
  9.6 7.4 %all-to-all-start = ((bf16[16,160,65]{1,2,0:T(8,128)(2,1)}), bf16[16,160,65]{1,2,0:T(8,128)(2,1)S(1)}, u32[]{:S(2)}, u32[]{:S(2)}) async-start(bf16[16,160,65]{1,2,0:T(8,128)(2,1)} %broadcast_in_dim.35), calls=%async_computation | async-start | bytes 1179648 | tf_op jit(solution)/shard_map/all_to_all | solution.py:341
  17.2 1.0 gather_fusion
  18.4 0.5 concatenate.46.refs_10_
  19.4 0.8 copy.40.refs_11_
  20.2 0.5 concatenate.56
  21.0 0.8 pad_maximum_fusion
  21.7 1.0 fusion.5.refs_5_
  22.8 18.7 %all-to-all-done = bf16[16,160,65]{1,2,0:T(8,128)(2,1)S(1)} async-done(((bf16[16,160,65]{1,2,0:T(8,128)(2,1)}), bf16[16,160,65]{1,2,0:T(8,128)(2,1)S(1)}, u32[]{:S(2)}, u32[]{:S(2)}) %all-to-all-start) | async-done | bytes 332832 | tf_op jit(solution)/shard_map/all_to_all | solution.py:341
  41.6 0.7 reshape.238.refs_12_
  42.4 1.1 copy.38
  44.2 0.7 copy.39.refs_2_
  44.9 1.1 fusion.1.refs_1_
  46.0 46.8 %all-gather.3.cloned.1.call-done = bf16[1,2560,2560]{2,1,0:T(8,128)(2,1)} async-done(((bf16[1,160,2560]{2,1,0:T(8,128)(2,1)}), bf16[1,2560,2560]{2,1,0:T(8,128)(2,1)}) %all-gather.3.cloned.1.call-update) | async-done | bytes 13107216 | tf_op jit(solution)/shard_map/all_gather | solution.py:364
  92.8 18.3 %first_step.1 = (bf16[4,2560,640]{2,1,0:T(8,128)(2,1)S(1)}, bf16[128,2560]{1,0:T(8,128)(2,1)S(1)}, bf16[64,2560]{1,0:T(8,128)(2,1)}, bf16[2,64,2560]{2,1,0:T(8,1...) custom-call(s32[5]{0:T(128)S(1)} %pad_add_fusion.chosen, ...), custom_call_target="tpu_custom_call" | custom-call | flops 1845493760 | bytes 13107200 | tf_op jit(solution)/shard_map/first_step/pallas_call | solution.py:261
  111.1 1.5 collective-permute-start
  112.6 11.1 %step.3 = (bf16[64,2560]{1,0:T(8,128)(2,1)}, bf16[2,64,2560]{2,1,0:T(8,128)(2,1)S(1)}, bf16[2,64,32]{2,1,0:T(8,128)(2,1)S(1)}, bf16[2,64,2560]{2,1,0:T(8,128)(2,1)}, bf16[4,2560,640]{2,1,0:T(8,128)(2,1)S(1)}) custom-call(s32[5]{0:T(128)S(1)} %pad_add_fusion.chosen, ...), custom_call_target="tpu_custom_call", output_to_operand_aliasing={{4}: (14, {}), {1}: (16, {}), {2}: (17, {}), {3}: (18, {})} | custom-call | flops 1845493760 | bytes 13107200 | tf_op jit(solution)/shard_map/step/pallas_call | solution.py:261
  123.8 1.3 collective-permute-start.1
  125.1 11.1 %step.4 = (bf16[64,2560]{1,0:T(8,128)(2,1)}, bf16[2,64,2560]{2,1,0:T(8,128)(2,1)S(1)}, bf16[2,64,32]{2,1,0:T(8,128)(2,1)S(1)}, bf16[2,64,2560]{2,1,0:T(8,128)(2,1)}, bf16[4,2560,640]{2,1,0:T(8,128)(2,1)S(1)}) custom-call(s32[5]{0:T(128)S(1)} %pad_add_fusion.chosen, ...), custom_call_target="tpu_custom_call", output_to_operand_aliasing={{4}: (14, {}), {1}: (17, {}), {2}: (18, {}), {3}: (19, {})} | custom-call | flops 1845493760 | bytes 13107200 | tf_op jit(solution)/shard_map/step/pallas_call | solution.py:261
  136.2 11.1 %step.5 = (bf16[64,2560]{1,0:T(8,128)(2,1)}, bf16[2,64,2560]{2,1,0:T(8,128)(2,1)S(1)}, bf16[2,64,32]{2,1,0:T(8,128)(2,1)S(1)}, bf16[2,64,2560]{2,1,0:T(8,128)(2,1)}, bf16[4,2560,640]{2,1,0:T(8,128)(2,1)S(1)}) custom-call(s32[5]{0:T(128)S(1)} %pad_add_fusion.chosen, ...), custom_call_target="tpu_custom_call", output_to_operand_aliasing={{4}: (14, {}), {1}: (17, {}), {2}: (18, {}), {3}: (19, {})} | custom-call | flops 1845493760 | bytes 13107200 | tf_op jit(solution)/shard_map/step/pallas_call | solution.py:261
  147.8 17.8 %all_to_all.10 = bf16[16,80,128]{2,1,0:T(8,128)(2,1)S(1)} all-to-all(bf16[16,80,128]{2,1,0:T(8,128)(2,1)S(1)} %gradients.1), channel_id=1, replica_groups=mesh['pipe'=2,'dp'=16] {'dp'}, dimensions={0} | all-to-all | bytes 655360 | tf_op jit(solution)/shard_map/all_to_all | solution.py:431
  166.1 0.6 fusion.8
  (53 shorter events, 3.2 us)
Async XLA Ops:
  7.2 9.8 %copy-start.4 = (s32[1,2]{1,0:T(1,128)S(1)}, s32[1,2]{1,0:T(1,128)}, u32[]{:S(2)}) copy-start(s32[1,2]{1,0:T(1,128)} %param.18) | copy-start | bytes 28
  7.2 10.0 %copy-start = (s32[1,1024]{1,0:T(1,128)S(1)}, s32[1,1024]{1,0:T(1,128)}, u32[]{:S(2)}) copy-start(s32[1,1024]{1,0:T(1,128)} %param.19) | copy-start | bytes 12292
  7.2 85.7 %all-gather.3.cloned.1.call-start = ((), (), s32[]{:S(2)}) async-start(), calls=%async_computation.2 | async-start | bytes 13926400 | tf_op jit(solution)/shard_map/all_gather | solution.py:364
  7.9 10.3 %copy-start.3 = (bf16[1,1,2,64,2560]{4,3,2,1,0:T(8,128)(2,1)S(1)}, bf16[1,1,2,64,2560]{4,3,2,1,0:T(8,128)(2,1)}, u32[]{:S(2)}) copy-start(bf16[1,1,2,64,2560]{4,3,2,1,0:T(8,128)(2,1)} %param.10) | copy-start | bytes 1966084
  9.6 31.8 %all-to-all-start = ((bf16[16,160,65]{1,2,0:T(8,128)(2,1)}), bf16[16,160,65]{1,2,0:T(8,128)(2,1)S(1)}, u32[]{:S(2)}, u32[]{:S(2)}) async-start(bf16[16,160,65]{1,2,0:T(8,128)(2,1)} %broadcast_in_dim.35), calls=%async_computation | async-start | bytes 1179648 | tf_op jit(solution)/shard_map/all_to_all | solution.py:341
  18.9 26.0 %copy-start.1 = (bf16[2,64,2560]{2,1,0:T(8,128)(2,1)}, bf16[2,64,2560]{2,1,0:T(8,128)(2,1)S(1)}, u32[]{:S(2)}) copy-start(bf16[2,64,2560]{2,1,0:T(8,128)(2,1)S(1)} %concatenate.46.refs_10_) | copy-start | bytes 1966084
  43.8 2.2 %copy-start.2 = (bf16[16,160,32]{2,1,0:T(8,128)(2,1)}, bf16[16,160,32]{2,1,0:T(8,128)(2,1)S(1)}, u32[]{:S(2)}) copy-start(bf16[16,160,32]{2,1,0:T(8,128)(2,1)S(1)} %copy.37) | copy-start | bytes 491524
  111.1 13.9 %collective-permute-start = (bf16[64,2560]{1,0:T(8,128)(2,1)}, bf16[64,2560]{1,0:T(8,128)(2,1)S(1)}, u32[]{:S(2)}, u32[]{:S(2)}) collective-permute-start(bf16[64,2560]{1,0:T(8,128)(2,1)} %get-tuple-element.53), channel_id=1, source_target_pairs={{16,0},{17,1},{18,2},{19,3},{20,4},{21,5},{22,6},{23,7},{24,8},{25... | collective-permute-start | bytes 983048 | tf_op jit(solution)/shard_map/ppermute | solution.py:426
  123.8 12.5 %collective-permute-start.1 = (bf16[64,2560]{1,0:T(8,128)(2,1)}, bf16[64,2560]{1,0:T(8,128)(2,1)S(1)}, u32[]{:S(2)}, u32[]{:S(2)}) collective-permute-start(bf16[64,2560]{1,0:T(8,128)(2,1)} %get-tuple-element.58), channel_id=1, source_target_pairs={{16,0},{17,1},{18,2},{19,3},{20,4},{21,5},{22,6},{23,7},{24,8},{25... | collective-permute-start | bytes 983048 | tf_op jit(solution)/shard_map/ppermute | solution.py:426
Sparse Core Ops, SparseCore 0:
  9.6 83.1 all-gather.2

commit v6 on v5

--- a/solution.py
+++ b/solution.py
@@ -72,21 +72,51 @@
     return pltpu.with_memory_space_constraint(value, pltpu.HBM)
 
 
-def step_kernel(order, step, chosen, *refs):
+def weight_pieces(shard, order):
+    count = len(order)
+    if count > 16 or count % 4:
+        whole = lax.all_gather(shard, "dp", axis=0, tiled=True, axis_index_groups=[order])
+        return [whole], jnp.zeros((1,), jnp.int32)
+    chips = count // 2
+    ahead = [
+        (order[2 * k + core], order[2 * ((k + 1) % chips) + core])
+        for k in range(chips)
+        for core in range(2)
+    ]
+    behind = [(to, source) for source, to in ahead]
+    pair = [(i, i ^ 1) for i in range(count)]
+    table = jnp.array([order.index(i) for i in range(count)], jnp.int32)
+    me = table[lax.axis_index("dp")]
+    pieces, places = [shard], [me]
+    forward = backward = shard
+    for hop in range(1, chips // 2 + 1):
+        forward = lax.ppermute(forward, "dp", ahead)
+        pieces.append(forward)
+        places.append((me - 2 * hop) % count)
+        if hop <= (chips - 1) // 2:
+            backward = lax.ppermute(backward, "dp", behind)
+            pieces.append(backward)
+            places.append((me + 2 * hop) % count)
+    pieces += [lax.ppermute(piece, "dp", pair) for piece in pieces]
+    places += [place ^ 1 for place in places]
+    return pieces, jnp.stack(places)
+
+
+def step_kernel(order, step, steps, chosen, *refs):
     first = step == 0
     refs = list(refs)
-    given, weight = refs[:13], refs[13]
-    arrays = given
+    given = arrays = refs[:13]
     incoming = refs[14] if step >= 2 else None
     if first:
-        held, rotated, input_gradient, dquery, middle, grads = refs[14:20]
-        staged = refs[20:33]
+        pieces = refs[13:-25]
+        held, rotated, input_gradient, dquery, middle, grads = refs[-25:-19]
+        staged = refs[-19:-6]
         sems, stage_sems = refs[-2:]
         upstream, dq, total, middle_sum = refs[-6:-2]
         stage = lambda i: pltpu.make_async_copy(given[i], staged[i], stage_sems.at[i])
         arrays = staged
     else:
-        held = weight
+        held = refs[13]
         rotated = refs[14 + (step >= 2)]
         input_gradient, dquery, middle, grads = refs[-9:-5]
         upstream, dq, total, middle_sum = refs[-4:]
@@ -94,24 +124,37 @@
     factor_bt, factor_a, rows_in, reciprocal, gain = arrays[8:]
     h = pl.program_id(0)
     groups = pl.num_programs(0) - 1
-    micro = chosen[step]
+    micro = chosen[1 + step]
     tokens = bias.shape[1]
     width = gain.shape[1]
     block = GROUP * HEAD_DIM
     columns = lambda g: pl.ds(pl.multiple_of(g * block, HEAD_DIM), block)
-    fetch = lambda g: pltpu.make_async_copy(
-        weight.at[:, columns(g)], held.at[g], sems.at[g]
-    )
+
+    def fetch(g):
+        copies = []
+        for i, piece in enumerate(pieces):
+            share = piece.shape[0]
+            place = chosen[1 + steps + i] if len(pieces) > 1 else 0
+            rows = pl.ds(pl.multiple_of(place * share, share), share)
+            copies.append(
+                pltpu.make_async_copy(
+                    piece.at[:, columns(g)], held.at[g, rows, :], sems.at[g, i]
+                )
+            )
+        return copies
+
 
     @pl.when(h == 0)
     def _():
         if first:
             for i in NEEDED_FIRST:
                 stage(i).start()
-            fetch(0).start()
+            for copy in fetch(0):
+                copy.start()
             for i in NEEDED_NEXT:
                 stage(i).start()
-            fetch(1).start()
+            for copy in fetch(1):
+                copy.start()
             for i in NEEDED_LAST:
                 stage(i).start()
             for i in NEEDED_FIRST:
@@ -123,7 +166,7 @@
         elif incoming is None:
             upstream[...] = own[micro]
         else:
-            is_last = chosen[chosen.shape[0] - 1] == 1
+            is_last = chosen[0] == 1
             upstream[...] = jnp.where(is_last, own[micro], incoming[...])
 
     def project():
@@ -169,7 +212,8 @@
     @pl.when(h == 0)
     def _():
         if first:
-            fetch(h).wait()
+            for copy in fetch(h):
+                copy.wait()
             project()
             for i in NEEDED_NEXT:
                 stage(i).wait()
@@ -180,12 +224,14 @@
 
         @pl.when((h > 0) & (h + 1 < groups))
         def _():
-            fetch(h + 1).start()
+            for copy in fetch(h + 1):
+                copy.start()
 
     @pl.when((h > 0) & (h < groups))
     def _():
         if first:
-            fetch(h).wait()
+            for copy in fetch(h):
+                copy.wait()
             project()
         attend(dq[...])
 
@@ -210,7 +256,7 @@
         grads[0] = input_gradient[...]
 
 
-def backward(order, step, chosen, staged, weight, incoming, rotated, kept):
+def backward(order, step, steps, chosen, staged, weight, incoming, rotated, kept):
     first = step == 0
     own, keys, factor_a = staged[0], staged[3], staged[9]
     micros, tokens, features = own.shape
@@ -221,7 +267,7 @@
     untouched = pl.BlockSpec(memory_space=pl.ANY)
     in_vmem = pl.BlockSpec(memory_space=pltpu.VMEM)
     ins = [(in_hbm(a), untouched) if first else (a, in_vmem) for a in staged]
-    ins.append((in_hbm(weight), untouched) if first else (weight, in_vmem))
+    ins += [(piece, untouched) for piece in weight] if first else [(weight, in_vmem)]
     if incoming is not None:
         ins.append((incoming, in_vmem))
     if not first:
@@ -236,7 +282,7 @@
         (pltpu.VMEM((micros, tokens, rank), jnp.bfloat16), in_vmem),
         (
             pltpu.HBM((micros, tokens, width), jnp.bfloat16),
-            pl.BlockSpec((1, tokens, width), lambda h, m: (m[step], 0, 0)),
+            pl.BlockSpec((1, tokens, width), lambda h, m: (m[1 + step], 0, 0)),
         ),
     ]
     scratch = [
@@ -251,7 +297,7 @@
             (pltpu.VMEM((rows, features), jnp.bfloat16), in_vmem),
         ]
         outs += [(pltpu.VMEM(a.shape, a.dtype), in_vmem) for a in staged]
-        scratch.append(pltpu.SemaphoreType.DMA((KV_HEADS,)))
+        scratch.append(pltpu.SemaphoreType.DMA((KV_HEADS, len(weight))))
         scratch.append(pltpu.SemaphoreType.DMA((len(staged),)))
         aliases = {}
     else:
@@ -259,7 +305,7 @@
         at = len(staged)
         aliases = {1 + at: 4, len(ins) - 2: 1, len(ins) - 1: 2, len(ins): 3}
     return pl.pallas_call(
-        functools.partial(step_kernel, order, step),
+        functools.partial(step_kernel, order, step, steps),
         grid_spec=pltpu.PrefetchScalarGridSpec(
             num_scalar_prefetch=1,
             grid=(KV_HEADS + 1,),
@@ -361,9 +407,7 @@
     features = query_weight.shape[2]
     rank = adapter_a.shape[2]
 
-    weight = lax.all_gather(
-        query_weight[0], "dp", axis=0, tiled=True, axis_index_groups=[order]
-    )
+    weight, places = weight_pieces(query_weight[0], order)
     small = gather_small(adapter_a[0], adapter_bt[0], norm_gain[0])
     factor_bt = small[:, :, rank : 2 * rank].reshape(features, rank)
     walked = jnp.concatenate([small[i : i + 1] for i in order], axis=0)
@@ -395,7 +439,8 @@
     steps = 2 * last + micros
     kept, arrived, rotated = (), [], None
     micro = jnp.clip(jnp.arange(steps) - 2 * (last - section), 0, micros - 1)
-    chosen = jnp.append(micro, section == last).astype(jnp.int32)
+    is_last = jnp.reshape(section == last, 1).astype(jnp.int32)
+    chosen = jnp.concatenate([is_last, micro.astype(jnp.int32), places])
     bias, cosine, sine, reciprocal = map(by_micro, (bias, cosine, sine, reciprocal))
     staged = [
         top_grad[0],
@@ -414,7 +459,7 @@
     ]
     for step in range(steps):
         incoming = arrived[step - 2] if step >= 2 else None
-        made = list(backward(order, step, chosen, staged, weight, incoming, rotated, kept))
+        made = list(backward(order, step, steps, chosen, staged, weight, incoming, rotated, kept))
         if rotated is None:
             weight, rotated = made.pop(0), made.pop(0)
             made, staged = made[:4], made[4:]

time: 174 us -> 174 us (level)
  waiting for transfers between devices: 66.2 us -> 42.9 us
  local copies, waits for them, and re-layouts: 7.39 us -> 22.9 us
  starting transfers between devices: 10.1 us -> 22.8 us
  between operations: 14.3 us -> 5.94 us
  other arithmetic: 5.23 us -> 8.99 us
  blocking collectives: 17.8 us -> 15 us
  matrix products: 0.39 us -> 2.27 us
    all_gather x1 -> x0, waiting for transfers between devices: 46.8 us -> none  [per_device(): lax.all_gather(query_weight[0], 'dp', axis=0, tiled=True, axis_index_grou...]
    ppermute x0 -> x15, waiting for transfers between devices: none -> 42.9 us  [the longest x4 32.3 us: weight_pieces(): forward = lax.ppermute(forward, 'dp', ahead)]
    all_to_all x1, waiting for transfers between devices: 18.7 us -> 0.01 us  [gather_small(): return lax.all_to_all(sent, 'dp', split_axis=0, concat_axis=0, tiled=True)]
    ppermute x0 -> x15, starting transfers between devices: none -> 13.8 us  [the longest x4 7.57 us: weight_pieces(): forward = lax.ppermute(forward, 'dp', ahead)]
    unnamed x23 -> x29, local copies, waits for them, and re-layouts: 0.43 us -> 5.76 us
    all_to_all x1, blocking collectives: 17.8 us -> 15 us  [per_device(): got = lax.all_to_all(partial, 'dp', split_axis=0, concat_axis=0, tiled=True)]
    concatenate x2, local copies, waits for them, and re-layouts: 0.95 us -> 3.25 us  [reordered(): jnp.concatenate([value[..., i * share:(i + 1) * share] for i in order], a...]
    dot_general x1, matrix products: 0.39 us -> 2.27 us  [dot(): return lax.dot_general(a, b, dims, preferred_element_type=jnp.float32)]
  transfers between devices with their start and end apart: 4 -> 18, of which waited for: 2 -> 5; matrix products, arithmetic and copies ran while one was open for 7% -> 19% of each run, Pallas kernels for 13% -> 13%
where the time goes in v6:
time: 174 us; the launch traced here: 173 us
  Pallas kernels  51.9 us (30%)
  waiting for transfers between devices  42.9 us (25%)
  local copies, waits for them, and re-layouts  22.9 us (13%)
  starting transfers between devices  22.8 us (13%)
  blocking collectives  15 us (9%)
  other arithmetic  8.99 us (5%)
  between operations  5.94 us (3%)
  matrix products  2.27 us (1%)
    pallas_call x4, Pallas kernels, backward(): pl.pallas_call(functools.partial(step_kernel, order, step, steps), grid_s...  51.4 us
    ppermute x4, waiting for transfers between devices, weight_pieces(): forward = lax.ppermute(forward, 'dp', ahead)  32.3 us
    all_to_all x1, blocking collectives, per_device(): got = lax.all_to_all(partial, 'dp', split_axis=0, concat_axis=0, tiled=True)  15 us
    ppermute x3, waiting for transfers between devices, weight_pieces(): backward = lax.ppermute(backward, 'dp', behind)  10.6 us
    ppermute x4, starting transfers between devices, weight_pieces(): forward = lax.ppermute(forward, 'dp', ahead)  7.57 us
    all_to_all x1, starting transfers between devices, gather_small(): return lax.all_to_all(sent, 'dp', split_axis=0, concat_axis=0, tiled=True)  6.32 us
    unnamed x29, local copies, waits for them, and re-layouts  5.76 us
    ppermute x3, starting transfers between devices, weight_pieces(): backward = lax.ppermute(backward, 'dp', behind)  4.58 us
  transfers between devices with their start and end apart: 18, of which 5 were waited for; matrix products, arithmetic and copies ran while one was open for 19% of the time, Pallas kernels for 13%

profile of v6, /device:TPU:0, one launch (start us, length us, event | category | flops | bytes accessed | tf_op | source)
XLA Modules:
  0.0 172.8 jit_solution(7872381313193206524)
XLA Ops:
  1.2 2.6 %collective-permute-start.1 = (bf16[160,2560]{1,0:T(8,128)(2,1)}, bf16[160,2560]{1,0:T(8,128)(2,1)S(1)}, u32[]{:S(2)}, u32[]{:S(2)}) collective-permute-start(bf16[160,2560]{1,0:T(8,128)(2,1)} %bitcast.62), channel_id=1, source_target_pairs={{4,0},{5,1},{8,4},{9,5},{12,8},{13,9},{14,12},{15,13},{10,14},{11,... | collective-permute-start | bytes 2457608 | tf_op jit(solution)/shard_map/ppermute | solution.py:97
  5.5 6.3 %all-to-all-start = ((bf16[16,160,65]{1,2,0:T(8,128)(2,1)}), bf16[16,160,65]{1,2,0:T(8,128)(2,1)}, u32[]{:S(2)}, u32[]{:S(2)}) async-start(bf16[16,160,65]{1,2,0:T(8,128)(2,1)} %broadcast_in_dim.35), calls=%async_computation | async-start | bytes 1179648 | tf_op jit(solution)/shard_map/all_to_all | solution.py:387
  14.0 1.3 concatenate.45.refs_10_
  15.6 9.9 %collective-permute-done.refs_14_ = bf16[160,2560]{1,0:T(8,128)(2,1)S(1)} collective-permute-done((bf16[160,2560]{1,0:T(8,128)(2,1)}, bf16[160,2560]{1,0:T(8,128)(2,1)S(1)}, u32[]{:S(2)}, u32[]{:S(2)}) %collective-permute-start) | collective-permute-done | bytes 819232 | tf_op jit(solution)/shard_map/ppermute | solution.py:93
  28.1 2.0 %collective-permute-start.3 = (bf16[160,2560]{1,0:T(8,128)(2,1)S(1)}, bf16[160,2560]{1,0:T(8,128)(2,1)}, u32[]{:S(2)}, u32[]{:S(2)}) collective-permute-start(bf16[160,2560]{1,0:T(8,128)(2,1)S(1)} %collective-permute-done.1.refs_15_), channel_id=1, source_target_pairs={{4,0},{5,1},{8,4},{9,5},{12,8},{13,9},{14,12},{15,13},{10,14},{11,... | collective-permute-start | bytes 2457608 | tf_op jit(solution)/shard_map/ppermute | solution.py:97
  30.1 19.2 %collective-permute-done.2.refs_16_ = bf16[160,2560]{1,0:T(8,128)(2,1)} collective-permute-done((bf16[160,2560]{1,0:T(8,128)(2,1)S(1)}, bf16[160,2560]{1,0:T(8,128)(2,1)}, u32[]{:S(2)}, u32[]{:S(2)}) %collective-permute-start.2) | collective-permute-done | bytes 819232 | tf_op jit(solution)/shard_map/ppermute | solution.py:93
  49.3 4.8 %collective-permute-start.4 = (bf16[160,2560]{1,0:T(8,128)(2,1)}, bf16[160,2560]{1,0:T(8,128)(2,1)}, u32[]{:S(2)}, u32[]{:S(2)}) collective-permute-start(bf16[160,2560]{1,0:T(8,128)(2,1)} %collective-permute-done.2.refs_16_), channel_id=1, source_target_pairs={{0,4},{1,5},{4,8},{5,9},{8,12},{9,13},{12,14},{13,15},{14,10},{15,... | collective-permute-start | bytes 2457608 | tf_op jit(solution)/shard_map/ppermute | solution.py:93
  60.4 1.3 rsqrt.24
  62.4 2.0 %concatenate.55 = bf16[128,2560]{1,0:T(8,128)(2,1)} concatenate(bf16[128,320]{1,0:T(8,128)(2,1)} %bitcast.79, bf16[128,320]{1,0:T(8,128)(2,1)} %bitcast.78, bf16[128,320]{1,0:T(8,128)(2,1)} %bitcast.77, bf16[128,640]{1,0:T(8,128)(2,1)S(1)} %bitcast.71, bf16[128,320]{1,0:T(8,128)(2,1)} %bitcast.76, bf16[128,320]{1,0:T(8,128)(2,1)S(1)} %bitcast.75, bf16[128,320]{1,0:T(8,128)(2,1)S(1)} %bitcast.74), dimensions={1} | concatenate | bytes 1310720 | tf_op jit(solution)/shard_map/concatenate | solution.py:55
  65.1 1.7 pad_maximum_fusion
  70.0 1.4 collective-permute-done.4.refs_18_
  71.4 2.6 %collective-permute-start.6 = (bf16[160,2560]{1,0:T(8,128)(2,1)}, bf16[160,2560]{1,0:T(8,128)(2,1)}, u32[]{:S(2)}, u32[]{:S(2)}) collective-permute-start(bf16[160,2560]{1,0:T(8,128)(2,1)} %collective-permute-done.4.refs_18_), channel_id=1, source_target_pairs={{0,4},{1,5},{4,8},{5,9},{8,12},{9,13},{12,14},{13,15},{14,10},{15,... | collective-permute-start | bytes 2457608 | tf_op jit(solution)/shard_map/ppermute | solution.py:93
  80.7 10.6 %collective-permute-done.5.refs_19_ = bf16[160,2560]{1,0:T(8,128)(2,1)} collective-permute-done((bf16[160,2560]{1,0:T(8,128)(2,1)}, bf16[160,2560]{1,0:T(8,128)(2,1)}, u32[]{:S(2)}, u32[]{:S(2)}) %collective-permute-start.5) | collective-permute-done | bytes 819232 | tf_op jit(solution)/shard_map/ppermute | solution.py:97
  91.3 1.8 %collective-permute-done.6.refs_20_ = bf16[160,2560]{1,0:T(8,128)(2,1)} collective-permute-done((bf16[160,2560]{1,0:T(8,128)(2,1)}, bf16[160,2560]{1,0:T(8,128)(2,1)}, u32[]{:S(2)}, u32[]{:S(2)}) %collective-permute-start.6) | collective-permute-done | bytes 819232 | tf_op jit(solution)/shard_map/ppermute | solution.py:93
  93.2 2.3 %convolution_convert_fusion = bf16[128,32]{0,1:T(8,128)(2,1)} fusion(bf16[2560,32]{1,0:T(8,128)(2,1)} %bitcast.68, bf16[128,2560]{1,0:T(8,128)(2,1)} %concatenate.55, f32[2560]{0:T(1024)S(1)} %reshape.253, f32[128]{0:T(128)} %rsqrt.24), kind=kOutput, calls=%fused_computation.6 | convolution fusion | flops 22286336 | bytes 838144 | tf_op jit(solution)/shard_map/dot_general | solution.py:25
  98.3 1.4 copy.40.refs_2_
  99.7 2.2 %fusion.1.refs_1_ = bf16[128,2560]{1,0:T(8,128)(2,1)} fusion(f32[2560]{0:T(1024)S(1)} %reshape.253, f32[128]{0:T(128)} %rsqrt.24, bf16[2,64,2560]{2,1,0:T(8,128)(2,1)} %copy-done.4), kind=kLoop, calls=%fused_computation.3 | loop fusion | flops 1310720 | bytes 1321472 | tf_op jit(solution)/shard_map/convert_element_type | solution.py:420
  102.0 18.3 %first_step.1 = (bf16[4,2560,640]{2,1,0:T(8,128)(2,1)S(1)}, bf16[128,2560]{1,0:T(8,128)(2,1)S(1)}, bf16[64,2560]{1,0:T(8,128)(2,1)}, bf16[2,64,2560]{2,1,0:T(8,1...) custom-call(s32[21]{0:T(128)S(1)} %concatenate.44.chosen, ...), custom_call_target="tpu_custom_call" | custom-call | flops 1845493760 | bytes 13107200 | tf_op jit(solution)/shard_map/first_step/pallas_call | solution.py:307
  120.3 1.5 collective-permute-start.15
  121.8 11.0 %step.3 = (bf16[64,2560]{1,0:T(8,128)(2,1)}, bf16[2,64,2560]{2,1,0:T(8,128)(2,1)S(1)}, bf16[2,64,32]{2,1,0:T(8,128)(2,1)S(1)}, bf16[2,64,2560]{2,1,0:T(8,128)(2,1)}, bf16[4,2560,640]{2,1,0:T(8,128)(2,1)S(1)}) custom-call(s32[21]{0:T(128)S(1)} %concatenate.44.chosen, ...), custom_call_target="tpu_custom_call", output_to_operand_aliasing={{4}: (14, {}), {1}: (16, {}), {2}: (17, {}), {3}: (18, {})} | custom-call | flops 1845493760 | bytes 13107200 | tf_op jit(solution)/shard_map/step/pallas_call | solution.py:307
  132.8 1.3 collective-permute-start.16
  134.1 11.0 %step.4 = (bf16[64,2560]{1,0:T(8,128)(2,1)}, bf16[2,64,2560]{2,1,0:T(8,128)(2,1)S(1)}, bf16[2,64,32]{2,1,0:T(8,128)(2,1)S(1)}, bf16[2,64,2560]{2,1,0:T(8,128)(2,1)}, bf16[4,2560,640]{2,1,0:T(8,128)(2,1)S(1)}) custom-call(s32[21]{0:T(128)S(1)} %concatenate.44.chosen, ...), custom_call_target="tpu_custom_call", output_to_operand_aliasing={{4}: (14, {}), {1}: (17, {}), {2}: (18, {}), {3}: (19, {})} | custom-call | flops 1845493760 | bytes 13107200 | tf_op jit(solution)/shard_map/step/pallas_call | solution.py:307
  145.2 11.0 %step.5 = (bf16[64,2560]{1,0:T(8,128)(2,1)}, bf16[2,64,2560]{2,1,0:T(8,128)(2,1)S(1)}, bf16[2,64,32]{2,1,0:T(8,128)(2,1)S(1)}, bf16[2,64,2560]{2,1,0:T(8,128)(2,1)}, bf16[4,2560,640]{2,1,0:T(8,128)(2,1)S(1)}) custom-call(s32[21]{0:T(128)S(1)} %concatenate.44.chosen, ...), custom_call_target="tpu_custom_call", output_to_operand_aliasing={{4}: (14, {}), {1}: (17, {}), {2}: (18, {}), {3}: (19, {})} | custom-call | flops 1845493760 | bytes 13107200 | tf_op jit(solution)/shard_map/step/pallas_call | solution.py:307
  156.7 15.0 %all_to_all.10 = bf16[16,80,128]{2,1,0:T(8,128)(2,1)S(1)} all-to-all(bf16[16,80,128]{2,1,0:T(8,128)(2,1)S(1)} %gradients.1), channel_id=1, replica_groups=mesh['pipe'=2,'dp'=16] {'dp'}, dimensions={0} | all-to-all | bytes 655360 | tf_op jit(solution)/shard_map/all_to_all | solution.py:476
  (87 shorter events, 24.4 us)
Async XLA Ops:
  0.6 11.2 %copy-start.7 = (s32[1,2]{1,0:T(1,128)S(1)}, s32[1,2]{1,0:T(1,128)}, u32[]{:S(2)}) copy-start(s32[1,2]{1,0:T(1,128)} %param.19) | copy-start | bytes 28
  0.6 11.4 %copy-start.3 = (s32[1,1024]{1,0:T(1,128)S(1)}, s32[1,1024]{1,0:T(1,128)}, u32[]{:S(2)}) copy-start(s32[1,1024]{1,0:T(1,128)} %param.20) | copy-start | bytes 12292
  0.7 12.5 %copy-start.5 = (bf16[1,1,2,64,2560]{4,3,2,1,0:T(8,128)(2,1)S(1)}, bf16[1,1,2,64,2560]{4,3,2,1,0:T(8,128)(2,1)}, u32[]{:S(2)}) copy-start(bf16[1,1,2,64,2560]{4,3,2,1,0:T(8,128)(2,1)} %param.11) | copy-start | bytes 1966084
  0.7 79.5 %collective-permute-start.7 = (bf16[160,2560]{1,0:T(8,128)(2,1)}, bf16[160,2560]{1,0:T(8,128)(2,1)S(1)}, u32[]{:S(2)}, u32[]{:S(2)}) collective-permute-start(bf16[160,2560]{1,0:T(8,128)(2,1)} %bitcast.61), channel_id=1, source_target_pairs={{0,1},{1,0},{2,3},{3,2},{4,5},{5,4},{6,7},{7,6},{8,9},{9,8},{10,11... | collective-permute-start | bytes 2457608 | tf_op jit(solution)/shard_map/ppermute | solution.py:100
  1.2 26.9 %collective-permute-start.1 = (bf16[160,2560]{1,0:T(8,128)(2,1)}, bf16[160,2560]{1,0:T(8,128)(2,1)S(1)}, u32[]{:S(2)}, u32[]{:S(2)}) collective-permute-start(bf16[160,2560]{1,0:T(8,128)(2,1)} %bitcast.62), channel_id=1, source_target_pairs={{4,0},{5,1},{8,4},{9,5},{12,8},{13,9},{14,12},{15,13},{10,14},{11,... | collective-permute-start | bytes 2457608 | tf_op jit(solution)/shard_map/ppermute | solution.py:97
  3.7 21.7 %collective-permute-start = (bf16[160,2560]{1,0:T(8,128)(2,1)}, bf16[160,2560]{1,0:T(8,128)(2,1)S(1)}, u32[]{:S(2)}, u32[]{:S(2)}) collective-permute-start(bf16[160,2560]{1,0:T(8,128)(2,1)} %bitcast.63), channel_id=1, source_target_pairs={{0,4},{1,5},{4,8},{5,9},{8,12},{9,13},{12,14},{13,15},{14,10},{15,... | collective-permute-start | bytes 2457608 | tf_op jit(solution)/shard_map/ppermute | solution.py:93
  5.5 61.2 %all-to-all-start = ((bf16[16,160,65]{1,2,0:T(8,128)(2,1)}), bf16[16,160,65]{1,2,0:T(8,128)(2,1)}, u32[]{:S(2)}, u32[]{:S(2)}) async-start(bf16[16,160,65]{1,2,0:T(8,128)(2,1)} %broadcast_in_dim.35), calls=%async_computation | async-start | bytes 1179648 | tf_op jit(solution)/shard_map/all_to_all | solution.py:387
  15.3 49.1 %copy-start.4 = (bf16[2,64,2560]{2,1,0:T(8,128)(2,1)}, bf16[2,64,2560]{2,1,0:T(8,128)(2,1)S(1)}, u32[]{:S(2)}) copy-start(bf16[2,64,2560]{2,1,0:T(8,128)(2,1)S(1)} %concatenate.45.refs_10_) | copy-start | bytes 1966084
  25.4 23.8 %collective-permute-start.2 = (bf16[160,2560]{1,0:T(8,128)(2,1)S(1)}, bf16[160,2560]{1,0:T(8,128)(2,1)}, u32[]{:S(2)}, u32[]{:S(2)}) collective-permute-start(bf16[160,2560]{1,0:T(8,128)(2,1)S(1)} %collective-permute-done.refs_14_), channel_id=1, source_target_pairs={{0,4},{1,5},{4,8},{5,9},{8,12},{9,13},{12,14},{13,15},{14,10},{15,... | collective-permute-start | bytes 2457608 | tf_op jit(solution)/shard_map/ppermute | solution.py:93
  28.1 41.9 %collective-permute-start.3 = (bf16[160,2560]{1,0:T(8,128)(2,1)S(1)}, bf16[160,2560]{1,0:T(8,128)(2,1)}, u32[]{:S(2)}, u32[]{:S(2)}) collective-permute-start(bf16[160,2560]{1,0:T(8,128)(2,1)S(1)} %collective-permute-done.1.refs_15_), channel_id=1, source_target_pairs={{4,0},{5,1},{8,4},{9,5},{12,8},{13,9},{14,12},{15,13},{10,14},{11,... | collective-permute-start | bytes 2457608 | tf_op jit(solution)/shard_map/ppermute | solution.py:97
  49.3 22.1 %collective-permute-start.4 = (bf16[160,2560]{1,0:T(8,128)(2,1)}, bf16[160,2560]{1,0:T(8,128)(2,1)}, u32[]{:S(2)}, u32[]{:S(2)}) collective-permute-start(bf16[160,2560]{1,0:T(8,128)(2,1)} %collective-permute-done.2.refs_16_), channel_id=1, source_target_pairs={{0,4},{1,5},{4,8},{5,9},{8,12},{9,13},{12,14},{13,15},{14,10},{15,... | collective-permute-start | bytes 2457608 | tf_op jit(solution)/shard_map/ppermute | solution.py:93
  69.5 10.7 %collective-permute-start.9 = (bf16[160,2560]{1,0:T(8,128)(2,1)S(1)}, bf16[160,2560]{1,0:T(8,128)(2,1)S(1)}, u32[]{:S(2)}, u32[]{:S(2)}) collective-permute-start(bf16[160,2560]{1,0:T(8,128)(2,1)S(1)} %collective-permute-done.1.refs_15_), channel_id=1, source_target_pairs={{0,1},{1,0},{2,3},{3,2},{4,5},{5,4},{6,7},{7,6},{8,9},{9,8},{10,11... | collective-permute-start | bytes 2457608 | tf_op jit(solution)/shard_map/ppermute | solution.py:100
  69.5 11.2 %collective-permute-start.8 = (bf16[160,2560]{1,0:T(8,128)(2,1)S(1)}, bf16[160,2560]{1,0:T(8,128)(2,1)}, u32[]{:S(2)}, u32[]{:S(2)}) collective-permute-start(bf16[160,2560]{1,0:T(8,128)(2,1)S(1)} %collective-permute-done.refs_14_), channel_id=1, source_target_pairs={{0,1},{1,0},{2,3},{3,2},{4,5},{5,4},{6,7},{7,6},{8,9},{9,8},{10,11... | collective-permute-start | bytes 2457608 | tf_op jit(solution)/shard_map/ppermute | solution.py:100
  70.0 21.4 %collective-permute-start.5 = (bf16[160,2560]{1,0:T(8,128)(2,1)}, bf16[160,2560]{1,0:T(8,128)(2,1)}, u32[]{:S(2)}, u32[]{:S(2)}) collective-permute-start(bf16[160,2560]{1,0:T(8,128)(2,1)} %collective-permute-done.3.refs_17_), channel_id=1, source_target_pairs={{4,0},{5,1},{8,4},{9,5},{12,8},{13,9},{14,12},{15,13},{10,14},{11,... | collective-permute-start | bytes 2457608 | tf_op jit(solution)/shard_map/ppermute | solution.py:97
  71.4 21.8 %collective-permute-start.6 = (bf16[160,2560]{1,0:T(8,128)(2,1)}, bf16[160,2560]{1,0:T(8,128)(2,1)}, u32[]{:S(2)}, u32[]{:S(2)}) collective-permute-start(bf16[160,2560]{1,0:T(8,128)(2,1)} %collective-permute-done.4.refs_18_), channel_id=1, source_target_pairs={{0,4},{1,5},{4,8},{5,9},{8,12},{9,13},{12,14},{13,15},{14,10},{15,... | collective-permute-start | bytes 2457608 | tf_op jit(solution)/shard_map/ppermute | solution.py:93
  80.1 15.3 %copy-start.6 = (f32[16,160]{1,0:T(8,128)S(1)}, f32[16,160]{1,0:T(8,128)}, u32[]{:S(2)}) copy-start(f32[16,160]{1,0:T(8,128)} %fusion.10) | copy-start | bytes 30724
  80.1 21.8 %collective-permute-start.11 = (bf16[160,2560]{1,0:T(8,128)(2,1)}, bf16[160,2560]{1,0:T(8,128)(2,1)}, u32[]{:S(2)}, u32[]{:S(2)}) collective-permute-start(bf16[160,2560]{1,0:T(8,128)(2,1)} %collective-permute-done.3.refs_17_), channel_id=1, source_target_pairs={{0,1},{1,0},{2,3},{3,2},{4,5},{5,4},{6,7},{7,6},{8,9},{9,8},{10,11... | collective-permute-start | bytes 2457608 | tf_op jit(solution)/shard_map/ppermute | solution.py:100
  80.2 15.3 %copy-start.1 = (bf16[160,2560]{1,0:T(8,128)(2,1)}, bf16[160,2560]{1,0:T(8,128)(2,1)S(1)}, u32[]{:S(2)}) copy-start(bf16[160,2560]{1,0:T(8,128)(2,1)S(1)} %collective-permute-done.9.refs_23_) | copy-start | bytes 2457604
  80.2 21.8 %collective-permute-start.10 = (bf16[160,2560]{1,0:T(8,128)(2,1)}, bf16[160,2560]{1,0:T(8,128)(2,1)}, u32[]{:S(2)}, u32[]{:S(2)}) collective-permute-start(bf16[160,2560]{1,0:T(8,128)(2,1)} %collective-permute-done.2.refs_16_), channel_id=1, source_target_pairs={{0,1},{1,0},{2,3},{3,2},{4,5},{5,4},{6,7},{7,6},{8,9},{9,8},{10,11... | collective-permute-start | bytes 2457608 | tf_op jit(solution)/shard_map/ppermute | solution.py:100
  80.7 21.3 %collective-permute-start.12 = (bf16[160,2560]{1,0:T(8,128)(2,1)}, bf16[160,2560]{1,0:T(8,128)(2,1)}, u32[]{:S(2)}, u32[]{:S(2)}) collective-permute-start(bf16[160,2560]{1,0:T(8,128)(2,1)} %collective-permute-done.4.refs_18_), channel_id=1, source_target_pairs={{0,1},{1,0},{2,3},{3,2},{4,5},{5,4},{6,7},{7,6},{8,9},{9,8},{10,11... | collective-permute-start | bytes 2457608 | tf_op jit(solution)/shard_map/ppermute | solution.py:100
  91.3 10.6 %collective-permute-start.13 = (bf16[160,2560]{1,0:T(8,128)(2,1)}, bf16[160,2560]{1,0:T(8,128)(2,1)}, u32[]{:S(2)}, u32[]{:S(2)}) collective-permute-start(bf16[160,2560]{1,0:T(8,128)(2,1)} %collective-permute-done.5.refs_19_), channel_id=1, source_target_pairs={{0,1},{1,0},{2,3},{3,2},{4,5},{5,4},{6,7},{7,6},{8,9},{9,8},{10,11... | collective-permute-start | bytes 2457608 | tf_op jit(solution)/shard_map/ppermute | solution.py:100
  93.2 8.8 %collective-permute-start.14 = (bf16[160,2560]{1,0:T(8,128)(2,1)}, bf16[160,2560]{1,0:T(8,128)(2,1)}, u32[]{:S(2)}, u32[]{:S(2)}) collective-permute-start(bf16[160,2560]{1,0:T(8,128)(2,1)} %collective-permute-done.6.refs_20_), channel_id=1, source_target_pairs={{0,1},{1,0},{2,3},{3,2},{4,5},{5,4},{6,7},{7,6},{8,9},{9,8},{10,11... | collective-permute-start | bytes 2457608 | tf_op jit(solution)/shard_map/ppermute | solution.py:100
  120.3 13.8 %collective-permute-start.15 = (bf16[64,2560]{1,0:T(8,128)(2,1)}, bf16[64,2560]{1,0:T(8,128)(2,1)S(1)}, u32[]{:S(2)}, u32[]{:S(2)}) collective-permute-start(bf16[64,2560]{1,0:T(8,128)(2,1)} %get-tuple-element.53), channel_id=1, source_target_pairs={{16,0},{17,1},{18,2},{19,3},{20,4},{21,5},{22,6},{23,7},{24,8},{25... | collective-permute-start | bytes 983048 | tf_op jit(solution)/shard_map/ppermute | solution.py:471
  132.8 12.3 %collective-permute-start.16 = (bf16[64,2560]{1,0:T(8,128)(2,1)}, bf16[64,2560]{1,0:T(8,128)(2,1)S(1)}, u32[]{:S(2)}, u32[]{:S(2)}) collective-permute-start(bf16[64,2560]{1,0:T(8,128)(2,1)} %get-tuple-element.58), channel_id=1, source_target_pairs={{16,0},{17,1},{18,2},{19,3},{20,4},{21,5},{22,6},{23,7},{24,8},{25... | collective-permute-start | bytes 983048 | tf_op jit(solution)/shard_map/ppermute | solution.py:471
  (2 other events, 8.1 us)

commit v7 on v6

--- a/solution.py
+++ b/solution.py
@@ -72,11 +72,24 @@
     return pltpu.with_memory_space_constraint(value, pltpu.HBM)
 
 
-def weight_pieces(shard, order):
+def places_of(order):
+    count = len(order)
+    if count > 16 or count % 4:
+        return jnp.zeros((1,), jnp.int32)
+    chips = count // 2
+    table = jnp.array([order.index(i) for i in range(count)], jnp.int32)
+    hops = [0]
+    for hop in range(1, chips // 2 + 1):
+        hops += [-hop, hop] if hop <= (chips - 1) // 2 else [-hop]
+    own = (table[lax.axis_index("dp")] + 2 * jnp.array(hops, jnp.int32)) % count
+    return jnp.concatenate([own, own ^ 1])
+
+
+def weight_pieces(shard, order, early, small, make_late):
     count = len(order)
     if count > 16 or count % 4:
         whole = lax.all_gather(shard, "dp", axis=0, tiled=True, axis_index_groups=[order])
-        return [whole], jnp.zeros((1,), jnp.int32)
+        return [whole], early, make_late(small)
     chips = count // 2
     ahead = [
         (order[2 * k + core], order[2 * ((k + 1) % chips) + core])
@@ -85,21 +98,23 @@
     ]
     behind = [(to, source) for source, to in ahead]
     pair = [(i, i ^ 1) for i in range(count)]
-    table = jnp.array([order.index(i) for i in range(count)], jnp.int32)
-    me = table[lax.axis_index("dp")]
-    pieces, places = [shard], [me]
+    pieces = [shard]
     forward = backward = shard
     for hop in range(1, chips // 2 + 1):
+        if hop == 2:
+            forward, backward, early = lax.optimization_barrier((forward, backward, early))
+        if hop == chips // 2 - 1:
+            forward, backward, small = lax.optimization_barrier((forward, backward, small))
+            late = make_late(small)
+        if hop == chips // 2:
+            forward, late = lax.optimization_barrier((forward, late))
         forward = lax.ppermute(forward, "dp", ahead)
         pieces.append(forward)
-        places.append((me - 2 * hop) % count)
         if hop <= (chips - 1) // 2:
             backward = lax.ppermute(backward, "dp", behind)
             pieces.append(backward)
-            places.append((me + 2 * hop) % count)
     pieces += [lax.ppermute(piece, "dp", pair) for piece in pieces]
-    places += [place ^ 1 for place in places]
-    return pieces, jnp.stack(places)
+    return pieces, early, late
 
 
 def step_kernel(order, step, steps, chosen, *refs):
@@ -407,18 +422,21 @@
     features = query_weight.shape[2]
     rank = adapter_a.shape[2]
 
-    weight, places = weight_pieces(query_weight[0], order)
     small = gather_small(adapter_a[0], adapter_bt[0], norm_gain[0])
-    factor_bt = small[:, :, rank : 2 * rank].reshape(features, rank)
-    walked = jnp.concatenate([small[i : i + 1] for i in order], axis=0)
-    factor_a = walked[:, :, :rank].reshape(width, rank)
-    gain = walked[:, :, 2 * rank].reshape(1, width).astype(jnp.float32)
-
     rows_in = reordered(layer_inputs[0, 0], order)
     flat = rows_in.reshape(rows, width).astype(jnp.float32)
     reciprocal = lax.rsqrt(jnp.mean(flat * flat, axis=1, keepdims=True) + norm_eps)
-    normed = (flat * reciprocal * gain).astype(jnp.bfloat16)
-    lowrank = dot(normed, factor_a).astype(jnp.bfloat16)
+
+    def make_late(given):
+        small, rows_in, reciprocal = given
+        factor_bt = small[:, :, rank : 2 * rank].reshape(features, rank)
+        walked = jnp.concatenate([small[i : i + 1] for i in order], axis=0)
+        factor_a = walked[:, :, :rank].reshape(width, rank)
+        gain = walked[:, :, 2 * rank].reshape(1, width).astype(jnp.float32)
+        flat = rows_in.reshape(rows, width).astype(jnp.float32)
+        normed = (flat * reciprocal * gain).astype(jnp.bfloat16)
+        lowrank = dot(normed, factor_a).astype(jnp.bfloat16)
+        return normed, lowrank, factor_bt, factor_a, gain
 
     positions = (
         offsets[0][:, None] + jnp.arange(tokens, dtype=jnp.int32)[None, :]
@@ -440,8 +458,12 @@
     kept, arrived, rotated = (), [], None
     micro = jnp.clip(jnp.arange(steps) - 2 * (last - section), 0, micros - 1)
     is_last = jnp.reshape(section == last, 1).astype(jnp.int32)
-    chosen = jnp.concatenate([is_last, micro.astype(jnp.int32), places])
-    bias, cosine, sine, reciprocal = map(by_micro, (bias, cosine, sine, reciprocal))
+    chosen = jnp.concatenate([is_last, micro.astype(jnp.int32), places_of(order)])
+    given = small, rows_in, reciprocal
+    early = (chosen, *map(by_micro, (bias, cosine, sine, reciprocal)))
+    weight, early, late = weight_pieces(query_weight[0], order, early, given, make_late)
+    chosen, bias, cosine, sine, reciprocal = early
+    normed, lowrank, factor_bt, factor_a, gain = late
     staged = [
         top_grad[0],
         normed,

time: 174 us -> 187 us (1.075)
  waiting for transfers between devices: 42.9 us -> 67.3 us
  starting transfers between devices: 22.8 us -> 16.8 us
  between operations: 5.94 us -> 0.91 us
  local copies, waits for them, and re-layouts: 22.9 us -> 20.6 us
  Pallas kernels: 51.9 us -> 53.8 us
    all_to_all x1, waiting for transfers between devices: 0.01 us -> 22.1 us  [gather_small(): return lax.all_to_all(sent, 'dp', split_axis=0, concat_axis=0, tiled=True)]
    ppermute x4, starting transfers between devices: 7.57 us -> 0.75 us  [weight_pieces(): forward = lax.ppermute(forward, 'dp', ahead)]
    concatenate x2 -> x1, local copies, waits for them, and re-layouts: 3.25 us -> 0.48 us  [reordered(): jnp.concatenate([value[..., i * share:(i + 1) * share] for i in order], a...]
    pallas_call x4, Pallas kernels: 51.4 us -> 53.4 us  [backward(): pl.pallas_call(functools.partial(step_kernel, order, step, steps), grid_s...]
    ppermute x8, waiting for transfers between devices: 0.02 us -> 1.94 us  [weight_pieces(): pieces += [lax.ppermute(piece, 'dp', pair) for piece in pieces]]
    ppermute x3, starting transfers between devices: 4.58 us -> 6.45 us  [weight_pieces(): backward = lax.ppermute(backward, 'dp', behind)]
    unnamed x29 -> x37, local copies, waits for them, and re-layouts: 5.76 us -> 5.79 us
  transfers between devices with their start and end apart: 18 -> 18, of which waited for: 5 -> 7; matrix products, arithmetic and copies ran while one was open for 19% -> 16% of each run, Pallas kernels for 13% -> 12%
where the time goes in v7:
time: 187 us; the launch traced here: 186 us
  waiting for transfers between devices  67.3 us (36%)
  Pallas kernels  53.8 us (29%)
  local copies, waits for them, and re-layouts  20.6 us (11%)
  starting transfers between devices  16.8 us (9%)
  blocking collectives  15.6 us (8%)
  other arithmetic  10.2 us (5%)
    pallas_call x4, Pallas kernels, backward(): pl.pallas_call(functools.partial(step_kernel, order, step, steps), grid_s...  53.4 us
    ppermute x4, waiting for transfers between devices, weight_pieces(): forward = lax.ppermute(forward, 'dp', ahead)  33.1 us
    all_to_all x1, waiting for transfers between devices, gather_small(): return lax.all_to_all(sent, 'dp', split_axis=0, concat_axis=0, tiled=True)  22.1 us
    all_to_all x1, blocking collectives, per_device(): got = lax.all_to_all(partial, 'dp', split_axis=0, concat_axis=0, tiled=True)  15.6 us
    ppermute x3, waiting for transfers between devices, weight_pieces(): backward = lax.ppermute(backward, 'dp', behind)  10.2 us
    ppermute x3, starting transfers between devices, weight_pieces(): backward = lax.ppermute(backward, 'dp', behind)  6.45 us
    unnamed x37, local copies, waits for them, and re-layouts  5.79 us
    all_to_all x1, starting transfers between devices, gather_small(): return lax.all_to_all(sent, 'dp', split_axis=0, concat_axis=0, tiled=True)  5.03 us
  transfers between devices with their start and end apart: 18, of which 7 were waited for; matrix products, arithmetic and copies ran while one was open for 16% of the time, Pallas kernels for 12%

profile of v7, /device:TPU:0, one launch (start us, length us, event | category | flops | bytes accessed | tf_op | source)
XLA Modules:
  0.0 186.3 jit_solution(15018358766222944798)
XLA Ops:
  0.7 3.0 %collective-permute-start.1 = (bf16[160,2560]{1,0:T(8,128)(2,1)}, bf16[160,2560]{1,0:T(8,128)(2,1)S(1)}, u32[]{:S(2)}, u32[]{:S(2)}) collective-permute-start(bf16[160,2560]{1,0:T(8,128)(2,1)} %bitcast.38), channel_id=1, source_target_pairs={{4,0},{5,1},{8,4},{9,5},{12,8},{13,9},{14,12},{15,13},{10,14},{11,... | collective-permute-start | bytes 2457608 | tf_op jit(solution)/shard_map/ppermute | solution.py:114
  4.8 1.4 fusion.13
  12.4 9.8 %collective-permute-done.1.refs_15_ = bf16[160,2560]{1,0:T(8,128)(2,1)S(1)} collective-permute-done((bf16[160,2560]{1,0:T(8,128)(2,1)}, bf16[160,2560]{1,0:T(8,128)(2,1)S(1)}, u32[]{:S(2)}, u32[]{:S(2)}) %collective-permute-start.1) | collective-permute-done | bytes 819232 | tf_op jit(solution)/shard_map/ppermute | solution.py:114
  22.2 1.4 collective-permute-done.refs_14_
  24.0 1.6 collective-permute-start.3
  26.5 5.0 %all-to-all-start = ((bf16[16,160,65]{1,2,0:T(8,128)(2,1)}), bf16[16,160,65]{1,2,0:T(8,128)(2,1)}, u32[]{:S(2)}, u32[]{:S(2)}) async-start(bf16[16,160,65]{1,2,0:T(8,128)(2,1)} %broadcast_in_dim.38), calls=%async_computation | async-start | bytes 1179648 | tf_op jit(solution)/shard_map/all_to_all | solution.py:402
  33.1 22.1 %all-to-all-done = bf16[16,160,65]{1,2,0:T(8,128)(2,1)} async-done(((bf16[16,160,65]{1,2,0:T(8,128)(2,1)}), bf16[16,160,65]{1,2,0:T(8,128)(2,1)}, u32[]{:S(2)}, u32[]{:S(2)}) %all-to-all-start) | async-done | bytes 332832 | tf_op jit(solution)/shard_map/all_to_all | solution.py:402
  62.1 1.4 reshape.238.refs_12_
  64.8 1.8 reduce.9
  66.7 1.3 mul.80
  69.2 1.9 %collective-permute-start.5 = (bf16[160,2560]{1,0:T(8,128)(2,1)}, bf16[160,2560]{1,0:T(8,128)(2,1)}, u32[]{:S(2)}, u32[]{:S(2)}) collective-permute-start(bf16[160,2560]{1,0:T(8,128)(2,1)} %collective-permute-done.3.refs_17_), channel_id=1, source_target_pairs={{4,0},{5,1},{8,4},{9,5},{12,8},{13,9},{14,12},{15,13},{10,14},{11,... | collective-permute-start | bytes 2457608 | tf_op jit(solution)/shard_map/ppermute | solution.py:114
  71.1 1.3 multiply_convert_fusion
  72.4 1.7 fusion.1.refs_1_
  76.1 1.1 copy.37
  77.2 12.7 %collective-permute-done.4.refs_18_ = bf16[160,2560]{1,0:T(8,128)(2,1)} collective-permute-done((bf16[160,2560]{1,0:T(8,128)(2,1)S(1)}, bf16[160,2560]{1,0:T(8,128)(2,1)}, u32[]{:S(2)}, u32[]{:S(2)}) %collective-permute-start.4) | collective-permute-done | bytes 819232 | tf_op jit(solution)/shard_map/ppermute | solution.py:111
  91.2 19.0 %collective-permute-done.6.refs_20_ = bf16[160,2560]{1,0:T(8,128)(2,1)} collective-permute-done((bf16[160,2560]{1,0:T(8,128)(2,1)}, bf16[160,2560]{1,0:T(8,128)(2,1)}, u32[]{:S(2)}, u32[]{:S(2)}) %collective-permute-start.6) | collective-permute-done | bytes 819232 | tf_op jit(solution)/shard_map/ppermute | solution.py:111
  111.0 1.9 %collective-permute-done.14.refs_28_ = bf16[160,2560]{1,0:T(8,128)(2,1)} collective-permute-done((bf16[160,2560]{1,0:T(8,128)(2,1)}, bf16[160,2560]{1,0:T(8,128)(2,1)}, u32[]{:S(2)}, u32[]{:S(2)}) %collective-permute-start.14) | collective-permute-done | bytes 819232 | tf_op jit(solution)/shard_map/ppermute | solution.py:116
  112.9 18.9 %first_step.1 = (bf16[4,2560,640]{2,1,0:T(8,128)(2,1)S(1)}, bf16[128,2560]{1,0:T(8,128)(2,1)S(1)}, bf16[64,2560]{1,0:T(8,128)(2,1)}, bf16[2,64,2560]{2,1,0:T(8,1...) custom-call(s32[21]{0:T(128)S(1)} %pad_add_fusion.chosen, ...), custom_call_target="tpu_custom_call" | custom-call | flops 1845493760 | bytes 13107200 | tf_op jit(solution)/shard_map/first_step/pallas_call | solution.py:322
  131.7 1.5 collective-permute-start.15
  133.2 11.5 %step.3 = (bf16[64,2560]{1,0:T(8,128)(2,1)}, bf16[2,64,2560]{2,1,0:T(8,128)(2,1)S(1)}, bf16[2,64,32]{2,1,0:T(8,128)(2,1)S(1)}, bf16[2,64,2560]{2,1,0:T(8,128)(2,1)}, bf16[4,2560,640]{2,1,0:T(8,128)(2,1)S(1)}) custom-call(s32[21]{0:T(128)S(1)} %pad_add_fusion.chosen, ...), custom_call_target="tpu_custom_call", output_to_operand_aliasing={{4}: (14, {}), {1}: (16, {}), {2}: (17, {}), {3}: (18, {})} | custom-call | flops 1845493760 | bytes 13107200 | tf_op jit(solution)/shard_map/step/pallas_call | solution.py:322
  144.7 1.3 collective-permute-start.16
  146.0 11.5 %step.4 = (bf16[64,2560]{1,0:T(8,128)(2,1)}, bf16[2,64,2560]{2,1,0:T(8,128)(2,1)S(1)}, bf16[2,64,32]{2,1,0:T(8,128)(2,1)S(1)}, bf16[2,64,2560]{2,1,0:T(8,128)(2,1)}, bf16[4,2560,640]{2,1,0:T(8,128)(2,1)S(1)}) custom-call(s32[21]{0:T(128)S(1)} %pad_add_fusion.chosen, ...), custom_call_target="tpu_custom_call", output_to_operand_aliasing={{4}: (14, {}), {1}: (17, {}), {2}: (18, {}), {3}: (19, {})} | custom-call | flops 1845493760 | bytes 13107200 | tf_op jit(solution)/shard_map/step/pallas_call | solution.py:322
  157.5 11.5 %step.5 = (bf16[64,2560]{1,0:T(8,128)(2,1)}, bf16[2,64,2560]{2,1,0:T(8,128)(2,1)S(1)}, bf16[2,64,32]{2,1,0:T(8,128)(2,1)S(1)}, bf16[2,64,2560]{2,1,0:T(8,128)(2,1)}, bf16[4,2560,640]{2,1,0:T(8,128)(2,1)S(1)}) custom-call(s32[21]{0:T(128)S(1)} %pad_add_fusion.chosen, ...), custom_call_target="tpu_custom_call", output_to_operand_aliasing={{4}: (14, {}), {1}: (17, {}), {2}: (18, {}), {3}: (19, {})} | custom-call | flops 1845493760 | bytes 13107200 | tf_op jit(solution)/shard_map/step/pallas_call | solution.py:322
  169.5 15.6 %all_to_all.10 = bf16[16,80,128]{2,1,0:T(8,128)(2,1)S(1)} all-to-all(bf16[16,80,128]{2,1,0:T(8,128)(2,1)S(1)} %gradients.1), channel_id=1, replica_groups=mesh['pipe'=2,'dp'=16] {'dp'}, dimensions={0} | all-to-all | bytes 655360 | tf_op jit(solution)/shard_map/all_to_all | solution.py:498
  (98 shorter events, 25.2 us)
Async XLA Ops:
  0.6 7.4 %copy-start.10 = (s32[8]{0:T(128)S(1)}, s32[8]{0:T(128)}, u32[]{:S(2)}) copy-start(s32[8]{0:T(128)} %constant.76) | copy-start | bytes 100
  0.7 21.5 %collective-permute-start.1 = (bf16[160,2560]{1,0:T(8,128)(2,1)}, bf16[160,2560]{1,0:T(8,128)(2,1)S(1)}, u32[]{:S(2)}, u32[]{:S(2)}) collective-permute-start(bf16[160,2560]{1,0:T(8,128)(2,1)} %bitcast.38), channel_id=1, source_target_pairs={{4,0},{5,1},{8,4},{9,5},{12,8},{13,9},{14,12},{15,13},{10,14},{11,... | collective-permute-start | bytes 2457608 | tf_op jit(solution)/shard_map/ppermute | solution.py:114
  3.7 19.9 %collective-permute-start = (bf16[160,2560]{1,0:T(8,128)(2,1)}, bf16[160,2560]{1,0:T(8,128)(2,1)S(1)}, u32[]{:S(2)}, u32[]{:S(2)}) collective-permute-start(bf16[160,2560]{1,0:T(8,128)(2,1)} %bitcast.39), channel_id=1, source_target_pairs={{0,4},{1,5},{4,8},{5,9},{8,12},{9,13},{12,14},{13,15},{14,10},{15,... | collective-permute-start | bytes 2457608 | tf_op jit(solution)/shard_map/ppermute | solution.py:111
  9.1 16.6 %copy-start.5 = (bf16[1,160,32]{1,2,0:T(8,128)(2,1)S(1)}, bf16[1,160,32]{1,2,0:T(8,128)(2,1)}, u32[]{:S(2)}) copy-start(bf16[1,160,32]{1,2,0:T(8,128)(2,1)} %param.18) | copy-start | bytes 30724
  9.1 16.5 %copy-start.6 = (bf16[1,160,32]{1,2,0:T(8,128)(2,1)S(1)}, bf16[1,160,32]{1,2,0:T(8,128)(2,1)}, u32[]{:S(2)}) copy-start(bf16[1,160,32]{1,2,0:T(8,128)(2,1)} %param.17) | copy-start | bytes 30724
  9.1 16.5 %copy-start.8 = (bf16[1,160]{1,0:T(2,128)(2,1)S(1)}, bf16[1,160]{1,0:T(2,128)(2,1)}, u32[]{:S(2)}) copy-start(bf16[1,160]{1,0:T(2,128)(2,1)} %param.19) | copy-start | bytes 964
  10.7 20.8 %copy-start = (bf16[1,160,2560]{2,1,0:T(8,128)(2,1)S(1)}, bf16[1,160,2560]{2,1,0:T(8,128)(2,1)}, u32[]{:S(2)}) copy-start(bf16[1,160,2560]{2,1,0:T(8,128)(2,1)} %param.16) | copy-start | bytes 2457604
  23.6 31.6 %collective-permute-start.2 = (bf16[160,2560]{1,0:T(8,128)(2,1)S(1)}, bf16[160,2560]{1,0:T(8,128)(2,1)S(1)}, u32[]{:S(2)}, u32[]{:S(2)}) collective-permute-start(bf16[160,2560]{1,0:T(8,128)(2,1)S(1)} %collective-permute-done.refs_14_), channel_id=1, source_target_pairs={{0,4},{1,5},{4,8},{5,9},{8,12},{9,13},{12,14},{13,15},{14,10},{15,... | collective-permute-start | bytes 2457608 | tf_op jit(solution)/shard_map/ppermute | solution.py:111
  24.0 31.2 %collective-permute-start.3 = (bf16[160,2560]{1,0:T(8,128)(2,1)S(1)}, bf16[160,2560]{1,0:T(8,128)(2,1)}, u32[]{:S(2)}, u32[]{:S(2)}) collective-permute-start(bf16[160,2560]{1,0:T(8,128)(2,1)S(1)} %collective-permute-done.1.refs_15_), channel_id=1, source_target_pairs={{4,0},{5,1},{8,4},{9,5},{12,8},{13,9},{14,12},{15,13},{10,14},{11,... | collective-permute-start | bytes 2457608 | tf_op jit(solution)/shard_map/ppermute | solution.py:114
  26.5 28.7 %all-to-all-start = ((bf16[16,160,65]{1,2,0:T(8,128)(2,1)}), bf16[16,160,65]{1,2,0:T(8,128)(2,1)}, u32[]{:S(2)}, u32[]{:S(2)}) async-start(bf16[16,160,65]{1,2,0:T(8,128)(2,1)} %broadcast_in_dim.38), calls=%async_computation | async-start | bytes 1179648 | tf_op jit(solution)/shard_map/all_to_all | solution.py:402
  31.5 58.4 %collective-permute-start.7 = (bf16[160,2560]{1,0:T(8,128)(2,1)S(1)}, bf16[160,2560]{1,0:T(8,128)(2,1)}, u32[]{:S(2)}, u32[]{:S(2)}) collective-permute-start(bf16[160,2560]{1,0:T(8,128)(2,1)S(1)} %bitcast.40), channel_id=1, source_target_pairs={{0,1},{1,0},{2,3},{3,2},{4,5},{5,4},{6,7},{7,6},{8,9},{9,8},{10,11... | collective-permute-start | bytes 2457608 | tf_op jit(solution)/shard_map/ppermute | solution.py:116
  32.6 57.7 %collective-permute-start.9 = (bf16[160,2560]{1,0:T(8,128)(2,1)S(1)}, bf16[160,2560]{1,0:T(8,128)(2,1)}, u32[]{:S(2)}, u32[]{:S(2)}) collective-permute-start(bf16[160,2560]{1,0:T(8,128)(2,1)S(1)} %collective-permute-done.1.refs_15_), channel_id=1, source_target_pairs={{0,1},{1,0},{2,3},{3,2},{4,5},{5,4},{6,7},{7,6},{8,9},{9,8},{10,11... | collective-permute-start | bytes 2457608 | tf_op jit(solution)/shard_map/ppermute | solution.py:116
  32.8 57.7 %collective-permute-start.8 = (bf16[160,2560]{1,0:T(8,128)(2,1)S(1)}, bf16[160,2560]{1,0:T(8,128)(2,1)}, u32[]{:S(2)}, u32[]{:S(2)}) collective-permute-start(bf16[160,2560]{1,0:T(8,128)(2,1)S(1)} %collective-permute-done.refs_14_), channel_id=1, source_target_pairs={{0,1},{1,0},{2,3},{3,2},{4,5},{5,4},{6,7},{7,6},{8,9},{9,8},{10,11... | collective-permute-start | bytes 2457608 | tf_op jit(solution)/shard_map/ppermute | solution.py:116
  69.1 20.8 %collective-permute-start.4 = (bf16[160,2560]{1,0:T(8,128)(2,1)S(1)}, bf16[160,2560]{1,0:T(8,128)(2,1)}, u32[]{:S(2)}, u32[]{:S(2)}) collective-permute-start(bf16[160,2560]{1,0:T(8,128)(2,1)S(1)} %collective-permute-done.2.refs_16_), channel_id=1, source_target_pairs={{0,4},{1,5},{4,8},{5,9},{8,12},{9,13},{12,14},{13,15},{14,10},{15,... | collective-permute-start | bytes 2457608 | tf_op jit(solution)/shard_map/ppermute | solution.py:111
  69.2 22.0 %collective-permute-start.5 = (bf16[160,2560]{1,0:T(8,128)(2,1)}, bf16[160,2560]{1,0:T(8,128)(2,1)}, u32[]{:S(2)}, u32[]{:S(2)}) collective-permute-start(bf16[160,2560]{1,0:T(8,128)(2,1)} %collective-permute-done.3.refs_17_), channel_id=1, source_target_pairs={{4,0},{5,1},{8,4},{9,5},{12,8},{13,9},{14,12},{15,13},{10,14},{11,... | collective-permute-start | bytes 2457608 | tf_op jit(solution)/shard_map/ppermute | solution.py:114
  74.2 36.0 %copy-start.7 = (f32[2,64,1]{1,0,2:T(2,128)S(1)}, f32[2,64,1]{1,0,2:T(2,128)}, u32[]{:S(2)}) copy-start(f32[2,64,1]{1,0,2:T(2,128)} %get-tuple-element.66) | copy-start | bytes 1540
  89.9 20.3 %collective-permute-start.6 = (bf16[160,2560]{1,0:T(8,128)(2,1)}, bf16[160,2560]{1,0:T(8,128)(2,1)}, u32[]{:S(2)}, u32[]{:S(2)}) collective-permute-start(bf16[160,2560]{1,0:T(8,128)(2,1)} %collective-permute-done.4.refs_18_), channel_id=1, source_target_pairs={{0,4},{1,5},{4,8},{5,9},{8,12},{9,13},{12,14},{13,15},{14,10},{15,... | collective-permute-start | bytes 2457608 | tf_op jit(solution)/shard_map/ppermute | solution.py:111
  89.9 21.0 %collective-permute-start.10 = (bf16[160,2560]{1,0:T(8,128)(2,1)S(1)}, bf16[160,2560]{1,0:T(8,128)(2,1)}, u32[]{:S(2)}, u32[]{:S(2)}) collective-permute-start(bf16[160,2560]{1,0:T(8,128)(2,1)S(1)} %collective-permute-done.2.refs_16_), channel_id=1, source_target_pairs={{0,1},{1,0},{2,3},{3,2},{4,5},{5,4},{6,7},{7,6},{8,9},{9,8},{10,11... | collective-permute-start | bytes 2457608 | tf_op jit(solution)/shard_map/ppermute | solution.py:116
  90.3 20.6 %collective-permute-start.11 = (bf16[160,2560]{1,0:T(8,128)(2,1)}, bf16[160,2560]{1,0:T(8,128)(2,1)}, u32[]{:S(2)}, u32[]{:S(2)}) collective-permute-start(bf16[160,2560]{1,0:T(8,128)(2,1)} %collective-permute-done.3.refs_17_), channel_id=1, source_target_pairs={{0,1},{1,0},{2,3},{3,2},{4,5},{5,4},{6,7},{7,6},{8,9},{9,8},{10,11... | collective-permute-start | bytes 2457608 | tf_op jit(solution)/shard_map/ppermute | solution.py:116
  90.4 20.5 %collective-permute-start.12 = (bf16[160,2560]{1,0:T(8,128)(2,1)}, bf16[160,2560]{1,0:T(8,128)(2,1)}, u32[]{:S(2)}, u32[]{:S(2)}) collective-permute-start(bf16[160,2560]{1,0:T(8,128)(2,1)} %collective-permute-done.4.refs_18_), channel_id=1, source_target_pairs={{0,1},{1,0},{2,3},{3,2},{4,5},{5,4},{6,7},{7,6},{8,9},{9,8},{10,11... | collective-permute-start | bytes 2457608 | tf_op jit(solution)/shard_map/ppermute | solution.py:116
  91.2 19.7 %collective-permute-start.13 = (bf16[160,2560]{1,0:T(8,128)(2,1)}, bf16[160,2560]{1,0:T(8,128)(2,1)}, u32[]{:S(2)}, u32[]{:S(2)}) collective-permute-start(bf16[160,2560]{1,0:T(8,128)(2,1)} %collective-permute-done.5.refs_19_), channel_id=1, source_target_pairs={{0,1},{1,0},{2,3},{3,2},{4,5},{5,4},{6,7},{7,6},{8,9},{9,8},{10,11... | collective-permute-start | bytes 2457608 | tf_op jit(solution)/shard_map/ppermute | solution.py:116
  110.2 2.7 %collective-permute-start.14 = (bf16[160,2560]{1,0:T(8,128)(2,1)}, bf16[160,2560]{1,0:T(8,128)(2,1)}, u32[]{:S(2)}, u32[]{:S(2)}) collective-permute-start(bf16[160,2560]{1,0:T(8,128)(2,1)} %collective-permute-done.6.refs_20_), channel_id=1, source_target_pairs={{0,1},{1,0},{2,3},{3,2},{4,5},{5,4},{6,7},{7,6},{8,9},{9,8},{10,11... | collective-permute-start | bytes 2457608 | tf_op jit(solution)/shard_map/ppermute | solution.py:116
  131.7 14.3 %collective-permute-start.15 = (bf16[64,2560]{1,0:T(8,128)(2,1)}, bf16[64,2560]{1,0:T(8,128)(2,1)S(1)}, u32[]{:S(2)}, u32[]{:S(2)}) collective-permute-start(bf16[64,2560]{1,0:T(8,128)(2,1)} %get-tuple-element.89), channel_id=1, source_target_pairs={{16,0},{17,1},{18,2},{19,3},{20,4},{21,5},{22,6},{23,7},{24,8},{25... | collective-permute-start | bytes 983048 | tf_op jit(solution)/shard_map/ppermute | solution.py:493
  144.7 12.8 %collective-permute-start.16 = (bf16[64,2560]{1,0:T(8,128)(2,1)}, bf16[64,2560]{1,0:T(8,128)(2,1)S(1)}, u32[]{:S(2)}, u32[]{:S(2)}) collective-permute-start(bf16[64,2560]{1,0:T(8,128)(2,1)} %get-tuple-element.94), channel_id=1, source_target_pairs={{16,0},{17,1},{18,2},{19,3},{20,4},{21,5},{22,6},{23,7},{24,8},{25... | collective-permute-start | bytes 983048 | tf_op jit(solution)/shard_map/ppermute | solution.py:493
  (6 other events, 27.4 us)

commit v8 on v7

--- a/solution.py
+++ b/solution.py
@@ -66,6 +66,7 @@
 NEEDED_FIRST = (1, 2, 8, 6, 7)
 NEEDED_NEXT = (0, 3, 4, 5)
 NEEDED_LAST = (9, 10, 11, 12)
+OF_FEATURES = 8
 
 
 def in_hbm(value):
@@ -74,7 +75,7 @@
 
 def places_of(order):
     count = len(order)
-    if count > 16 or count % 4:
+    if count != 16:
         return jnp.zeros((1,), jnp.int32)
     chips = count // 2
     table = jnp.array([order.index(i) for i in range(count)], jnp.int32)
@@ -87,7 +88,7 @@
 
 def weight_pieces(shard, order, early, small, make_late):
     count = len(order)
-    if count > 16 or count % 4:
+    if count != 16:
         whole = lax.all_gather(shard, "dp", axis=0, tiled=True, axis_index_groups=[order])
         return [whole], early, make_late(small)
     chips = count // 2
@@ -102,12 +103,11 @@
     forward = backward = shard
     for hop in range(1, chips // 2 + 1):
         if hop == 2:
-            forward, backward, early = lax.optimization_barrier((forward, backward, early))
-        if hop == chips // 2 - 1:
-            forward, backward, small = lax.optimization_barrier((forward, backward, small))
+            tied = (forward, backward, early, small)
+            forward, backward, early, small = lax.optimization_barrier(tied)
             late = make_late(small)
-        if hop == chips // 2:
-            forward, late = lax.optimization_barrier((forward, late))
+        if hop == 3:
+            forward, backward, late = lax.optimization_barrier((forward, backward, late))
         forward = lax.ppermute(forward, "dp", ahead)
         pieces.append(forward)
         if hop <= (chips - 1) // 2:
@@ -128,8 +128,21 @@
         staged = refs[-19:-6]
         sems, stage_sems = refs[-2:]
         upstream, dq, total, middle_sum = refs[-6:-2]
-        stage = lambda i: pltpu.make_async_copy(given[i], staged[i], stage_sems.at[i])
         arrays = staged
+
+        def stage(i):
+            if i != OF_FEATURES:
+                return [pltpu.make_async_copy(given[i], staged[i], stage_sems.at[i])]
+            share = given[i].shape[0] // len(order)
+            return [
+                pltpu.make_async_copy(
+                    given[i].at[k * share : (k + 1) * share],
+                    staged[i].at[to * share : (to + 1) * share],
+                    stage_sems.at[len(given) + k],
+                )
+                for k, to in enumerate(order)
+            ]
+
     else:
         held = refs[13]
         rotated = refs[14 + (step >= 2)]
@@ -163,17 +176,21 @@
     def _():
         if first:
             for i in NEEDED_FIRST:
-                stage(i).start()
+                for copy in stage(i):
+                    copy.start()
             for copy in fetch(0):
                 copy.start()
             for i in NEEDED_NEXT:
-                stage(i).start()
+                for copy in stage(i):
+                    copy.start()
             for copy in fetch(1):
                 copy.start()
             for i in NEEDED_LAST:
-                stage(i).start()
+                for copy in stage(i):
+                    copy.start()
             for i in NEEDED_FIRST:
-                stage(i).wait()
+                for copy in stage(i):
+                    copy.wait()
         total[...] = jnp.zeros_like(total)
         middle_sum[...] = jnp.zeros_like(middle_sum)
         if first:
@@ -231,7 +248,8 @@
                 copy.wait()
             project()
             for i in NEEDED_NEXT:
-                stage(i).wait()
+                for copy in stage(i):
+                    copy.wait()
             upstream[...] = own[micro]
         attend()
 
@@ -254,7 +272,8 @@
     def _():
         if first:
             for i in NEEDED_LAST:
-                stage(i).wait()
+                for copy in stage(i):
+                    copy.wait()
         for piece in range(GROUP):
             pull_back(piece, dq[...])
         mid = middle_sum[...].astype(jnp.bfloat16)
@@ -313,7 +332,7 @@
         ]
         outs += [(pltpu.VMEM(a.shape, a.dtype), in_vmem) for a in staged]
         scratch.append(pltpu.SemaphoreType.DMA((KV_HEADS, len(weight))))
-        scratch.append(pltpu.SemaphoreType.DMA((len(staged),)))
+        scratch.append(pltpu.SemaphoreType.DMA((len(staged) + len(order),)))
         aliases = {}
     else:
         outs.append((pltpu.VMEM((KV_HEADS, width, block), jnp.bfloat16), in_vmem))
@@ -395,11 +414,13 @@
     return jnp.concatenate([total[: 2 * rank], jnp.concatenate(parts, axis=0)], axis=1)
 
 
-def gather_small(adapter_a, adapter_bt, norm_gain):
+def gather_small(adapter_a, adapter_bt, norm_gain, order):
     count = lax.axis_size("dp")
     packed = jnp.concatenate([adapter_a, adapter_bt, norm_gain[:, None]], axis=1)
     sent = jnp.broadcast_to(packed[None], (count, *packed.shape))
-    return lax.all_to_all(sent, "dp", split_axis=0, concat_axis=0, tiled=True)
+    return lax.all_to_all(
+        sent, "dp", split_axis=0, concat_axis=0, tiled=True, axis_index_groups=[order]
+    )
 
 
 def per_device(
@@ -422,7 +443,7 @@
     features = query_weight.shape[2]
     rank = adapter_a.shape[2]
 
-    small = gather_small(adapter_a[0], adapter_bt[0], norm_gain[0])
+    small = gather_small(adapter_a[0], adapter_bt[0], norm_gain[0], order)
     rows_in = reordered(layer_inputs[0, 0], order)
     flat = rows_in.reshape(rows, width).astype(jnp.float32)
     reciprocal = lax.rsqrt(jnp.mean(flat * flat, axis=1, keepdims=True) + norm_eps)
@@ -430,9 +451,8 @@
     def make_late(given):
         small, rows_in, reciprocal = given
         factor_bt = small[:, :, rank : 2 * rank].reshape(features, rank)
-        walked = jnp.concatenate([small[i : i + 1] for i in order], axis=0)
-        factor_a = walked[:, :, :rank].reshape(width, rank)
-        gain = walked[:, :, 2 * rank].reshape(1, width).astype(jnp.float32)
+        factor_a = small[:, :, :rank].reshape(width, rank)
+        gain = small[:, :, 2 * rank].reshape(1, width).astype(jnp.float32)
         flat = rows_in.reshape(rows, width).astype(jnp.float32)
         normed = (flat * reciprocal * gain).astype(jnp.bfloat16)
         lowrank = dot(normed, factor_a).astype(jnp.bfloat16)

time: 187 us -> 180 us (0.963)
  waiting for transfers between devices: 67.3 us -> 64.3 us
    ppermute x4, waiting for transfers between devices: 33.1 us -> 45.5 us  [weight_pieces(): forward = lax.ppermute(forward, 'dp', ahead)]
    all_to_all x1, waiting for transfers between devices: 22.1 us -> 14.6 us  [gather_small(): lax.all_to_all(sent, 'dp', split_axis=0, concat_axis=0, tiled=True, axis_...]
    ppermute x3, waiting for transfers between devices: 10.2 us -> 2.91 us  [weight_pieces(): backward = lax.ppermute(backward, 'dp', behind)]
    ppermute x4, starting transfers between devices: 0.75 us -> 3.68 us  [weight_pieces(): forward = lax.ppermute(forward, 'dp', ahead)]
    ppermute x3, starting transfers between devices: 6.45 us -> 3.94 us  [weight_pieces(): backward = lax.ppermute(backward, 'dp', behind)]
    unnamed x37 -> x39, local copies, waits for them, and re-layouts: 5.79 us -> 6.68 us
  transfers between devices with their start and end apart: 18 -> 18, of which waited for: 7 -> 6; matrix products, arithmetic and copies ran while one was open for 16% -> 9% of each run, Pallas kernels for 12% -> 13%
where the time goes in v8:
time: 180 us
  waiting for transfers between devices  64.3 us (36%)
  Pallas kernels  54 us (30%)
  local copies, waits for them, and re-layouts  19 us (11%)
  starting transfers between devices  18.3 us (10%)
  blocking collectives  13.9 us (8%)
  other arithmetic  8.44 us (5%)
    pallas_call x4, Pallas kernels, backward(): pl.pallas_call(functools.partial(step_kernel, order, step, steps), grid_s...  53.5 us
    ppermute x4, waiting for transfers between devices, weight_pieces(): forward = lax.ppermute(forward, 'dp', ahead)  45.5 us
    all_to_all x1, waiting for transfers between devices, gather_small(): lax.all_to_all(sent, 'dp', split_axis=0, concat_axis=0, tiled=True, axis_...  14.6 us
    all_to_all x1, blocking collectives, per_device(): got = lax.all_to_all(partial, 'dp', split_axis=0, concat_axis=0, tiled=True)  13.9 us
    unnamed x39, local copies, waits for them, and re-layouts  6.68 us
    all_to_all x1, starting transfers between devices, gather_small(): lax.all_to_all(sent, 'dp', split_axis=0, concat_axis=0, tiled=True, axis_...  6.42 us
    ppermute x3, starting transfers between devices, weight_pieces(): backward = lax.ppermute(backward, 'dp', behind)  3.94 us
    ppermute x4, starting transfers between devices, weight_pieces(): forward = lax.ppermute(forward, 'dp', ahead)  3.68 us
  transfers between devices with their start and end apart: 18, of which 6 were waited for; matrix products, arithmetic and copies ran while one was open for 9% of the time, Pallas kernels for 13%

profile of v8, /device:TPU:0, one launch (start us, length us, event | category | flops | bytes accessed | tf_op | source)
XLA Modules:
  0.0 179.8 jit_solution(15591760551545191347)
XLA Ops:
  0.6 3.0 %collective-permute-start.1 = (bf16[160,2560]{1,0:T(8,128)(2,1)}, bf16[160,2560]{1,0:T(8,128)(2,1)S(1)}, u32[]{:S(2)}, u32[]{:S(2)}) collective-permute-start(bf16[160,2560]{1,0:T(8,128)(2,1)} %bitcast.38), channel_id=1, source_target_pairs={{4,0},{5,1},{8,4},{9,5},{12,8},{13,9},{14,12},{15,13},{10,14},{11,... | collective-permute-start | bytes 2457608 | tf_op jit(solution)/shard_map/ppermute | solution.py:114
  5.4 6.4 %all-to-all-start = ((bf16[16,160,65]{1,2,0:T(8,128)(2,1)}), bf16[16,160,65]{1,2,0:T(8,128)(2,1)S(1)}, u32[]{:S(2)}, u32[]{:S(2)}) async-start(bf16[16,160,65]{1,2,0:T(8,128)(2,1)} %broadcast_in_dim.38), calls=%async_computation | async-start | bytes 1179648 | tf_op jit(solution)/shard_map/all_to_all | solution.py:421
  14.1 1.3 concatenate.26.refs_10_
  19.8 14.6 %all-to-all-done = bf16[16,160,65]{1,2,0:T(8,128)(2,1)S(1)} async-done(((bf16[16,160,65]{1,2,0:T(8,128)(2,1)}), bf16[16,160,65]{1,2,0:T(8,128)(2,1)S(1)}, u32[]{:S(2)}, u32[]{:S(2)}) %all-to-all-start) | async-done | bytes 332832 | tf_op jit(solution)/shard_map/all_to_all | solution.py:421
  36.5 2.1 %copy.35 = bf16[16,160,32]{2,1,0:T(8,128)(2,1)} copy(bf16[16,160,32]{1,2,0:T(8,128)(2,1)} %get-tuple-element.108) | data formatting | bytes 327680 | tf_op jit(solution)/shard_map/slice | solution.py:454
  38.6 2.1 %collective-permute-start.2 = (bf16[160,2560]{1,0:T(8,128)(2,1)S(1)}, bf16[160,2560]{1,0:T(8,128)(2,1)S(1)}, u32[]{:S(2)}, u32[]{:S(2)}) collective-permute-start(bf16[160,2560]{1,0:T(8,128)(2,1)S(1)} %collective-permute-done.refs_14_), channel_id=1, source_target_pairs={{0,4},{1,5},{4,8},{5,9},{8,12},{9,13},{12,14},{13,15},{14,10},{15,... | collective-permute-start | bytes 2457608 | tf_op jit(solution)/shard_map/ppermute | solution.py:111
  41.9 1.5 reshape.238.refs_12_
  44.5 2.2 %fusion.1.refs_1_ = bf16[128,2560]{1,0:T(8,128)(2,1)} fusion(f32[2560]{0:T(1024)S(1)} %reshape.237, f32[128]{0:T(128)} %bitcast.57, bf16[2,64,2560]{2,1,0:T(8,128)(2,1)} %copy-done.8), kind=kLoop, calls=%fused_computation.3 | loop fusion | flops 1310720 | bytes 1321472 | tf_op jit(solution)/shard_map/convert_element_type | solution.py:457
  46.7 12.0 %collective-permute-done.2.refs_16_ = bf16[160,2560]{1,0:T(8,128)(2,1)S(1)} collective-permute-done((bf16[160,2560]{1,0:T(8,128)(2,1)S(1)}, bf16[160,2560]{1,0:T(8,128)(2,1)S(1)}, u32[]{:S(2)}, u32[]{:S(2)}) %collective-permute-start.2) | collective-permute-done | bytes 819232 | tf_op jit(solution)/shard_map/ppermute | solution.py:111
  58.7 2.9 %collective-permute-done.3.refs_17_ = bf16[160,2560]{1,0:T(8,128)(2,1)} collective-permute-done((bf16[160,2560]{1,0:T(8,128)(2,1)S(1)}, bf16[160,2560]{1,0:T(8,128)(2,1)}, u32[]{:S(2)}, u32[]{:S(2)}) %collective-permute-start.3) | collective-permute-done | bytes 819232 | tf_op jit(solution)/shard_map/ppermute | solution.py:114
  64.2 17.9 %collective-permute-done.4.refs_18_ = bf16[160,2560]{1,0:T(8,128)(2,1)} collective-permute-done((bf16[160,2560]{1,0:T(8,128)(2,1)S(1)}, bf16[160,2560]{1,0:T(8,128)(2,1)}, u32[]{:S(2)}, u32[]{:S(2)}) %collective-permute-start.4) | collective-permute-done | bytes 819232 | tf_op jit(solution)/shard_map/ppermute | solution.py:111
  86.2 15.6 %collective-permute-done.6.refs_20_ = bf16[160,2560]{1,0:T(8,128)(2,1)} collective-permute-done((bf16[160,2560]{1,0:T(8,128)(2,1)}, bf16[160,2560]{1,0:T(8,128)(2,1)}, u32[]{:S(2)}, u32[]{:S(2)}) %collective-permute-start.6) | collective-permute-done | bytes 819232 | tf_op jit(solution)/shard_map/ppermute | solution.py:111
  101.9 1.4 copy.38.refs_11_
  103.3 1.3 collective-permute-done.14.refs_28_
  104.5 1.1 copy-done.2
  105.7 1.1 copy-done.4
  106.8 1.1 copy-done.6
  108.0 19.0 %first_step.1 = (bf16[4,2560,640]{2,1,0:T(8,128)(2,1)S(1)}, bf16[128,2560]{1,0:T(8,128)(2,1)S(1)}, bf16[64,2560]{1,0:T(8,128)(2,1)}, bf16[2,64,2560]{2,1,0:T(8,1...) custom-call(s32[21]{0:T(128)S(1)} %pad_add_fusion.chosen, ...), custom_call_target="tpu_custom_call" | custom-call | flops 1845493760 | bytes 13107200 | tf_op jit(solution)/shard_map/first_step/pallas_call | solution.py:341
  127.0 1.5 collective-permute-start.15
  128.5 11.5 %step.3 = (bf16[64,2560]{1,0:T(8,128)(2,1)}, bf16[2,64,2560]{2,1,0:T(8,128)(2,1)S(1)}, bf16[2,64,32]{2,1,0:T(8,128)(2,1)S(1)}, bf16[2,64,2560]{2,1,0:T(8,128)(2,1)}, bf16[4,2560,640]{2,1,0:T(8,128)(2,1)S(1)}) custom-call(s32[21]{0:T(128)S(1)} %pad_add_fusion.chosen, ...), custom_call_target="tpu_custom_call", output_to_operand_aliasing={{4}: (14, {}), {1}: (16, {}), {2}: (17, {}), {3}: (18, {})} | custom-call | flops 1845493760 | bytes 13107200 | tf_op jit(solution)/shard_map/step/pallas_call | solution.py:341
  140.0 1.3 collective-permute-start.16
  141.3 11.5 %step.4 = (bf16[64,2560]{1,0:T(8,128)(2,1)}, bf16[2,64,2560]{2,1,0:T(8,128)(2,1)S(1)}, bf16[2,64,32]{2,1,0:T(8,128)(2,1)S(1)}, bf16[2,64,2560]{2,1,0:T(8,128)(2,1)}, bf16[4,2560,640]{2,1,0:T(8,128)(2,1)S(1)}) custom-call(s32[21]{0:T(128)S(1)} %pad_add_fusion.chosen, ...), custom_call_target="tpu_custom_call", output_to_operand_aliasing={{4}: (14, {}), {1}: (17, {}), {2}: (18, {}), {3}: (19, {})} | custom-call | flops 1845493760 | bytes 13107200 | tf_op jit(solution)/shard_map/step/pallas_call | solution.py:341
  152.8 11.5 %step.5 = (bf16[64,2560]{1,0:T(8,128)(2,1)}, bf16[2,64,2560]{2,1,0:T(8,128)(2,1)S(1)}, bf16[2,64,32]{2,1,0:T(8,128)(2,1)S(1)}, bf16[2,64,2560]{2,1,0:T(8,128)(2,1)}, bf16[4,2560,640]{2,1,0:T(8,128)(2,1)S(1)}) custom-call(s32[21]{0:T(128)S(1)} %pad_add_fusion.chosen, ...), custom_call_target="tpu_custom_call", output_to_operand_aliasing={{4}: (14, {}), {1}: (17, {}), {2}: (18, {}), {3}: (19, {})} | custom-call | flops 1845493760 | bytes 13107200 | tf_op jit(solution)/shard_map/step/pallas_call | solution.py:341
  164.8 13.9 %all_to_all.10 = bf16[16,80,128]{2,1,0:T(8,128)(2,1)S(1)} all-to-all(bf16[16,80,128]{2,1,0:T(8,128)(2,1)S(1)} %gradients.1), channel_id=1, replica_groups=mesh['pipe'=2,'dp'=16] {'dp'}, dimensions={0} | all-to-all | bytes 655360 | tf_op jit(solution)/shard_map/all_to_all | solution.py:518
  (98 shorter events, 21.1 us)
Async XLA Ops:
  0.6 11.2 %copy-start.10 = (bf16[1,1,2,64,2560]{4,3,2,1,0:T(8,128)(2,1)S(1)}, bf16[1,1,2,64,2560]{4,3,2,1,0:T(8,128)(2,1)}, u32[]{:S(2)}) copy-start(bf16[1,1,2,64,2560]{4,3,2,1,0:T(8,128)(2,1)} %param.12) | copy-start | bytes 1966084
  0.6 33.7 %collective-permute-start.1 = (bf16[160,2560]{1,0:T(8,128)(2,1)}, bf16[160,2560]{1,0:T(8,128)(2,1)S(1)}, u32[]{:S(2)}, u32[]{:S(2)}) collective-permute-start(bf16[160,2560]{1,0:T(8,128)(2,1)} %bitcast.38), channel_id=1, source_target_pairs={{4,0},{5,1},{8,4},{9,5},{12,8},{13,9},{14,12},{15,13},{10,14},{11,... | collective-permute-start | bytes 2457608 | tf_op jit(solution)/shard_map/ppermute | solution.py:114
  3.6 30.7 %collective-permute-start = (bf16[160,2560]{1,0:T(8,128)(2,1)}, bf16[160,2560]{1,0:T(8,128)(2,1)S(1)}, u32[]{:S(2)}, u32[]{:S(2)}) collective-permute-start(bf16[160,2560]{1,0:T(8,128)(2,1)} %bitcast.39), channel_id=1, source_target_pairs={{0,4},{1,5},{4,8},{5,9},{8,12},{9,13},{12,14},{13,15},{14,10},{15,... | collective-permute-start | bytes 2457608 | tf_op jit(solution)/shard_map/ppermute | solution.py:111
  5.4 7.3 %copy-start.13 = (s32[1,2]{1,0:T(1,128)S(1)}, s32[1,2]{1,0:T(1,128)}, u32[]{:S(2)}) copy-start(s32[1,2]{1,0:T(1,128)} %param.20) | copy-start | bytes 28
  5.4 7.5 %copy-start.7 = (s32[1,1024]{1,0:T(1,128)S(1)}, s32[1,1024]{1,0:T(1,128)}, u32[]{:S(2)}) copy-start(s32[1,1024]{1,0:T(1,128)} %param.21) | copy-start | bytes 12292
  5.4 29.0 %all-to-all-start = ((bf16[16,160,65]{1,2,0:T(8,128)(2,1)}), bf16[16,160,65]{1,2,0:T(8,128)(2,1)S(1)}, u32[]{:S(2)}, u32[]{:S(2)}) async-start(bf16[16,160,65]{1,2,0:T(8,128)(2,1)} %broadcast_in_dim.38), calls=%async_computation | async-start | bytes 1179648 | tf_op jit(solution)/shard_map/all_to_all | solution.py:421
  15.4 25.4 %copy-start.8 = (bf16[2,64,2560]{2,1,0:T(8,128)(2,1)}, bf16[2,64,2560]{2,1,0:T(8,128)(2,1)S(1)}, u32[]{:S(2)}) copy-start(bf16[2,64,2560]{2,1,0:T(8,128)(2,1)S(1)} %concatenate.26.refs_10_) | copy-start | bytes 1966084
  17.6 18.9 %copy-start.12 = (f32[128,1]{0,1:T(1,128)}, f32[128,1]{0,1:T(1,128)S(1)}, u32[]{:S(2)}) copy-start(f32[128,1]{0,1:T(1,128)S(1)} %rsqrt.26) | copy-start | bytes 1540
  38.6 20.1 %collective-permute-start.2 = (bf16[160,2560]{1,0:T(8,128)(2,1)S(1)}, bf16[160,2560]{1,0:T(8,128)(2,1)S(1)}, u32[]{:S(2)}, u32[]{:S(2)}) collective-permute-start(bf16[160,2560]{1,0:T(8,128)(2,1)S(1)} %collective-permute-done.refs_14_), channel_id=1, source_target_pairs={{0,4},{1,5},{4,8},{5,9},{8,12},{9,13},{12,14},{13,15},{14,10},{15,... | collective-permute-start | bytes 2457608 | tf_op jit(solution)/shard_map/ppermute | solution.py:111
  40.7 20.9 %collective-permute-start.3 = (bf16[160,2560]{1,0:T(8,128)(2,1)S(1)}, bf16[160,2560]{1,0:T(8,128)(2,1)}, u32[]{:S(2)}, u32[]{:S(2)}) collective-permute-start(bf16[160,2560]{1,0:T(8,128)(2,1)S(1)} %collective-permute-done.1.refs_15_), channel_id=1, source_target_pairs={{4,0},{5,1},{8,4},{9,5},{12,8},{13,9},{14,12},{15,13},{10,14},{11,... | collective-permute-start | bytes 2457608 | tf_op jit(solution)/shard_map/ppermute | solution.py:114
  41.9 20.8 %copy-start = (bf16[1,160,2560]{2,1,0:T(8,128)(2,1)S(1)}, bf16[1,160,2560]{2,1,0:T(8,128)(2,1)}, u32[]{:S(2)}) copy-start(bf16[1,160,2560]{2,1,0:T(8,128)(2,1)} %param.16) | copy-start | bytes 2457604
  61.6 20.4 %collective-permute-start.4 = (bf16[160,2560]{1,0:T(8,128)(2,1)S(1)}, bf16[160,2560]{1,0:T(8,128)(2,1)}, u32[]{:S(2)}, u32[]{:S(2)}) collective-permute-start(bf16[160,2560]{1,0:T(8,128)(2,1)S(1)} %collective-permute-done.2.refs_16_), channel_id=1, source_target_pairs={{0,4},{1,5},{4,8},{5,9},{8,12},{9,13},{12,14},{13,15},{14,10},{15,... | collective-permute-start | bytes 2457608 | tf_op jit(solution)/shard_map/ppermute | solution.py:111
  62.7 19.7 %collective-permute-start.7 = (bf16[160,2560]{1,0:T(8,128)(2,1)S(1)}, bf16[160,2560]{1,0:T(8,128)(2,1)S(1)}, u32[]{:S(2)}, u32[]{:S(2)}) collective-permute-start(bf16[160,2560]{1,0:T(8,128)(2,1)S(1)} %bitcast.40), channel_id=1, source_target_pairs={{0,1},{1,0},{2,3},{3,2},{4,5},{5,4},{6,7},{7,6},{8,9},{9,8},{10,11... | collective-permute-start | bytes 2457608 | tf_op jit(solution)/shard_map/ppermute | solution.py:116
  62.7 20.6 %collective-permute-start.9 = (bf16[160,2560]{1,0:T(8,128)(2,1)S(1)}, bf16[160,2560]{1,0:T(8,128)(2,1)S(1)}, u32[]{:S(2)}, u32[]{:S(2)}) collective-permute-start(bf16[160,2560]{1,0:T(8,128)(2,1)S(1)} %collective-permute-done.1.refs_15_), channel_id=1, source_target_pairs={{0,1},{1,0},{2,3},{3,2},{4,5},{5,4},{6,7},{7,6},{8,9},{9,8},{10,11... | collective-permute-start | bytes 2457608 | tf_op jit(solution)/shard_map/ppermute | solution.py:116
  63.2 21.6 %collective-permute-start.8 = (bf16[160,2560]{1,0:T(8,128)(2,1)S(1)}, bf16[160,2560]{1,0:T(8,128)(2,1)S(1)}, u32[]{:S(2)}, u32[]{:S(2)}) collective-permute-start(bf16[160,2560]{1,0:T(8,128)(2,1)S(1)} %collective-permute-done.refs_14_), channel_id=1, source_target_pairs={{0,1},{1,0},{2,3},{3,2},{4,5},{5,4},{6,7},{7,6},{8,9},{9,8},{10,11... | collective-permute-start | bytes 2457608 | tf_op jit(solution)/shard_map/ppermute | solution.py:116
  63.2 22.5 %collective-permute-start.5 = (bf16[160,2560]{1,0:T(8,128)(2,1)}, bf16[160,2560]{1,0:T(8,128)(2,1)}, u32[]{:S(2)}, u32[]{:S(2)}) collective-permute-start(bf16[160,2560]{1,0:T(8,128)(2,1)} %collective-permute-done.3.refs_17_), channel_id=1, source_target_pairs={{4,0},{5,1},{8,4},{9,5},{12,8},{13,9},{14,12},{15,13},{10,14},{11,... | collective-permute-start | bytes 2457608 | tf_op jit(solution)/shard_map/ppermute | solution.py:114
  82.0 19.8 %collective-permute-start.6 = (bf16[160,2560]{1,0:T(8,128)(2,1)}, bf16[160,2560]{1,0:T(8,128)(2,1)}, u32[]{:S(2)}, u32[]{:S(2)}) collective-permute-start(bf16[160,2560]{1,0:T(8,128)(2,1)} %collective-permute-done.4.refs_18_), channel_id=1, source_target_pairs={{0,4},{1,5},{4,8},{5,9},{8,12},{9,13},{12,14},{13,15},{14,10},{15,... | collective-permute-start | bytes 2457608 | tf_op jit(solution)/shard_map/ppermute | solution.py:111
  83.3 19.9 %collective-permute-start.10 = (bf16[160,2560]{1,0:T(8,128)(2,1)S(1)}, bf16[160,2560]{1,0:T(8,128)(2,1)}, u32[]{:S(2)}, u32[]{:S(2)}) collective-permute-start(bf16[160,2560]{1,0:T(8,128)(2,1)S(1)} %collective-permute-done.2.refs_16_), channel_id=1, source_target_pairs={{0,1},{1,0},{2,3},{3,2},{4,5},{5,4},{6,7},{7,6},{8,9},{9,8},{10,11... | collective-permute-start | bytes 2457608 | tf_op jit(solution)/shard_map/ppermute | solution.py:116
  84.3 19.0 %collective-permute-start.11 = (bf16[160,2560]{1,0:T(8,128)(2,1)}, bf16[160,2560]{1,0:T(8,128)(2,1)}, u32[]{:S(2)}, u32[]{:S(2)}) collective-permute-start(bf16[160,2560]{1,0:T(8,128)(2,1)} %collective-permute-done.3.refs_17_), channel_id=1, source_target_pairs={{0,1},{1,0},{2,3},{3,2},{4,5},{5,4},{6,7},{7,6},{8,9},{9,8},{10,11... | collective-permute-start | bytes 2457608 | tf_op jit(solution)/shard_map/ppermute | solution.py:116
  85.7 17.6 %collective-permute-start.12 = (bf16[160,2560]{1,0:T(8,128)(2,1)}, bf16[160,2560]{1,0:T(8,128)(2,1)}, u32[]{:S(2)}, u32[]{:S(2)}) collective-permute-start(bf16[160,2560]{1,0:T(8,128)(2,1)} %collective-permute-done.4.refs_18_), channel_id=1, source_target_pairs={{0,1},{1,0},{2,3},{3,2},{4,5},{5,4},{6,7},{7,6},{8,9},{9,8},{10,11... | collective-permute-start | bytes 2457608 | tf_op jit(solution)/shard_map/ppermute | solution.py:116
  85.7 17.6 %collective-permute-start.13 = (bf16[160,2560]{1,0:T(8,128)(2,1)}, bf16[160,2560]{1,0:T(8,128)(2,1)}, u32[]{:S(2)}, u32[]{:S(2)}) collective-permute-start(bf16[160,2560]{1,0:T(8,128)(2,1)} %collective-permute-done.5.refs_19_), channel_id=1, source_target_pairs={{0,1},{1,0},{2,3},{3,2},{4,5},{5,4},{6,7},{7,6},{8,9},{9,8},{10,11... | collective-permute-start | bytes 2457608 | tf_op jit(solution)/shard_map/ppermute | solution.py:116
  101.9 2.7 %collective-permute-start.14 = (bf16[160,2560]{1,0:T(8,128)(2,1)}, bf16[160,2560]{1,0:T(8,128)(2,1)}, u32[]{:S(2)}, u32[]{:S(2)}) collective-permute-start(bf16[160,2560]{1,0:T(8,128)(2,1)} %collective-permute-done.6.refs_20_), channel_id=1, source_target_pairs={{0,1},{1,0},{2,3},{3,2},{4,5},{5,4},{6,7},{7,6},{8,9},{9,8},{10,11... | collective-permute-start | bytes 2457608 | tf_op jit(solution)/shard_map/ppermute | solution.py:116
  127.0 14.3 %collective-permute-start.15 = (bf16[64,2560]{1,0:T(8,128)(2,1)}, bf16[64,2560]{1,0:T(8,128)(2,1)S(1)}, u32[]{:S(2)}, u32[]{:S(2)}) collective-permute-start(bf16[64,2560]{1,0:T(8,128)(2,1)} %get-tuple-element.87), channel_id=1, source_target_pairs={{16,0},{17,1},{18,2},{19,3},{20,4},{21,5},{22,6},{23,7},{24,8},{25... | collective-permute-start | bytes 983048 | tf_op jit(solution)/shard_map/ppermute | solution.py:513
  140.0 12.8 %collective-permute-start.16 = (bf16[64,2560]{1,0:T(8,128)(2,1)}, bf16[64,2560]{1,0:T(8,128)(2,1)S(1)}, u32[]{:S(2)}, u32[]{:S(2)}) collective-permute-start(bf16[64,2560]{1,0:T(8,128)(2,1)} %get-tuple-element.92), channel_id=1, source_target_pairs={{16,0},{17,1},{18,2},{19,3},{20,4},{21,5},{22,6},{23,7},{24,8},{25... | collective-permute-start | bytes 983048 | tf_op jit(solution)/shard_map/ppermute | solution.py:513
  (10 other events, 22.4 us)

commit v9 on v8

--- a/solution.py
+++ b/solution.py
@@ -103,17 +103,17 @@
     forward = backward = shard
     for hop in range(1, chips // 2 + 1):
         if hop == 2:
-            tied = (forward, backward, early, small)
-            forward, backward, early, small = lax.optimization_barrier(tied)
-            late = make_late(small)
+            forward, backward, early = lax.optimization_barrier((forward, backward, early))
         if hop == 3:
-            forward, backward, late = lax.optimization_barrier((forward, backward, late))
+            late = make_late(lax.optimization_barrier((small, forward))[0])
         forward = lax.ppermute(forward, "dp", ahead)
         pieces.append(forward)
         if hop <= (chips - 1) // 2:
             backward = lax.ppermute(backward, "dp", behind)
             pieces.append(backward)
-    pieces += [lax.ppermute(piece, "dp", pair) for piece in pieces]
+    copied = list(pieces)
+    copied[-2], late = lax.optimization_barrier((copied[-2], late))
+    pieces += [lax.ppermute(piece, "dp", pair) for piece in copied]
     return pieces, early, late
 
 
@@ -301,7 +301,7 @@
     untouched = pl.BlockSpec(memory_space=pl.ANY)
     in_vmem = pl.BlockSpec(memory_space=pltpu.VMEM)
     ins = [(in_hbm(a), untouched) if first else (a, in_vmem) for a in staged]
-    ins += [(piece, untouched) for piece in weight] if first else [(weight, in_vmem)]
+    ins += [(in_hbm(a), untouched) for a in weight] if first else [(weight, in_vmem)]
     if incoming is not None:
         ins.append((incoming, in_vmem))
     if not first:

time: 180 us -> 172 us (0.956)
  local copies, waits for them, and re-layouts: 19 us -> 9.48 us
  waiting for transfers between devices: 64.3 us -> 69.8 us
  other arithmetic: 8.44 us -> 6.02 us
    ppermute x4, waiting for transfers between devices: 45.5 us -> 30.3 us  [weight_pieces(): forward = lax.ppermute(forward, 'dp', ahead)]
    ppermute x3, waiting for transfers between devices: 2.91 us -> 16.2 us  [weight_pieces(): backward = lax.ppermute(backward, 'dp', behind)]
    all_to_all x1, waiting for transfers between devices: 14.6 us -> 21.4 us  [gather_small(): lax.all_to_all(sent, 'dp', split_axis=0, concat_axis=0, tiled=True, axis_...]
    unnamed x39 -> x37, local copies, waits for them, and re-layouts: 6.68 us -> 0.44 us
  transfers between devices with their start and end apart: 18 -> 18, of which waited for: 6 -> 8; matrix products, arithmetic and copies ran while one was open for 9% -> 9% of each run, Pallas kernels for 13% -> 13%
where the time goes in v9:
time: 172 us; the launch traced here: 171 us
  waiting for transfers between devices  69.8 us (41%)
  Pallas kernels  52.6 us (31%)
  starting transfers between devices  17.7 us (10%)
  blocking collectives  13.7 us (8%)
  local copies, waits for them, and re-layouts  9.48 us (6%)
  other arithmetic  6.02 us (4%)
    pallas_call x4, Pallas kernels, backward(): pl.pallas_call(functools.partial(step_kernel, order, step, steps), grid_s...  52.1 us
    ppermute x4, waiting for transfers between devices, weight_pieces(): forward = lax.ppermute(forward, 'dp', ahead)  30.3 us
    all_to_all x1, waiting for transfers between devices, gather_small(): lax.all_to_all(sent, 'dp', split_axis=0, concat_axis=0, tiled=True, axis_...  21.4 us
    ppermute x3, waiting for transfers between devices, weight_pieces(): backward = lax.ppermute(backward, 'dp', behind)  16.2 us
    all_to_all x1, blocking collectives, per_device(): got = lax.all_to_all(partial, 'dp', split_axis=0, concat_axis=0, tiled=True)  13.7 us
    all_to_all x1, starting transfers between devices, gather_small(): lax.all_to_all(sent, 'dp', split_axis=0, concat_axis=0, tiled=True, axis_...  6.01 us
    ppermute x3, starting transfers between devices, weight_pieces(): backward = lax.ppermute(backward, 'dp', behind)  4.93 us
  transfers between devices with their start and end apart: 18, of which 8 were waited for; matrix products, arithmetic and copies ran while one was open for 9% of the time, Pallas kernels for 13%

profile of v9, /device:TPU:0, one launch (start us, length us, event | category | flops | bytes accessed | tf_op | source)
XLA Modules:
  0.0 171.2 jit_solution(16019859044217486347)
XLA Ops:
  0.7 3.0 %collective-permute-start.1 = (bf16[160,2560]{1,0:T(8,128)(2,1)}, bf16[160,2560]{1,0:T(8,128)(2,1)S(1)}, u32[]{:S(2)}, u32[]{:S(2)}) collective-permute-start(bf16[160,2560]{1,0:T(8,128)(2,1)} %bitcast.49), channel_id=1, source_target_pairs={{4,0},{5,1},{8,4},{9,5},{12,8},{13,9},{14,12},{15,13},{10,14},{11,... | collective-permute-start | bytes 2457608 | tf_op jit(solution)/shard_map/ppermute | solution.py:112
  4.8 1.4 fusion.12
  6.4 1.0 gather_fusion
  10.7 1.0 fusion.3.refs_5_
  11.7 10.5 %collective-permute-done.1.refs_15_ = bf16[160,2560]{1,0:T(8,128)(2,1)S(1)} collective-permute-done((bf16[160,2560]{1,0:T(8,128)(2,1)}, bf16[160,2560]{1,0:T(8,128)(2,1)S(1)}, u32[]{:S(2)}, u32[]{:S(2)}) %collective-permute-start.1) | collective-permute-done | bytes 819232 | tf_op jit(solution)/shard_map/ppermute | solution.py:112
  22.2 1.5 collective-permute-done.refs_14_
  25.0 6.0 %all-to-all-start = ((bf16[16,160,65]{1,2,0:T(8,128)(2,1)}), bf16[16,160,65]{1,2,0:T(8,128)(2,1)S(1)}, u32[]{:S(2)}, u32[]{:S(2)}) async-start(bf16[16,160,65]{1,2,0:T(8,128)(2,1)} %broadcast_in_dim.38), calls=%async_computation | async-start | bytes 1179648 | tf_op jit(solution)/shard_map/all_to_all | solution.py:421
  31.0 1.9 %collective-permute-start.2 = (bf16[160,2560]{1,0:T(8,128)(2,1)S(1)}, bf16[160,2560]{1,0:T(8,128)(2,1)}, u32[]{:S(2)}, u32[]{:S(2)}) collective-permute-start(bf16[160,2560]{1,0:T(8,128)(2,1)S(1)} %collective-permute-done.1.refs_15_), channel_id=1, source_target_pairs={{4,0},{5,1},{8,4},{9,5},{12,8},{13,9},{14,12},{15,13},{10,14},{11,... | collective-permute-start | bytes 2457608 | tf_op jit(solution)/shard_map/ppermute | solution.py:112
  33.5 21.4 %all-to-all-done = bf16[16,160,65]{1,2,0:T(8,128)(2,1)S(1)} async-done(((bf16[16,160,65]{1,2,0:T(8,128)(2,1)}), bf16[16,160,65]{1,2,0:T(8,128)(2,1)S(1)}, u32[]{:S(2)}, u32[]{:S(2)}) %all-to-all-start) | async-done | bytes 332832 | tf_op jit(solution)/shard_map/all_to_all | solution.py:421
  56.2 1.0 collective-permute-start.5
  57.7 3.6 %collective-permute-done.2.refs_17_ = bf16[160,2560]{1,0:T(8,128)(2,1)} collective-permute-done((bf16[160,2560]{1,0:T(8,128)(2,1)S(1)}, bf16[160,2560]{1,0:T(8,128)(2,1)}, u32[]{:S(2)}, u32[]{:S(2)}) %collective-permute-start.2) | collective-permute-done | bytes 819232 | tf_op jit(solution)/shard_map/ppermute | solution.py:112
  61.5 15.8 %collective-permute-done.5.refs_18_ = bf16[160,2560]{1,0:T(8,128)(2,1)} collective-permute-done((bf16[160,2560]{1,0:T(8,128)(2,1)}, bf16[160,2560]{1,0:T(8,128)(2,1)}, u32[]{:S(2)}, u32[]{:S(2)}) %collective-permute-start.5) | collective-permute-done | bytes 819232 | tf_op jit(solution)/shard_map/ppermute | solution.py:109
  79.9 1.1 copy.37
  81.0 1.1 fusion.1.refs_1_
  82.1 2.2 %collective-permute-done.3.refs_19_ = bf16[160,2560]{1,0:T(8,128)(2,1)} collective-permute-done((bf16[160,2560]{1,0:T(8,128)(2,1)}, bf16[160,2560]{1,0:T(8,128)(2,1)}, u32[]{:S(2)}, u32[]{:S(2)}) %collective-permute-start.3) | collective-permute-done | bytes 819232 | tf_op jit(solution)/shard_map/ppermute | solution.py:112
  85.3 13.0 %collective-permute-done.6.refs_20_ = bf16[160,2560]{1,0:T(8,128)(2,1)} collective-permute-done((bf16[160,2560]{1,0:T(8,128)(2,1)}, bf16[160,2560]{1,0:T(8,128)(2,1)}, u32[]{:S(2)}, u32[]{:S(2)}) %collective-permute-start.6) | collective-permute-done | bytes 819232 | tf_op jit(solution)/shard_map/ppermute | solution.py:109
  99.1 1.9 %collective-permute-done.14.refs_28_ = bf16[160,2560]{1,0:T(8,128)(2,1)} collective-permute-done((bf16[160,2560]{1,0:T(8,128)(2,1)}, bf16[160,2560]{1,0:T(8,128)(2,1)}, u32[]{:S(2)}, u32[]{:S(2)}) %collective-permute-start.14) | collective-permute-done | bytes 819232 | tf_op jit(solution)/shard_map/ppermute | solution.py:116
  101.0 18.7 %first_step.1 = (bf16[4,2560,640]{2,1,0:T(8,128)(2,1)S(1)}, bf16[128,2560]{1,0:T(8,128)(2,1)S(1)}, bf16[64,2560]{1,0:T(8,128)(2,1)}, bf16[2,64,2560]{2,1,0:T(8,1...) custom-call(s32[21]{0:T(128)S(1)} %pad_add_fusion.chosen, ...), custom_call_target="tpu_custom_call" | custom-call | flops 1845493760 | bytes 13107200 | tf_op jit(solution)/shard_map/first_step/pallas_call | solution.py:341
  119.6 1.5 collective-permute-start.15
  121.1 11.1 %step.3 = (bf16[64,2560]{1,0:T(8,128)(2,1)}, bf16[2,64,2560]{2,1,0:T(8,128)(2,1)S(1)}, bf16[2,64,32]{2,1,0:T(8,128)(2,1)S(1)}, bf16[2,64,2560]{2,1,0:T(8,128)(2,1)}, bf16[4,2560,640]{2,1,0:T(8,128)(2,1)S(1)}) custom-call(s32[21]{0:T(128)S(1)} %pad_add_fusion.chosen, ...), custom_call_target="tpu_custom_call", output_to_operand_aliasing={{4}: (14, {}), {1}: (16, {}), {2}: (17, {}), {3}: (18, {})} | custom-call | flops 1845493760 | bytes 13107200 | tf_op jit(solution)/shard_map/step/pallas_call | solution.py:341
  132.3 1.3 collective-permute-start.16
  133.6 11.1 %step.4 = (bf16[64,2560]{1,0:T(8,128)(2,1)}, bf16[2,64,2560]{2,1,0:T(8,128)(2,1)S(1)}, bf16[2,64,32]{2,1,0:T(8,128)(2,1)S(1)}, bf16[2,64,2560]{2,1,0:T(8,128)(2,1)}, bf16[4,2560,640]{2,1,0:T(8,128)(2,1)S(1)}) custom-call(s32[21]{0:T(128)S(1)} %pad_add_fusion.chosen, ...), custom_call_target="tpu_custom_call", output_to_operand_aliasing={{4}: (14, {}), {1}: (17, {}), {2}: (18, {}), {3}: (19, {})} | custom-call | flops 1845493760 | bytes 13107200 | tf_op jit(solution)/shard_map/step/pallas_call | solution.py:341
  144.7 11.1 %step.5 = (bf16[64,2560]{1,0:T(8,128)(2,1)}, bf16[2,64,2560]{2,1,0:T(8,128)(2,1)S(1)}, bf16[2,64,32]{2,1,0:T(8,128)(2,1)S(1)}, bf16[2,64,2560]{2,1,0:T(8,128)(2,1)}, bf16[4,2560,640]{2,1,0:T(8,128)(2,1)S(1)}) custom-call(s32[21]{0:T(128)S(1)} %pad_add_fusion.chosen, ...), custom_call_target="tpu_custom_call", output_to_operand_aliasing={{4}: (14, {}), {1}: (17, {}), {2}: (18, {}), {3}: (19, {})} | custom-call | flops 1845493760 | bytes 13107200 | tf_op jit(solution)/shard_map/step/pallas_call | solution.py:341
  156.3 13.7 %all_to_all.10 = bf16[16,80,128]{2,1,0:T(8,128)(2,1)S(1)} all-to-all(bf16[16,80,128]{2,1,0:T(8,128)(2,1)S(1)} %gradients.1), channel_id=1, replica_groups=mesh['pipe'=2,'dp'=16] {'dp'}, dimensions={0} | all-to-all | bytes 655360 | tf_op jit(solution)/shard_map/all_to_all | solution.py:518
  (96 shorter events, 14.4 us)
Async XLA Ops:
  0.7 21.5 %collective-permute-start.1 = (bf16[160,2560]{1,0:T(8,128)(2,1)}, bf16[160,2560]{1,0:T(8,128)(2,1)S(1)}, u32[]{:S(2)}, u32[]{:S(2)}) collective-permute-start(bf16[160,2560]{1,0:T(8,128)(2,1)} %bitcast.49), channel_id=1, source_target_pairs={{4,0},{5,1},{8,4},{9,5},{12,8},{13,9},{14,12},{15,13},{10,14},{11,... | collective-permute-start | bytes 2457608 | tf_op jit(solution)/shard_map/ppermute | solution.py:112
  3.7 20.0 %collective-permute-start = (bf16[160,2560]{1,0:T(8,128)(2,1)}, bf16[160,2560]{1,0:T(8,128)(2,1)}, u32[]{:S(2)}, u32[]{:S(2)}) collective-permute-start(bf16[160,2560]{1,0:T(8,128)(2,1)} %bitcast.50), channel_id=1, source_target_pairs={{0,4},{1,5},{4,8},{5,9},{8,12},{9,13},{12,14},{13,15},{14,10},{15,... | collective-permute-start | bytes 2457608 | tf_op jit(solution)/shard_map/ppermute | solution.py:109
  9.1 15.1 %copy-start.9 = (bf16[1,160,32]{1,2,0:T(8,128)(2,1)S(1)}, bf16[1,160,32]{1,2,0:T(8,128)(2,1)}, u32[]{:S(2)}) copy-start(bf16[1,160,32]{1,2,0:T(8,128)(2,1)} %param.18) | copy-start | bytes 30724
  9.1 15.1 %copy-start.10 = (bf16[1,160,32]{1,2,0:T(8,128)(2,1)S(1)}, bf16[1,160,32]{1,2,0:T(8,128)(2,1)}, u32[]{:S(2)}) copy-start(bf16[1,160,32]{1,2,0:T(8,128)(2,1)} %param.17) | copy-start | bytes 30724
  9.6 71.4 %copy-start.1 = (bf16[2,64,2560]{2,1,0:T(8,128)(2,1)}, bf16[2,64,2560]{2,1,0:T(8,128)(2,1)S(1)}, u32[]{:S(2)}) copy-start(bf16[2,64,2560]{2,1,0:T(8,128)(2,1)S(1)} %concatenate.26.refs_10_) | copy-start | bytes 1966084
  10.7 22.3 %copy-start.3 = (bf16[1,160,2560]{2,1,0:T(8,128)(2,1)S(1)}, bf16[1,160,2560]{2,1,0:T(8,128)(2,1)}, u32[]{:S(2)}) copy-start(bf16[1,160,2560]{2,1,0:T(8,128)(2,1)} %param.16) | copy-start | bytes 2457604
  22.2 35.1 %copy-start.4 = (bf16[160,2560]{1,0:T(8,128)(2,1)}, bf16[160,2560]{1,0:T(8,128)(2,1)S(1)}, u32[]{:S(2)}) copy-start(bf16[160,2560]{1,0:T(8,128)(2,1)S(1)} %collective-permute-done.1.refs_15_) | copy-start | bytes 2457604
  23.7 31.3 %collective-permute-start.4 = (bf16[160,2560]{1,0:T(8,128)(2,1)}, bf16[160,2560]{1,0:T(8,128)(2,1)}, u32[]{:S(2)}, u32[]{:S(2)}) collective-permute-start(bf16[160,2560]{1,0:T(8,128)(2,1)} %collective-permute-done.refs_14_), channel_id=1, source_target_pairs={{0,4},{1,5},{4,8},{5,9},{8,12},{9,13},{12,14},{13,15},{14,10},{15,... | collective-permute-start | bytes 2457608 | tf_op jit(solution)/shard_map/ppermute | solution.py:109
  25.0 30.0 %all-to-all-start = ((bf16[16,160,65]{1,2,0:T(8,128)(2,1)}), bf16[16,160,65]{1,2,0:T(8,128)(2,1)S(1)}, u32[]{:S(2)}, u32[]{:S(2)}) async-start(bf16[16,160,65]{1,2,0:T(8,128)(2,1)} %broadcast_in_dim.38), calls=%async_computation | async-start | bytes 1179648 | tf_op jit(solution)/shard_map/all_to_all | solution.py:421
  31.0 30.3 %collective-permute-start.2 = (bf16[160,2560]{1,0:T(8,128)(2,1)S(1)}, bf16[160,2560]{1,0:T(8,128)(2,1)}, u32[]{:S(2)}, u32[]{:S(2)}) collective-permute-start(bf16[160,2560]{1,0:T(8,128)(2,1)S(1)} %collective-permute-done.1.refs_15_), channel_id=1, source_target_pairs={{4,0},{5,1},{8,4},{9,5},{12,8},{13,9},{14,12},{15,13},{10,14},{11,... | collective-permute-start | bytes 2457608 | tf_op jit(solution)/shard_map/ppermute | solution.py:112
  33.0 51.3 %collective-permute-start.7 = (bf16[160,2560]{1,0:T(8,128)(2,1)S(1)}, bf16[160,2560]{1,0:T(8,128)(2,1)}, u32[]{:S(2)}, u32[]{:S(2)}) collective-permute-start(bf16[160,2560]{1,0:T(8,128)(2,1)S(1)} %bitcast.52), channel_id=1, source_target_pairs={{0,1},{1,0},{2,3},{3,2},{4,5},{5,4},{6,7},{7,6},{8,9},{9,8},{10,11... | collective-permute-start | bytes 2457608 | tf_op jit(solution)/shard_map/ppermute | solution.py:116
  33.0 51.7 %collective-permute-start.9 = (bf16[160,2560]{1,0:T(8,128)(2,1)S(1)}, bf16[160,2560]{1,0:T(8,128)(2,1)}, u32[]{:S(2)}, u32[]{:S(2)}) collective-permute-start(bf16[160,2560]{1,0:T(8,128)(2,1)S(1)} %collective-permute-done.1.refs_15_), channel_id=1, source_target_pairs={{0,1},{1,0},{2,3},{3,2},{4,5},{5,4},{6,7},{7,6},{8,9},{9,8},{10,11... | collective-permute-start | bytes 2457608 | tf_op jit(solution)/shard_map/ppermute | solution.py:116
  33.5 51.3 %collective-permute-start.8 = (bf16[160,2560]{1,0:T(8,128)(2,1)}, bf16[160,2560]{1,0:T(8,128)(2,1)}, u32[]{:S(2)}, u32[]{:S(2)}) collective-permute-start(bf16[160,2560]{1,0:T(8,128)(2,1)} %collective-permute-done.refs_14_), channel_id=1, source_target_pairs={{0,1},{1,0},{2,3},{3,2},{4,5},{5,4},{6,7},{7,6},{8,9},{9,8},{10,11... | collective-permute-start | bytes 2457608 | tf_op jit(solution)/shard_map/ppermute | solution.py:116
  56.2 21.1 %collective-permute-start.5 = (bf16[160,2560]{1,0:T(8,128)(2,1)}, bf16[160,2560]{1,0:T(8,128)(2,1)}, u32[]{:S(2)}, u32[]{:S(2)}) collective-permute-start(bf16[160,2560]{1,0:T(8,128)(2,1)} %collective-permute-done.4.refs_16_), channel_id=1, source_target_pairs={{0,4},{1,5},{4,8},{5,9},{8,12},{9,13},{12,14},{13,15},{14,10},{15,... | collective-permute-start | bytes 2457608 | tf_op jit(solution)/shard_map/ppermute | solution.py:109
  57.7 21.5 %copy-start.2 = (bf16[16,160,32]{2,1,0:T(8,128)(2,1)}, bf16[16,160,32]{2,1,0:T(8,128)(2,1)S(1)}, u32[]{:S(2)}) copy-start(bf16[16,160,32]{2,1,0:T(8,128)(2,1)S(1)} %copy.35) | copy-start | bytes 491524
  61.3 23.0 %collective-permute-start.3 = (bf16[160,2560]{1,0:T(8,128)(2,1)}, bf16[160,2560]{1,0:T(8,128)(2,1)}, u32[]{:S(2)}, u32[]{:S(2)}) collective-permute-start(bf16[160,2560]{1,0:T(8,128)(2,1)} %collective-permute-done.2.refs_17_), channel_id=1, source_target_pairs={{4,0},{5,1},{8,4},{9,5},{12,8},{13,9},{14,12},{15,13},{10,14},{11,... | collective-permute-start | bytes 2457608 | tf_op jit(solution)/shard_map/ppermute | solution.py:112
  77.3 20.9 %collective-permute-start.6 = (bf16[160,2560]{1,0:T(8,128)(2,1)}, bf16[160,2560]{1,0:T(8,128)(2,1)}, u32[]{:S(2)}, u32[]{:S(2)}) collective-permute-start(bf16[160,2560]{1,0:T(8,128)(2,1)} %collective-permute-done.5.refs_18_), channel_id=1, source_target_pairs={{0,4},{1,5},{4,8},{5,9},{8,12},{9,13},{12,14},{13,15},{14,10},{15,... | collective-permute-start | bytes 2457608 | tf_op jit(solution)/shard_map/ppermute | solution.py:109
  84.3 14.7 %collective-permute-start.11 = (bf16[160,2560]{1,0:T(8,128)(2,1)}, bf16[160,2560]{1,0:T(8,128)(2,1)S(1)}, u32[]{:S(2)}, u32[]{:S(2)}) collective-permute-start(bf16[160,2560]{1,0:T(8,128)(2,1)} %collective-permute-done.2.refs_17_), channel_id=1, source_target_pairs={{0,1},{1,0},{2,3},{3,2},{4,5},{5,4},{6,7},{7,6},{8,9},{9,8},{10,11... | collective-permute-start | bytes 2457608 | tf_op jit(solution)/shard_map/ppermute | solution.py:116
  84.3 14.7 %collective-permute-start.10 = (bf16[160,2560]{1,0:T(8,128)(2,1)}, bf16[160,2560]{1,0:T(8,128)(2,1)S(1)}, u32[]{:S(2)}, u32[]{:S(2)}) collective-permute-start(bf16[160,2560]{1,0:T(8,128)(2,1)} %collective-permute-done.4.refs_16_), channel_id=1, source_target_pairs={{0,1},{1,0},{2,3},{3,2},{4,5},{5,4},{6,7},{7,6},{8,9},{9,8},{10,11... | collective-permute-start | bytes 2457608 | tf_op jit(solution)/shard_map/ppermute | solution.py:116
  84.8 14.3 %collective-permute-start.13 = (bf16[160,2560]{1,0:T(8,128)(2,1)}, bf16[160,2560]{1,0:T(8,128)(2,1)S(1)}, u32[]{:S(2)}, u32[]{:S(2)}) collective-permute-start(bf16[160,2560]{1,0:T(8,128)(2,1)} %collective-permute-done.3.refs_19_), channel_id=1, source_target_pairs={{0,1},{1,0},{2,3},{3,2},{4,5},{5,4},{6,7},{7,6},{8,9},{9,8},{10,11... | collective-permute-start | bytes 2457608 | tf_op jit(solution)/shard_map/ppermute | solution.py:116
  84.9 14.2 %collective-permute-start.12 = (bf16[160,2560]{1,0:T(8,128)(2,1)}, bf16[160,2560]{1,0:T(8,128)(2,1)S(1)}, u32[]{:S(2)}, u32[]{:S(2)}) collective-permute-start(bf16[160,2560]{1,0:T(8,128)(2,1)} %collective-permute-done.5.refs_18_), channel_id=1, source_target_pairs={{0,1},{1,0},{2,3},{3,2},{4,5},{5,4},{6,7},{7,6},{8,9},{9,8},{10,11... | collective-permute-start | bytes 2457608 | tf_op jit(solution)/shard_map/ppermute | solution.py:116
  98.3 2.7 %collective-permute-start.14 = (bf16[160,2560]{1,0:T(8,128)(2,1)}, bf16[160,2560]{1,0:T(8,128)(2,1)}, u32[]{:S(2)}, u32[]{:S(2)}) collective-permute-start(bf16[160,2560]{1,0:T(8,128)(2,1)} %collective-permute-done.6.refs_20_), channel_id=1, source_target_pairs={{0,1},{1,0},{2,3},{3,2},{4,5},{5,4},{6,7},{7,6},{8,9},{9,8},{10,11... | collective-permute-start | bytes 2457608 | tf_op jit(solution)/shard_map/ppermute | solution.py:116
  119.6 13.9 %collective-permute-start.15 = (bf16[64,2560]{1,0:T(8,128)(2,1)}, bf16[64,2560]{1,0:T(8,128)(2,1)S(1)}, u32[]{:S(2)}, u32[]{:S(2)}) collective-permute-start(bf16[64,2560]{1,0:T(8,128)(2,1)} %get-tuple-element.85), channel_id=1, source_target_pairs={{16,0},{17,1},{18,2},{19,3},{20,4},{21,5},{22,6},{23,7},{24,8},{25... | collective-permute-start | bytes 983048 | tf_op jit(solution)/shard_map/ppermute | solution.py:513
  132.3 12.5 %collective-permute-start.16 = (bf16[64,2560]{1,0:T(8,128)(2,1)}, bf16[64,2560]{1,0:T(8,128)(2,1)S(1)}, u32[]{:S(2)}, u32[]{:S(2)}) collective-permute-start(bf16[64,2560]{1,0:T(8,128)(2,1)} %get-tuple-element.90), channel_id=1, source_target_pairs={{16,0},{17,1},{18,2},{19,3},{20,4},{21,5},{22,6},{23,7},{24,8},{25... | collective-permute-start | bytes 983048 | tf_op jit(solution)/shard_map/ppermute | solution.py:513
  (9 other events, 48.1 us)

commit v10 on v9

--- a/solution.py
+++ b/solution.py
@@ -105,7 +105,7 @@
         if hop == 2:
             forward, backward, early = lax.optimization_barrier((forward, backward, early))
         if hop == 3:
-            late = make_late(lax.optimization_barrier((small, forward))[0])
+            late = make_late(small)
         forward = lax.ppermute(forward, "dp", ahead)
         pieces.append(forward)
         if hop <= (chips - 1) // 2:

time: 172 us -> 166 us (0.965)
  waiting for transfers between devices: 69.8 us -> 51.2 us
  starting transfers between devices: 17.7 us -> 28 us
  blocking collectives: 13.7 us -> 17.1 us
    all_to_all x1, waiting for transfers between devices: 21.4 us -> 3.87 us  [gather_small(): lax.all_to_all(sent, 'dp', split_axis=0, concat_axis=0, tiled=True, axis_...]
    ppermute x4, starting transfers between devices: 2.5 us -> 9.13 us  [weight_pieces(): forward = lax.ppermute(forward, 'dp', ahead)]
    ppermute x4, waiting for transfers between devices: 30.3 us -> 24.3 us  [weight_pieces(): forward = lax.ppermute(forward, 'dp', ahead)]
    ppermute x3, waiting for transfers between devices: 16.2 us -> 20.8 us  [weight_pieces(): backward = lax.ppermute(backward, 'dp', behind)]
    ppermute x8, starting transfers between devices: 1.54 us -> 5.17 us  [weight_pieces(): pieces += [lax.ppermute(piece, 'dp', pair) for piece in copied]]
    all_to_all x1, blocking collectives: 13.7 us -> 17.1 us  [per_device(): got = lax.all_to_all(partial, 'dp', split_axis=0, concat_axis=0, tiled=True)]
  transfers between devices with their start and end apart: 18 -> 18, of which waited for: 8 -> 10; matrix products, arithmetic and copies ran while one was open for 9% -> 9% of each run, Pallas kernels for 13% -> 13%
where the time goes in v10:
time: 166 us; the launch traced here: 165 us
  Pallas kernels  52.6 us (32%)
  waiting for transfers between devices  51.2 us (31%)
  starting transfers between devices  28 us (17%)
  blocking collectives  17.1 us (10%)
  local copies, waits for them, and re-layouts  9.32 us (6%)
  other arithmetic  5.17 us (3%)
    pallas_call x4, Pallas kernels, backward(): pl.pallas_call(functools.partial(step_kernel, order, step, steps), grid_s...  52.1 us
    ppermute x4, waiting for transfers between devices, weight_pieces(): forward = lax.ppermute(forward, 'dp', ahead)  24.3 us
    ppermute x3, waiting for transfers between devices, weight_pieces(): backward = lax.ppermute(backward, 'dp', behind)  20.8 us
    all_to_all x1, blocking collectives, per_device(): got = lax.all_to_all(partial, 'dp', split_axis=0, concat_axis=0, tiled=True)  17.1 us
    ppermute x4, starting transfers between devices, weight_pieces(): forward = lax.ppermute(forward, 'dp', ahead)  9.13 us
    all_to_all x1, starting transfers between devices, gather_small(): lax.all_to_all(sent, 'dp', split_axis=0, concat_axis=0, tiled=True, axis_...  6.01 us
    ppermute x8, starting transfers between devices, weight_pieces(): pieces += [lax.ppermute(piece, 'dp', pair) for piece in copied]  5.17 us
    ppermute x3, starting transfers between devices, weight_pieces(): backward = lax.ppermute(backward, 'dp', behind)  4.93 us
  transfers between devices with their start and end apart: 18, of which 10 were waited for; matrix products, arithmetic and copies ran while one was open for 9% of the time, Pallas kernels for 13%

profile of v10, /device:TPU:0, one launch (start us, length us, event | category | flops | bytes accessed | tf_op | source)
XLA Modules:
  0.0 165.3 jit_solution(16969977575761006445)
XLA Ops:
  0.7 3.0 %collective-permute-start.1 = (bf16[160,2560]{1,0:T(8,128)(2,1)}, bf16[160,2560]{1,0:T(8,128)(2,1)}, u32[]{:S(2)}, u32[]{:S(2)}) collective-permute-start(bf16[160,2560]{1,0:T(8,128)(2,1)} %bitcast.58), channel_id=1, source_target_pairs={{4,0},{5,1},{8,4},{9,5},{12,8},{13,9},{14,12},{15,13},{10,14},{11,... | collective-permute-start | bytes 2457608 | tf_op jit(solution)/shard_map/ppermute | solution.py:112
  4.8 1.4 fusion.15
  11.7 10.6 %collective-permute-done.1.refs_15_ = bf16[160,2560]{1,0:T(8,128)(2,1)} collective-permute-done((bf16[160,2560]{1,0:T(8,128)(2,1)}, bf16[160,2560]{1,0:T(8,128)(2,1)}, u32[]{:S(2)}, u32[]{:S(2)}) %collective-permute-start.1) | collective-permute-done | bytes 819232 | tf_op jit(solution)/shard_map/ppermute | solution.py:112
  22.3 1.4 collective-permute-done.refs_14_
  25.0 6.0 %all-to-all-start = ((bf16[16,160,65]{1,2,0:T(8,128)(2,1)}), bf16[16,160,65]{1,2,0:T(8,128)(2,1)S(1)}, u32[]{:S(2)}, u32[]{:S(2)}) async-start(bf16[16,160,65]{1,2,0:T(8,128)(2,1)} %broadcast_in_dim.38), calls=%async_computation | async-start | bytes 1179648 | tf_op jit(solution)/shard_map/all_to_all | solution.py:421
  31.0 1.9 %collective-permute-start.2 = (bf16[160,2560]{1,0:T(8,128)(2,1)}, bf16[160,2560]{1,0:T(8,128)(2,1)}, u32[]{:S(2)}, u32[]{:S(2)}) collective-permute-start(bf16[160,2560]{1,0:T(8,128)(2,1)} %collective-permute-done.1.refs_15_), channel_id=1, source_target_pairs={{4,0},{5,1},{8,4},{9,5},{12,8},{13,9},{14,12},{15,13},{10,14},{11,... | collective-permute-start | bytes 2457608 | tf_op jit(solution)/shard_map/ppermute | solution.py:112
  32.9 12.7 %collective-permute-done.4.refs_16_ = bf16[160,2560]{1,0:T(8,128)(2,1)} collective-permute-done((bf16[160,2560]{1,0:T(8,128)(2,1)}, bf16[160,2560]{1,0:T(8,128)(2,1)}, u32[]{:S(2)}, u32[]{:S(2)}) %collective-permute-start.4) | collective-permute-done | bytes 819232 | tf_op jit(solution)/shard_map/ppermute | solution.py:109
  45.7 3.9 %collective-permute-start.5 = (bf16[160,2560]{1,0:T(8,128)(2,1)}, bf16[160,2560]{1,0:T(8,128)(2,1)}, u32[]{:S(2)}, u32[]{:S(2)}) collective-permute-start(bf16[160,2560]{1,0:T(8,128)(2,1)} %collective-permute-done.4.refs_16_), channel_id=1, source_target_pairs={{0,4},{1,5},{4,8},{5,9},{8,12},{9,13},{12,14},{13,15},{14,10},{15,... | collective-permute-start | bytes 2457608 | tf_op jit(solution)/shard_map/ppermute | solution.py:109
  50.2 3.9 %all-to-all-done = bf16[16,160,65]{1,2,0:T(8,128)(2,1)S(1)} async-done(((bf16[16,160,65]{1,2,0:T(8,128)(2,1)}), bf16[16,160,65]{1,2,0:T(8,128)(2,1)S(1)}, u32[]{:S(2)}, u32[]{:S(2)}) %all-to-all-start) | async-done | bytes 332832 | tf_op jit(solution)/shard_map/all_to_all | solution.py:421
  54.5 4.1 %collective-permute-start.9 = (bf16[160,2560]{1,0:T(8,128)(2,1)}, bf16[160,2560]{1,0:T(8,128)(2,1)}, u32[]{:S(2)}, u32[]{:S(2)}) collective-permute-start(bf16[160,2560]{1,0:T(8,128)(2,1)} %collective-permute-done.1.refs_15_), channel_id=1, source_target_pairs={{0,1},{1,0},{2,3},{3,2},{4,5},{5,4},{6,7},{7,6},{8,9},{9,8},{10,11... | collective-permute-start | bytes 2457608 | tf_op jit(solution)/shard_map/ppermute | solution.py:116
  58.7 2.6 %collective-permute-done.2.refs_17_ = bf16[160,2560]{1,0:T(8,128)(2,1)} collective-permute-done((bf16[160,2560]{1,0:T(8,128)(2,1)}, bf16[160,2560]{1,0:T(8,128)(2,1)}, u32[]{:S(2)}, u32[]{:S(2)}) %collective-permute-start.2) | collective-permute-done | bytes 819232 | tf_op jit(solution)/shard_map/ppermute | solution.py:112
  61.3 6.9 %collective-permute-done.5.refs_18_ = bf16[160,2560]{1,0:T(8,128)(2,1)} collective-permute-done((bf16[160,2560]{1,0:T(8,128)(2,1)}, bf16[160,2560]{1,0:T(8,128)(2,1)}, u32[]{:S(2)}, u32[]{:S(2)}) %collective-permute-start.5) | collective-permute-done | bytes 819232 | tf_op jit(solution)/shard_map/ppermute | solution.py:109
  68.1 4.6 %collective-permute-start.6 = (bf16[160,2560]{1,0:T(8,128)(2,1)}, bf16[160,2560]{1,0:T(8,128)(2,1)}, u32[]{:S(2)}, u32[]{:S(2)}) collective-permute-start(bf16[160,2560]{1,0:T(8,128)(2,1)} %collective-permute-done.5.refs_18_), channel_id=1, source_target_pairs={{0,4},{1,5},{4,8},{5,9},{8,12},{9,13},{12,14},{13,15},{14,10},{15,... | collective-permute-start | bytes 2457608 | tf_op jit(solution)/shard_map/ppermute | solution.py:109
  75.6 1.1 fusion.1.refs_1_
  76.7 7.6 %collective-permute-done.3.refs_19_ = bf16[160,2560]{1,0:T(8,128)(2,1)} collective-permute-done((bf16[160,2560]{1,0:T(8,128)(2,1)}, bf16[160,2560]{1,0:T(8,128)(2,1)}, u32[]{:S(2)}, u32[]{:S(2)}) %collective-permute-start.3) | collective-permute-done | bytes 819232 | tf_op jit(solution)/shard_map/ppermute | solution.py:112
  85.3 3.3 %collective-permute-done.6.refs_20_ = bf16[160,2560]{1,0:T(8,128)(2,1)} collective-permute-done((bf16[160,2560]{1,0:T(8,128)(2,1)}, bf16[160,2560]{1,0:T(8,128)(2,1)}, u32[]{:S(2)}, u32[]{:S(2)}) %collective-permute-start.6) | collective-permute-done | bytes 819232 | tf_op jit(solution)/shard_map/ppermute | solution.py:109
  90.3 1.3 collective-permute-done.14.refs_28_
  91.6 18.7 %first_step.1 = (bf16[4,2560,640]{2,1,0:T(8,128)(2,1)S(1)}, bf16[128,2560]{1,0:T(8,128)(2,1)S(1)}, bf16[64,2560]{1,0:T(8,128)(2,1)}, bf16[2,64,2560]{2,1,0:T(8,1...) custom-call(s32[21]{0:T(128)S(1)} %pad_add_fusion.chosen, ...), custom_call_target="tpu_custom_call" | custom-call | flops 1845493760 | bytes 13107200 | tf_op jit(solution)/shard_map/first_step/pallas_call | solution.py:341
  110.3 1.5 collective-permute-start.15
  111.8 11.1 %step.3 = (bf16[64,2560]{1,0:T(8,128)(2,1)}, bf16[2,64,2560]{2,1,0:T(8,128)(2,1)S(1)}, bf16[2,64,32]{2,1,0:T(8,128)(2,1)S(1)}, bf16[2,64,2560]{2,1,0:T(8,128)(2,1)}, bf16[4,2560,640]{2,1,0:T(8,128)(2,1)S(1)}) custom-call(s32[21]{0:T(128)S(1)} %pad_add_fusion.chosen, ...), custom_call_target="tpu_custom_call", output_to_operand_aliasing={{4}: (14, {}), {1}: (16, {}), {2}: (17, {}), {3}: (18, {})} | custom-call | flops 1845493760 | bytes 13107200 | tf_op jit(solution)/shard_map/step/pallas_call | solution.py:341
  123.0 1.3 collective-permute-start.16
  124.3 11.1 %step.4 = (bf16[64,2560]{1,0:T(8,128)(2,1)}, bf16[2,64,2560]{2,1,0:T(8,128)(2,1)S(1)}, bf16[2,64,32]{2,1,0:T(8,128)(2,1)S(1)}, bf16[2,64,2560]{2,1,0:T(8,128)(2,1)}, bf16[4,2560,640]{2,1,0:T(8,128)(2,1)S(1)}) custom-call(s32[21]{0:T(128)S(1)} %pad_add_fusion.chosen, ...), custom_call_target="tpu_custom_call", output_to_operand_aliasing={{4}: (14, {}), {1}: (17, {}), {2}: (18, {}), {3}: (19, {})} | custom-call | flops 1845493760 | bytes 13107200 | tf_op jit(solution)/shard_map/step/pallas_call | solution.py:341
  135.4 11.1 %step.5 = (bf16[64,2560]{1,0:T(8,128)(2,1)}, bf16[2,64,2560]{2,1,0:T(8,128)(2,1)S(1)}, bf16[2,64,32]{2,1,0:T(8,128)(2,1)S(1)}, bf16[2,64,2560]{2,1,0:T(8,128)(2,1)}, bf16[4,2560,640]{2,1,0:T(8,128)(2,1)S(1)}) custom-call(s32[21]{0:T(128)S(1)} %pad_add_fusion.chosen, ...), custom_call_target="tpu_custom_call", output_to_operand_aliasing={{4}: (14, {}), {1}: (17, {}), {2}: (18, {}), {3}: (19, {})} | custom-call | flops 1845493760 | bytes 13107200 | tf_op jit(solution)/shard_map/step/pallas_call | solution.py:341
  147.0 17.1 %all_to_all.10 = bf16[16,80,128]{2,1,0:T(8,128)(2,1)S(1)} all-to-all(bf16[16,80,128]{2,1,0:T(8,128)(2,1)S(1)} %gradients.1), channel_id=1, replica_groups=mesh['pipe'=2,'dp'=16] {'dp'}, dimensions={0} | all-to-all | bytes 655360 | tf_op jit(solution)/shard_map/all_to_all | solution.py:518
  (91 shorter events, 16.1 us)
Async XLA Ops:
  0.7 21.6 %collective-permute-start.1 = (bf16[160,2560]{1,0:T(8,128)(2,1)}, bf16[160,2560]{1,0:T(8,128)(2,1)}, u32[]{:S(2)}, u32[]{:S(2)}) collective-permute-start(bf16[160,2560]{1,0:T(8,128)(2,1)} %bitcast.58), channel_id=1, source_target_pairs={{4,0},{5,1},{8,4},{9,5},{12,8},{13,9},{14,12},{15,13},{10,14},{11,... | collective-permute-start | bytes 2457608 | tf_op jit(solution)/shard_map/ppermute | solution.py:112
  3.7 20.0 %collective-permute-start = (bf16[160,2560]{1,0:T(8,128)(2,1)}, bf16[160,2560]{1,0:T(8,128)(2,1)}, u32[]{:S(2)}, u32[]{:S(2)}) collective-permute-start(bf16[160,2560]{1,0:T(8,128)(2,1)} %bitcast.59), channel_id=1, source_target_pairs={{0,4},{1,5},{4,8},{5,9},{8,12},{9,13},{12,14},{13,15},{14,10},{15,... | collective-permute-start | bytes 2457608 | tf_op jit(solution)/shard_map/ppermute | solution.py:109
  9.1 15.1 %copy-start.8 = (bf16[1,160,32]{1,2,0:T(8,128)(2,1)S(1)}, bf16[1,160,32]{1,2,0:T(8,128)(2,1)}, u32[]{:S(2)}) copy-start(bf16[1,160,32]{1,2,0:T(8,128)(2,1)} %param.18) | copy-start | bytes 30724
  9.1 15.1 %copy-start.9 = (bf16[1,160,32]{1,2,0:T(8,128)(2,1)S(1)}, bf16[1,160,32]{1,2,0:T(8,128)(2,1)}, u32[]{:S(2)}) copy-start(bf16[1,160,32]{1,2,0:T(8,128)(2,1)} %param.17) | copy-start | bytes 30724
  9.1 15.0 %copy-start.10 = (bf16[1,160]{1,0:T(2,128)(2,1)S(1)}, bf16[1,160]{1,0:T(2,128)(2,1)}, u32[]{:S(2)}) copy-start(bf16[1,160]{1,0:T(2,128)(2,1)} %param.19) | copy-start | bytes 964
  9.6 66.0 %copy-start.1 = (bf16[2,64,2560]{2,1,0:T(8,128)(2,1)}, bf16[2,64,2560]{2,1,0:T(8,128)(2,1)S(1)}, u32[]{:S(2)}) copy-start(bf16[2,64,2560]{2,1,0:T(8,128)(2,1)S(1)} %concatenate.43.refs_10_) | copy-start | bytes 1966084
  10.7 38.9 %copy-start.3 = (bf16[1,160,2560]{2,1,0:T(8,128)(2,1)S(1)}, bf16[1,160,2560]{2,1,0:T(8,128)(2,1)}, u32[]{:S(2)}) copy-start(bf16[1,160,2560]{2,1,0:T(8,128)(2,1)} %param.16) | copy-start | bytes 2457604
  23.7 22.0 %collective-permute-start.4 = (bf16[160,2560]{1,0:T(8,128)(2,1)}, bf16[160,2560]{1,0:T(8,128)(2,1)}, u32[]{:S(2)}, u32[]{:S(2)}) collective-permute-start(bf16[160,2560]{1,0:T(8,128)(2,1)} %collective-permute-done.refs_14_), channel_id=1, source_target_pairs={{0,4},{1,5},{4,8},{5,9},{8,12},{9,13},{12,14},{13,15},{14,10},{15,... | collective-permute-start | bytes 2457608 | tf_op jit(solution)/shard_map/ppermute | solution.py:109
  25.0 29.0 %all-to-all-start = ((bf16[16,160,65]{1,2,0:T(8,128)(2,1)}), bf16[16,160,65]{1,2,0:T(8,128)(2,1)S(1)}, u32[]{:S(2)}, u32[]{:S(2)}) async-start(bf16[16,160,65]{1,2,0:T(8,128)(2,1)} %broadcast_in_dim.38), calls=%async_computation | async-start | bytes 1179648 | tf_op jit(solution)/shard_map/all_to_all | solution.py:421
  31.0 30.3 %collective-permute-start.2 = (bf16[160,2560]{1,0:T(8,128)(2,1)}, bf16[160,2560]{1,0:T(8,128)(2,1)}, u32[]{:S(2)}, u32[]{:S(2)}) collective-permute-start(bf16[160,2560]{1,0:T(8,128)(2,1)} %collective-permute-done.1.refs_15_), channel_id=1, source_target_pairs={{4,0},{5,1},{8,4},{9,5},{12,8},{13,9},{14,12},{15,13},{10,14},{11,... | collective-permute-start | bytes 2457608 | tf_op jit(solution)/shard_map/ppermute | solution.py:112
  45.7 22.5 %collective-permute-start.5 = (bf16[160,2560]{1,0:T(8,128)(2,1)}, bf16[160,2560]{1,0:T(8,128)(2,1)}, u32[]{:S(2)}, u32[]{:S(2)}) collective-permute-start(bf16[160,2560]{1,0:T(8,128)(2,1)} %collective-permute-done.4.refs_16_), channel_id=1, source_target_pairs={{0,4},{1,5},{4,8},{5,9},{8,12},{9,13},{12,14},{13,15},{14,10},{15,... | collective-permute-start | bytes 2457608 | tf_op jit(solution)/shard_map/ppermute | solution.py:109
  49.6 34.7 %collective-permute-start.7 = (bf16[160,2560]{1,0:T(8,128)(2,1)S(1)}, bf16[160,2560]{1,0:T(8,128)(2,1)}, u32[]{:S(2)}, u32[]{:S(2)}) collective-permute-start(bf16[160,2560]{1,0:T(8,128)(2,1)S(1)} %bitcast.61), channel_id=1, source_target_pairs={{0,1},{1,0},{2,3},{3,2},{4,5},{5,4},{6,7},{7,6},{8,9},{9,8},{10,11... | collective-permute-start | bytes 2457608 | tf_op jit(solution)/shard_map/ppermute | solution.py:116
  54.5 21.0 %copy-start.2 = (bf16[16,160,32]{2,1,0:T(8,128)(2,1)}, bf16[16,160,32]{2,1,0:T(8,128)(2,1)S(1)}, u32[]{:S(2)}) copy-start(bf16[16,160,32]{2,1,0:T(8,128)(2,1)S(1)} %copy.35) | copy-start | bytes 491524
  54.5 30.2 %collective-permute-start.9 = (bf16[160,2560]{1,0:T(8,128)(2,1)}, bf16[160,2560]{1,0:T(8,128)(2,1)}, u32[]{:S(2)}, u32[]{:S(2)}) collective-permute-start(bf16[160,2560]{1,0:T(8,128)(2,1)} %collective-permute-done.1.refs_15_), channel_id=1, source_target_pairs={{0,1},{1,0},{2,3},{3,2},{4,5},{5,4},{6,7},{7,6},{8,9},{9,8},{10,11... | collective-permute-start | bytes 2457608 | tf_op jit(solution)/shard_map/ppermute | solution.py:116
  58.6 26.3 %collective-permute-start.8 = (bf16[160,2560]{1,0:T(8,128)(2,1)}, bf16[160,2560]{1,0:T(8,128)(2,1)}, u32[]{:S(2)}, u32[]{:S(2)}) collective-permute-start(bf16[160,2560]{1,0:T(8,128)(2,1)} %collective-permute-done.refs_14_), channel_id=1, source_target_pairs={{0,1},{1,0},{2,3},{3,2},{4,5},{5,4},{6,7},{7,6},{8,9},{9,8},{10,11... | collective-permute-start | bytes 2457608 | tf_op jit(solution)/shard_map/ppermute | solution.py:116
  61.3 23.0 %collective-permute-start.3 = (bf16[160,2560]{1,0:T(8,128)(2,1)}, bf16[160,2560]{1,0:T(8,128)(2,1)}, u32[]{:S(2)}, u32[]{:S(2)}) collective-permute-start(bf16[160,2560]{1,0:T(8,128)(2,1)} %collective-permute-done.2.refs_17_), channel_id=1, source_target_pairs={{4,0},{5,1},{8,4},{9,5},{12,8},{13,9},{14,12},{15,13},{10,14},{11,... | collective-permute-start | bytes 2457608 | tf_op jit(solution)/shard_map/ppermute | solution.py:112
  68.1 20.5 %collective-permute-start.6 = (bf16[160,2560]{1,0:T(8,128)(2,1)}, bf16[160,2560]{1,0:T(8,128)(2,1)}, u32[]{:S(2)}, u32[]{:S(2)}) collective-permute-start(bf16[160,2560]{1,0:T(8,128)(2,1)} %collective-permute-done.5.refs_18_), channel_id=1, source_target_pairs={{0,4},{1,5},{4,8},{5,9},{8,12},{9,13},{12,14},{13,15},{14,10},{15,... | collective-permute-start | bytes 2457608 | tf_op jit(solution)/shard_map/ppermute | solution.py:109
  84.3 5.1 %collective-permute-start.11 = (bf16[160,2560]{1,0:T(8,128)(2,1)}, bf16[160,2560]{1,0:T(8,128)(2,1)S(1)}, u32[]{:S(2)}, u32[]{:S(2)}) collective-permute-start(bf16[160,2560]{1,0:T(8,128)(2,1)} %collective-permute-done.2.refs_17_), channel_id=1, source_target_pairs={{0,1},{1,0},{2,3},{3,2},{4,5},{5,4},{6,7},{7,6},{8,9},{9,8},{10,11... | collective-permute-start | bytes 2457608 | tf_op jit(solution)/shard_map/ppermute | solution.py:116
  84.3 5.1 %collective-permute-start.10 = (bf16[160,2560]{1,0:T(8,128)(2,1)}, bf16[160,2560]{1,0:T(8,128)(2,1)S(1)}, u32[]{:S(2)}, u32[]{:S(2)}) collective-permute-start(bf16[160,2560]{1,0:T(8,128)(2,1)} %collective-permute-done.4.refs_16_), channel_id=1, source_target_pairs={{0,1},{1,0},{2,3},{3,2},{4,5},{5,4},{6,7},{7,6},{8,9},{9,8},{10,11... | collective-permute-start | bytes 2457608 | tf_op jit(solution)/shard_map/ppermute | solution.py:116
  84.8 4.6 %collective-permute-start.13 = (bf16[160,2560]{1,0:T(8,128)(2,1)}, bf16[160,2560]{1,0:T(8,128)(2,1)S(1)}, u32[]{:S(2)}, u32[]{:S(2)}) collective-permute-start(bf16[160,2560]{1,0:T(8,128)(2,1)} %collective-permute-done.3.refs_19_), channel_id=1, source_target_pairs={{0,1},{1,0},{2,3},{3,2},{4,5},{5,4},{6,7},{7,6},{8,9},{9,8},{10,11... | collective-permute-start | bytes 2457608 | tf_op jit(solution)/shard_map/ppermute | solution.py:116
  84.9 5.5 %collective-permute-start.12 = (bf16[160,2560]{1,0:T(8,128)(2,1)}, bf16[160,2560]{1,0:T(8,128)(2,1)S(1)}, u32[]{:S(2)}, u32[]{:S(2)}) collective-permute-start(bf16[160,2560]{1,0:T(8,128)(2,1)} %collective-permute-done.5.refs_18_), channel_id=1, source_target_pairs={{0,1},{1,0},{2,3},{3,2},{4,5},{5,4},{6,7},{7,6},{8,9},{9,8},{10,11... | collective-permute-start | bytes 2457608 | tf_op jit(solution)/shard_map/ppermute | solution.py:116
  88.6 3.0 %collective-permute-start.14 = (bf16[160,2560]{1,0:T(8,128)(2,1)}, bf16[160,2560]{1,0:T(8,128)(2,1)}, u32[]{:S(2)}, u32[]{:S(2)}) collective-permute-start(bf16[160,2560]{1,0:T(8,128)(2,1)} %collective-permute-done.6.refs_20_), channel_id=1, source_target_pairs={{0,1},{1,0},{2,3},{3,2},{4,5},{5,4},{6,7},{7,6},{8,9},{9,8},{10,11... | collective-permute-start | bytes 2457608 | tf_op jit(solution)/shard_map/ppermute | solution.py:116
  110.3 13.9 %collective-permute-start.15 = (bf16[64,2560]{1,0:T(8,128)(2,1)}, bf16[64,2560]{1,0:T(8,128)(2,1)S(1)}, u32[]{:S(2)}, u32[]{:S(2)}) collective-permute-start(bf16[64,2560]{1,0:T(8,128)(2,1)} %get-tuple-element.79), channel_id=1, source_target_pairs={{16,0},{17,1},{18,2},{19,3},{20,4},{21,5},{22,6},{23,7},{24,8},{25... | collective-permute-start | bytes 983048 | tf_op jit(solution)/shard_map/ppermute | solution.py:513
  123.0 12.5 %collective-permute-start.16 = (bf16[64,2560]{1,0:T(8,128)(2,1)}, bf16[64,2560]{1,0:T(8,128)(2,1)S(1)}, u32[]{:S(2)}, u32[]{:S(2)}) collective-permute-start(bf16[64,2560]{1,0:T(8,128)(2,1)} %get-tuple-element.84), channel_id=1, source_target_pairs={{16,0},{17,1},{18,2},{19,3},{20,4},{21,5},{22,6},{23,7},{24,8},{25... | collective-permute-start | bytes 983048 | tf_op jit(solution)/shard_map/ppermute | solution.py:513
  (8 other events, 33.5 us)
